TPU v7x, 32 devices: a whole 2x2x4 slice. The times are simulated.
32 devices in a mesh: space: 4 (over x, core), orient: 8 (over z, y).
Axes of the slice: x: 2, y: 2, z: 4, core: 2. Of those that a mesh axis runs over, the one named last changes fastest.
Arguments:
- q_init: bfloat16 [256, 64, 128, 128], P('orient', 'space'), may hold values from 0.5 to 1.5
- partner: bfloat16 [256, 64, 128, 128], P('orient', 'space'), may hold values from 0.5 to 1.5
- field: bfloat16 [6, 64, 128, 128], P(None, 'space'), may hold values from -3 to 3
- orientations: float32 [3, 256], replicated, may hold values from -1 to 1, as said below
- orient_weight: float32 [256], replicated, may hold values from 0.03 to 0.12
- rotation: bfloat16 [256, 256], replicated, may hold values from -1 to 1
Outputs:
- q_final: bfloat16 [256, 64, 128, 128], P('orient', 'space')
- new_field: float32 [6, 64, 128, 128], P(None, 'space', 'orient')
Inputs may be any that keep to these rules, and one draw needn't show every extreme that they name: `orientations`: each column is a unit vector.
All inputs are finite; a program needn't handle non-finite values.
Results may differ from a plain program's by a relative error of at most 0.0057.
Values may be sent and summed in bfloat16 or wider, within the bound.
No kernel may reach another device: no remote copies, remote signals or barrier semaphores. Data moves between devices by JAX's collectives and lax.ppermute only.
A program may use at most 320 MiB of HBM per device.

v0:
```python
import jax
import jax.numpy as jnp
from jax import lax
from jax.sharding import PartitionSpec as P

STEPS = 2


step_length = 0.3
relax_rate = 0.5
coupling = 8.0


def extended(block, sides, width):
    for axis, dim in sides:
        count = lax.axis_size(axis)
        forward = [(i, i + 1) for i in range(count - 1)]
        forward.append((count - 1, 0))
        backward = [(target, source) for source, target in forward]
        low = lax.ppermute(
            lax.slice_in_dim(block, block.shape[dim] - width, None, axis=dim), axis, forward
        )
        high = lax.ppermute(lax.slice_in_dim(block, 0, width, axis=dim), axis, backward)
        block = jnp.concatenate([low, block, high], axis=dim)
    return block


def angle_tables(orientations):
    along_x = orientations[0]
    along_y = orientations[1]
    along_z = orientations[2]
    field_terms = jnp.stack(
        [
            along_x * along_x,
            along_y * along_y,
            along_z * along_z,
            2.0 * along_x * along_y,
            2.0 * along_x * along_z,
            2.0 * along_y * along_z,
        ]
    )
    tensor_terms = jnp.stack(
        [
            along_x * along_x - 1.0 / 3.0,
            along_y * along_y - 1.0 / 3.0,
            along_z * along_z - 1.0 / 3.0,
            along_x * along_y,
            along_x * along_z,
            along_y * along_z,
        ]
    )
    return (field_terms, tensor_terms)


def upwind_padded(padded, speeds):
    speed_x, speed_y, speed_z = speeds
    center = padded[:, 1:-1, 1:-1]
    back_x = center - jnp.roll(center, 1, axis=-1)
    fore_x = jnp.roll(center, -1, axis=-1) - center
    back_y = center - padded[:, 1:-1, :-2]
    fore_y = padded[:, 1:-1, 2:] - center
    back_z = center - padded[:, :-2, 1:-1]
    fore_z = padded[:, 2:, 1:-1] - center
    total = jnp.maximum(speed_x, 0.0) * back_x + jnp.minimum(speed_x, 0.0) * fore_x
    total = total + jnp.maximum(speed_y, 0.0) * back_y + jnp.minimum(speed_y, 0.0) * fore_y
    total = total + jnp.maximum(speed_z, 0.0) * back_z + jnp.minimum(speed_z, 0.0) * fore_z
    return center - step_length * total


def per_device(q_init, partner, field, orientations, orient_weight, rotation):
    wide_field = field.astype(jnp.float32)
    all_terms = angle_tables(orientations)[1] * orient_weight[None, :]
    state, other = (
        lax.all_to_all(q_init, "orient", split_axis=2, concat_axis=0, tiled=True),
        lax.all_to_all(partner, "orient", split_axis=2, concat_axis=0, tiled=True),
    )
    owned_rows = state.shape[2]
    own_field = lax.dynamic_slice_in_dim(
        wide_field, lax.axis_index("orient") * owned_rows, owned_rows, 2
    )
    every_terms = angle_tables(orientations)[0]
    potential = jnp.einsum("co,czyx->ozyx", every_terms, own_field, precision=lax.Precision.HIGHEST)
    damping = jnp.exp(-step_length * potential)
    speeds = (
        orientations[0][:, None, None, None],
        orientations[1][:, None, None, None],
        orientations[2][:, None, None, None],
    )
    for contour in range(STEPS):
        padded = extended(state, (("space", 1), ("orient", 2)), 1).astype(jnp.float32)
        moved = upwind_padded(padded, speeds)
        block_in = (moved * damping).astype(jnp.bfloat16)
        flat = block_in.reshape(block_in.shape[0], -1)
        state = (
            jnp.dot(rotation, flat, preferred_element_type=jnp.float32)
            .astype(jnp.bfloat16)
            .reshape(block_in.shape)
        )
    product = state.astype(jnp.float32) * other.astype(jnp.float32)
    sums = jnp.dot(
        all_terms, product.reshape(product.shape[0], -1), precision=lax.Precision.HIGHEST
    )
    tensor = sums.reshape((6,) + product.shape[1:])
    state = lax.all_to_all(state, "orient", split_axis=0, concat_axis=2, tiled=True)
    new_field = (1.0 - relax_rate) * own_field + relax_rate * coupling * tensor
    return (state, new_field)


def solution(mesh):
    in_specs = (
        P("orient", "space", None, None),
        P("orient", "space", None, None),
        P(None, "space", None, None),
        P(),
        P(),
        P(),
    )
    out_specs = (P("orient", "space", None, None), P(None, "space", "orient", None))
    return jax.shard_map(
        per_device, mesh=mesh, in_specs=in_specs, out_specs=out_specs, check_vma=False
    )
```

profile of v0, /device:TPU:0, one launch (start us, length us, event | category | flops | bytes accessed | tf_op | source)
XLA Modules:
  0.0 1672.2 jit_solution(1033468117136542712)
XLA Ops:
  0.6 0.0 copy-start
  0.6 16.8 %copy.48 = bf16[32,16,128,128]{3,1,0,2:T(8,128)(2,1)} copy(bf16[32,16,128,128]{3,2,1,0:T(8,128)(2,1)} %param.6) | data formatting | bytes 33554432 | tf_op args[0]
  17.5 7.3 all-to-all-start
  24.8 16.8 %copy.57 = bf16[32,16,128,128]{3,1,0,2:T(8,128)(2,1)} copy(bf16[32,16,128,128]{3,2,1,0:T(8,128)(2,1)} %param.7) | data formatting | bytes 33554432 | tf_op args[1]
  41.6 346.1 %all-to-all-done = bf16[32,16,128,128]{3,1,0,2:T(8,128)(2,1)} async-done(((bf16[32,16,128,128]{3,1,0,2:T(8,128)(2,1)}), bf16[32,16,128,128]{3,1,0,2:T(8,128)(2,1)}, u32[]{:S(2)}, u32[]{:S(2)}) %all-to-all-start) | async-done | bytes 16777248 | tf_op jit(solution)/shard_map/all_to_all | solution.py:74
  387.7 5.7 all-to-all-start.2
  393.5 0.0 copy-start.1
  393.5 28.2 %copy.50 = bf16[8,32,16,16,128]{4,3,2,1,0:T(8,128)(2,1)} copy(bf16[8,32,16,16,128]{4,2,1,3,0:T(8,128)(2,1)} %bitcast.2) | data formatting | bytes 33554432 | tf_op jit(solution)/shard_map/all_to_all | solution.py:74
  421.7 24.0 %copy.51 = bf16[256,16,16,128]{0,3,2,1:T(8,128)(2,1)} copy(bf16[256,16,16,128]{3,2,1,0:T(8,128)(2,1)} %bitcast.62) | data formatting | bytes 33554432 | tf_op jit(solution)/shard_map/all_to_all | solution.py:74
  445.7 2.7 fusion.38
  448.4 0.0 collective-permute-start
  448.4 1.7 collective-permute-start.1
  450.2 1.0 constant_dynamic-slice_fusion
  451.2 1.1 copy.63
  452.3 0.0 copy-done.1
  452.3 0.6 slice_multiply_fusion
  452.9 0.6 slice_multiply_fusion.1
  453.5 18.9 %collective-permute-done = bf16[256,1,16,128]{0,3,2,1:T(8,128)(2,1)S(1)} collective-permute-done((bf16[256,1,16,128]{0,3,2,1:T(8,128)(2,1)}, bf16[256,1,16,128]{0,3,2,1:T(8,128)(2,1)S(1)}, u32[]{:S(2)}, u32[]{:S(2)}) %collective-permute-start) | collective-permute-done | bytes 1048608 | tf_op jit(solution)/shard_map/ppermute | solution.py:20
  472.4 0.7 collective-permute-done.1
  473.2 3.4 pad_maximum_fusion.5
  476.6 1.9 collective-permute-start.2
  478.5 3.0 collective-permute-start.3
  481.5 20.4 %fusion.39 = f32[256,32768]{0,1} fusion(f32[6,256]{1,0:T(8,128)S(1)} %stack.4, bf16[6,32768]{1,0:T(8,128)(2,1)} %bitcast.64), kind=kOutput, calls=%fused_computation.88 | convolution fusion | flops 603979776 | bytes 33953792
  501.9 190.9 %collective-permute-done.2 = bf16[256,18,1,128]{0,3,2,1:T(8,128)(2,1)S(1)} collective-permute-done((bf16[256,18,1,128]{0,3,2,1:T(8,128)(2,1)}, bf16[256,18,1,128]{0,3,2,1:T(8,128)(2,1)S(1)}, u32[]{:S(2)}, u32[]{:S(2)}) %collective-permute-start.2) | collective-permute-done | bytes 1179680 | tf_op jit(solution)/shard_map/ppermute | solution.py:20
  692.7 0.0 collective-permute-done.3
  692.8 0.0 slice-done.5
  692.8 0.0 slice-done.6
  692.8 0.0 slice-done.7
  692.8 0.5 maximum_convert_fusion.4
  693.3 18.2 %maximum_convert_fusion = f32[256,18,18,128]{0,3,2,1:T(8,128)} fusion(bf16[256,18,1,128]{0,3,2,1:T(8,128)(2,1)S(1)} %collective-permute-done.3, bf16[256,1,16,128]{0,3,2,1:T(8,128)(2,1)S(1)} %collective-permute-done.1, bf16[256,16,16,128]{0,3,2,1:T(8,128)(2,1)S(1)} %bitcast.56, bf16[256,1,16,128]{0,3,2,1:T(8,128)(2,1)S(1)} %collective-permute-done, ...), kind=kLoop, calls=%fused_computation.47 | loop fusion | flops 53084160 | bytes 63700992 | tf_op jit(solution)/shard_map/convert_element_type | solution.py:90
  711.6 42.7 %fusion.36 = (f32[256,16,16,127]{0,3,2,1:T(8,128)}, f32[256,16,16,127]{0,3,2,1:T(8,128)}) fusion(f32[256,18,18,128]{0,3,2,1:T(8,128)} %maximum_convert_fusion), kind=kLoop, calls=%fused_computation.85 | loop fusion | bytes 133169152 | tf_op jit(solution)/shard_map/jit(_roll_static)/slice | solution.py:59
  754.2 88.3 %fusion.17 = bf16[256,16,16,128]{0,3,2,1:T(8,128)(2,1)} fusion(f32[256,18,18,128]{0,3,2,1:T(8,128)} %maximum_convert_fusion, f32[256,16,16,127]{0,3,2,1:T(8,128)} %get-tuple-element.13, f32[256,16,16,1]{0,3,2,1:T(1,128)S(1)} %get-tuple-element.17, f32[256,16,16,1]{0,3,2,1:T(1,128)S(1)} %get-tuple-element.16, f32[256,16,16,127]{0,3,2,1:T(8,128)} %get-tuple-element.12, ...), kind=kLoop, calls=%fused_computation.24 | loop fusion | flops 201326592 | bytes 285218816 | tf_op jit(solution)/shard_map/convert_element_type | solution.py:92
  842.5 0.0 copy-done
  842.5 11.8 convolution_convert_fusion.1
  854.3 1.7 fusion.37
  856.0 0.1 collective-permute-start.4
  856.0 1.7 collective-permute-start.5
  857.8 21.8 %collective-permute-done.4 = bf16[256,1,16,128]{0,3,2,1:T(8,128)(2,1)S(1)} collective-permute-done((bf16[256,1,16,128]{0,3,2,1:T(8,128)(2,1)S(1)}, bf16[256,1,16,128]{0,3,2,1:T(8,128)(2,1)S(1)}, u32[]{:S(2)}, u32[]{:S(2)}) %collective-permute-start.4) | collective-permute-done | bytes 1048608 | tf_op jit(solution)/shard_map/ppermute | solution.py:20
  879.5 1.1 collective-permute-done.5
  880.6 3.2 pad_maximum_fusion.2
  883.9 0.0 collective-permute-start.6
  883.9 4.7 collective-permute-start.7
  888.6 0.0 all-to-all-done.2
  888.6 29.1 %copy.68 = f32[32,16,8,16,128]{4,3,1,0,2:T(8,128)} copy(bf16[32,16,8,16,128]{4,1,0,3,2:T(8,128)(2,1)} %bitcast.31) | data formatting | bytes 50331648 | tf_op jit(solution)/shard_map/convert_element_type | solution.py:99
  917.7 36.0 %reshape.83 = f32[256,32768]{1,0:T(8,128)} reshape(f32[8,32,16,16,128]{4,3,2,1,0:T(8,128)} %bitcast.58) | data formatting | bytes 67108864 | tf_op jit(solution)/shard_map/convert_element_type | solution.py:99
  953.7 33.5 %copy.59 = f32[256,32768]{0,1:T(8,128)} copy(f32[256,32768]{1,0:T(8,128)} %reshape.83) | data formatting | bytes 67108864 | tf_op jit(solution)/shard_map/convert_element_type | solution.py:99
  987.1 0.0 collective-permute-done.6
  987.1 0.0 collective-permute-done.7
  987.1 0.0 slice-start.1
  987.1 24.5 %maximum_convert_fusion.1 = f32[256,18,18,128]{0,3,2,1:T(8,128)} fusion(bf16[256,18,1,128]{0,3,2,1:T(8,128)(2,1)} %collective-permute-done.7, bf16[256,1,16,128]{0,3,2,1:T(8,128)(2,1)S(1)} %collective-permute-done.5, bf16[256,16,16,128]{0,3,2,1:T(8,128)(2,1)} %bitcast.51, bf16[256,1,16,128]{0,3,2,1:T(8,128)(2,1)S(1)} %collective-permute-done.4, ...), kind=kLoop, calls=%fused_computation.48 | loop fusion | flops 53084160 | bytes 63700992 | tf_op jit(solution)/shard_map/convert_element_type | solution.py:90
  1011.7 44.7 %fusion.35 = (f32[256,16,16,127]{0,3,2,1:T(8,128)}, f32[256,16,16,127]{0,3,2,1:T(8,128)}) fusion(f32[256,18,18,128]{0,3,2,1:T(8,128)} %maximum_convert_fusion.1), kind=kLoop, calls=%fused_computation.84 | loop fusion | bytes 133169152 | tf_op jit(solution)/shard_map/jit(_roll_static)/slice | solution.py:59
  1056.4 0.0 slice-done
  1056.4 0.0 slice-done.2
  1056.5 0.0 slice-done.3
  1056.5 0.5 maximum_convert_fusion.2
  1057.0 88.2 %fusion.5 = bf16[256,16,16,128]{0,3,2,1:T(8,128)(2,1)} fusion(f32[256,18,18,128]{0,3,2,1:T(8,128)} %maximum_convert_fusion.1, f32[256,16,16,127]{0,3,2,1:T(8,128)} %get-tuple-element.11, f32[256,16,16,1]{0,3,2,1:T(1,128)S(1)} %get-tuple-element.15, f32[256,16,16,1]{0,3,2,1:T(1,128)S(1)} %get-tuple-element.14, f32[256,16,16,127]{0,3,2,1:T(8,128)} %get-tuple-element.10, ...), kind=kLoop, calls=%fused_computation.8 | loop fusion | flops 201326592 | bytes 285218816 | tf_op jit(solution)/shard_map/convert_element_type | solution.py:92
  1145.2 33.1 %convert_multiply_fusion = (f32[256,32768]{0,1:T(8,128)}, bf16[32768,256]{1,0:T(8,128)(2,1)}) fusion(f32[256,32768]{0,1:T(8,128)} %copy.59, bf16[256,32768]{0,1:T(8,128)(2,1)} %bitcast.60, bf16[256,256]{1,0:T(8,128)(2,1)S(1)} %copy-done), kind=kOutput, calls=%fused_computation.45 | convolution fusion | flops 4320133120 | bytes 100794368 | tf_op jit(solution)/shard_map/dot_general | solution.py:95
  1178.4 0.0 copy-start.8
  1178.4 23.4 %copy.55 = bf16[256,16,16,128]{3,2,1,0:T(8,128)(2,1)} copy(bf16[256,16,16,128]{0,3,2,1:T(8,128)(2,1)} %bitcast.61) | data formatting | bytes 33554432 | tf_op jit(solution)/shard_map/reshape | solution.py:97
  1201.8 89.2 %all-to-all-start.1 = ((bf16[256,16,16,128]{3,2,1,0:T(8,128)(2,1)}), bf16[256,16,16,128]{3,2,1,0:T(8,128)(2,1)}, u32[]{:S(2)}, u32[]{:S(2)}) async-start(bf16[256,16,16,128]{3,2,1,0:T(8,128)(2,1)} %copy.55), calls=%async_computation.1 | async-start | bytes 33554432 | tf_op jit(solution)/shard_map/all_to_all | solution.py:104
  1291.1 30.6 %fusion.31 = f32[6,16,16,128]{3,0,2,1:T(8,128)S(1)} fusion(f32[16,16,128,256]{3,2,1,0:T(8,128)} %bitcast.57, f32[6,256]{1,0:T(8,128)S(1)} %stack.5, f32[256]{0:T(256)S(1)} %copy-done.8), kind=kOutput, calls=%fused_computation.61 | convolution fusion | flops 603981312 | bytes 34348032 | tf_op jit(solution)/shard_map/dot_general | solution.py:100
  1321.8 2.1 fusion.30
  1323.8 332.6 %all-to-all-done.1 = bf16[256,16,16,128]{3,2,1,0:T(8,128)(2,1)} async-done(((bf16[256,16,16,128]{3,2,1,0:T(8,128)(2,1)}), bf16[256,16,16,128]{3,2,1,0:T(8,128)(2,1)}, u32[]{:S(2)}, u32[]{:S(2)}) %all-to-all-start.1) | async-done | bytes 16777248 | tf_op jit(solution)/shard_map/all_to_all | solution.py:104
  1656.4 15.3 copy.56
  (26 shorter events, 0.1 us)
Async XLA Ops:
  0.6 841.9 %copy-start = (bf16[256,256]{1,0:T(8,128)(2,1)S(1)}, bf16[256,256]{1,0:T(8,128)(2,1)}, u32[]{:S(2)}) copy-start(bf16[256,256]{1,0:T(8,128)(2,1)} %param.11) | copy-start | bytes 393220
  17.5 370.2 %all-to-all-start = ((bf16[32,16,128,128]{3,1,0,2:T(8,128)(2,1)}), bf16[32,16,128,128]{3,1,0,2:T(8,128)(2,1)}, u32[]{:S(2)}, u32[]{:S(2)}) async-start(bf16[32,16,128,128]{3,1,0,2:T(8,128)(2,1)} %copy.48), calls=%async_computation | async-start | bytes 33554432 | tf_op jit(solution)/shard_map/all_to_all | solution.py:74
  387.7 500.8 %all-to-all-start.2 = ((bf16[32,16,128,128]{3,1,0,2:T(8,128)(2,1)}), bf16[32,16,128,128]{3,1,0,2:T(8,128)(2,1)}, u32[]{:S(2)}, u32[]{:S(2)}) async-start(bf16[32,16,128,128]{3,1,0,2:T(8,128)(2,1)} %copy.57), calls=%async_computation.2 | async-start | bytes 33554432 | tf_op jit(solution)/shard_map/all_to_all | solution.py:75
  393.5 58.8 %copy-start.1 = (f32[3,256]{1,0:T(4,128)S(1)}, f32[3,256]{1,0:T(4,128)}, u32[]{:S(2)}) copy-start(f32[3,256]{1,0:T(4,128)} %param.9) | copy-start | bytes 9220
  448.4 24.0 %collective-permute-start = (bf16[256,1,16,128]{0,3,2,1:T(8,128)(2,1)}, bf16[256,1,16,128]{0,3,2,1:T(8,128)(2,1)S(1)}, u32[]{:S(2)}, u32[]{:S(2)}) collective-permute-start(bf16[256,1,16,128]{0,3,2,1:T(8,128)(2,1)} %get-tuple-element.24), channel_id=1, source_target_pairs={{0,8},{8,16},{16,24},{24,0},{1,9},{9,17},{17,25},{25,1},{2,10},{10... | collective-permute-start | bytes 3145736 | tf_op jit(solution)/shard_map/ppermute | solution.py:20
  448.4 24.8 %collective-permute-start.1 = (bf16[256,1,16,128]{0,3,2,1:T(8,128)(2,1)S(1)}, bf16[256,1,16,128]{0,3,2,1:T(8,128)(2,1)S(1)}, u32[]{:S(2)}, u32[]{:S(2)}) collective-permute-start(bf16[256,1,16,128]{0,3,2,1:T(8,128)(2,1)S(1)} %get-tuple-element.25), channel_id=1, source_target_pairs={{8,0},{16,8},{24,16},{0,24},{9,1},{17,9},{25,17},{1,25},{10,2},{18... | collective-permute-start | bytes 3145736 | tf_op jit(solution)/shard_map/ppermute | solution.py:23
  473.2 219.6 %slice-start.4 = ((s8[16777216]{0:T(1024)(128)(4,1)}), s8[4194304]{0:T(1024)(128)(4,1)S(1)}, s32[]{:S(2)}) async-start(s8[16777216]{0:T(1024)(128)(4,1)} %bitcast.55), calls=%async_computation.7 | async-start | bytes 8388608
  476.6 216.2 %collective-permute-start.2 = (bf16[256,18,1,128]{0,3,2,1:T(8,128)(2,1)}, bf16[256,18,1,128]{0,3,2,1:T(8,128)(2,1)S(1)}, u32[]{:S(2)}, u32[]{:S(2)}) collective-permute-start(bf16[256,18,1,128]{0,3,2,1:T(8,128)(2,1)} %get-tuple-element.20), channel_id=1, source_target_pairs={{0,1},{1,2},{2,3},{3,4},{4,5},{5,6},{6,7},{7,0},{8,9},{9,10},{10,1... | collective-permute-start | bytes 3538952 | tf_op jit(solution)/shard_map/ppermute | solution.py:20
  478.5 214.3 %collective-permute-start.3 = (bf16[256,18,1,128]{0,3,2,1:T(8,128)(2,1)}, bf16[256,18,1,128]{0,3,2,1:T(8,128)(2,1)S(1)}, u32[]{:S(2)}, u32[]{:S(2)}) collective-permute-start(bf16[256,18,1,128]{0,3,2,1:T(8,128)(2,1)} %get-tuple-element.21), channel_id=1, source_target_pairs={{1,0},{2,1},{3,2},{4,3},{5,4},{6,5},{7,6},{0,7},{9,8},{10,9},{11,1... | collective-permute-start | bytes 3538952 | tf_op jit(solution)/shard_map/ppermute | solution.py:23
  481.5 211.3 %slice-start.5 = ((s8[16777216]{0:T(1024)(128)(4,1)}), s8[4194304]{0:T(1024)(128)(4,1)S(1)}, s32[]{:S(2)}) async-start(s8[16777216]{0:T(1024)(128)(4,1)} %bitcast.55), calls=%async_computation.8 | async-start | bytes 8388608
  481.5 211.3 %slice-start.6 = ((s8[16777216]{0:T(1024)(128)(4,1)}), s8[4194304]{0:T(1024)(128)(4,1)S(1)}, s32[]{:S(2)}) async-start(s8[16777216]{0:T(1024)(128)(4,1)} %bitcast.55), calls=%async_computation.9 | async-start | bytes 8388608
  481.5 211.3 %slice-start.7 = ((s8[16777216]{0:T(1024)(128)(4,1)}), s8[4194304]{0:T(1024)(128)(4,1)S(1)}, s32[]{:S(2)}) async-start(s8[16777216]{0:T(1024)(128)(4,1)} %bitcast.55), calls=%async_computation.10 | async-start | bytes 8388608
  856.0 23.6 %collective-permute-start.4 = (bf16[256,1,16,128]{0,3,2,1:T(8,128)(2,1)S(1)}, bf16[256,1,16,128]{0,3,2,1:T(8,128)(2,1)S(1)}, u32[]{:S(2)}, u32[]{:S(2)}) collective-permute-start(bf16[256,1,16,128]{0,3,2,1:T(8,128)(2,1)S(1)} %get-tuple-element.22), channel_id=1, source_target_pairs={{0,8},{8,16},{16,24},{24,0},{1,9},{9,17},{17,25},{25,1},{2,10},{10... | collective-permute-start | bytes 3145736 | tf_op jit(solution)/shard_map/ppermute | solution.py:20
  856.0 24.6 %collective-permute-start.5 = (bf16[256,1,16,128]{0,3,2,1:T(8,128)(2,1)S(1)}, bf16[256,1,16,128]{0,3,2,1:T(8,128)(2,1)S(1)}, u32[]{:S(2)}, u32[]{:S(2)}) collective-permute-start(bf16[256,1,16,128]{0,3,2,1:T(8,128)(2,1)S(1)} %get-tuple-element.23), channel_id=1, source_target_pairs={{8,0},{16,8},{24,16},{0,24},{9,1},{17,9},{25,17},{1,25},{10,2},{18... | collective-permute-start | bytes 3145736 | tf_op jit(solution)/shard_map/ppermute | solution.py:23
  883.9 103.3 %collective-permute-start.6 = (bf16[256,18,1,128]{0,3,2,1:T(8,128)(2,1)}, bf16[256,18,1,128]{0,3,2,1:T(8,128)(2,1)S(1)}, u32[]{:S(2)}, u32[]{:S(2)}) collective-permute-start(bf16[256,18,1,128]{0,3,2,1:T(8,128)(2,1)} %get-tuple-element.18), channel_id=1, source_target_pairs={{0,1},{1,2},{2,3},{3,4},{4,5},{5,6},{6,7},{7,0},{8,9},{9,10},{10,1... | collective-permute-start | bytes 3538952 | tf_op jit(solution)/shard_map/ppermute | solution.py:20
  883.9 103.3 %collective-permute-start.7 = (bf16[256,18,1,128]{0,3,2,1:T(8,128)(2,1)}, bf16[256,18,1,128]{0,3,2,1:T(8,128)(2,1)}, u32[]{:S(2)}, u32[]{:S(2)}) collective-permute-start(bf16[256,18,1,128]{0,3,2,1:T(8,128)(2,1)} %get-tuple-element.19), channel_id=1, source_target_pairs={{1,0},{2,1},{3,2},{4,3},{5,4},{6,5},{7,6},{0,7},{9,8},{10,9},{11,1... | collective-permute-start | bytes 3538952 | tf_op jit(solution)/shard_map/ppermute | solution.py:23
  987.1 69.3 %slice-start = ((s8[16777216]{0:T(1024)(128)(4,1)}), s8[4194304]{0:T(1024)(128)(4,1)S(1)}, s32[]{:S(2)}) async-start(s8[16777216]{0:T(1024)(128)(4,1)} %bitcast.52), calls=%async_computation.3 | async-start | bytes 8388608
  987.1 69.3 %slice-start.1 = ((s8[16777216]{0:T(1024)(128)(4,1)}), s8[4194304]{0:T(1024)(128)(4,1)S(1)}, s32[]{:S(2)}) async-start(s8[16777216]{0:T(1024)(128)(4,1)} %bitcast.52), calls=%async_computation.4 | async-start | bytes 8388608
  1011.7 44.7 %slice-start.2 = ((s8[16777216]{0:T(1024)(128)(4,1)}), s8[4194304]{0:T(1024)(128)(4,1)S(1)}, s32[]{:S(2)}) async-start(s8[16777216]{0:T(1024)(128)(4,1)} %bitcast.52), calls=%async_computation.5 | async-start | bytes 8388608
  1011.7 44.8 %slice-start.3 = ((s8[16777216]{0:T(1024)(128)(4,1)}), s8[4194304]{0:T(1024)(128)(4,1)S(1)}, s32[]{:S(2)}) async-start(s8[16777216]{0:T(1024)(128)(4,1)} %bitcast.52), calls=%async_computation.6 | async-start | bytes 8388608
  1178.4 112.6 %copy-start.2 = (f32[1,256]{1,0:T(1,128)S(1)}, f32[1,256]{1,0:T(1,128)}, u32[]{:S(2)}) copy-start(f32[1,256]{1,0:T(1,128)} %get-tuple-element.26) | copy-start | bytes 3076
  1178.4 112.6 %copy-start.3 = (f32[1,256]{1,0:T(1,128)S(1)}, f32[1,256]{1,0:T(1,128)}, u32[]{:S(2)}) copy-start(f32[1,256]{1,0:T(1,128)} %get-tuple-element.29) | copy-start | bytes 3076
  1178.4 112.7 %copy-start.4 = (f32[1,256]{1,0:T(1,128)S(1)}, f32[1,256]{1,0:T(1,128)}, u32[]{:S(2)}) copy-start(f32[1,256]{1,0:T(1,128)} %get-tuple-element.33) | copy-start | bytes 3076
  1178.4 112.7 %copy-start.5 = (f32[1,256]{1,0:T(1,128)S(1)}, f32[1,256]{1,0:T(1,128)}, u32[]{:S(2)}) copy-start(f32[1,256]{1,0:T(1,128)} %get-tuple-element.34) | copy-start | bytes 3076
  1178.4 112.7 %copy-start.6 = (f32[1,256]{1,0:T(1,128)S(1)}, f32[1,256]{1,0:T(1,128)}, u32[]{:S(2)}) copy-start(f32[1,256]{1,0:T(1,128)} %get-tuple-element.39) | copy-start | bytes 3076
  1178.4 112.7 %copy-start.7 = (f32[1,256]{1,0:T(1,128)S(1)}, f32[1,256]{1,0:T(1,128)}, u32[]{:S(2)}) copy-start(f32[1,256]{1,0:T(1,128)} %get-tuple-element.40) | copy-start | bytes 3076
  1178.4 112.7 %copy-start.8 = (f32[256]{0:T(256)S(1)}, f32[256]{0:T(256)}, u32[]{:S(2)}) copy-start(f32[256]{0:T(256)} %param.10) | copy-start | bytes 3076
  1201.8 454.6 %all-to-all-start.1 = ((bf16[256,16,16,128]{3,2,1,0:T(8,128)(2,1)}), bf16[256,16,16,128]{3,2,1,0:T(8,128)(2,1)}, u32[]{:S(2)}, u32[]{:S(2)}) async-start(bf16[256,16,16,128]{3,2,1,0:T(8,128)(2,1)} %copy.55), calls=%async_computation.1 | async-start | bytes 33554432 | tf_op jit(solution)/shard_map/all_to_all | solution.py:104
where the time goes:
time: 1680 us; the launch traced here: 1670 us
  waiting for transfers between devices  912 us (54%)
  local copies, waits for them, and re-layouts  317 us (19%)
  other arithmetic  230 us (14%)
  starting transfers between devices  115 us (7%)
  matrix products  96 us (6%)
    all_to_all x1, waiting for transfers between devices, per_device(): lax.all_to_all(q_init, 'orient', split_axis=2, concat_axis=0, tiled=True)  346 us
    all_to_all x1, waiting for transfers between devices, per_device(): lax.all_to_all(state, 'orient', split_axis=0, concat_axis=2, tiled=True)  333 us
    ppermute x4, waiting for transfers between devices, extended(): lax.ppermute(lax.slice_in_dim(block, block.shape[dim] - width, None, axis...  232 us
    convert_element_type x2, other arithmetic, per_device(): block_in = (moved * damping).astype(jnp.bfloat16)  176 us
    convert_element_type x3, local copies, waits for them, and re-layouts, per_device(): product = state.astype(jnp.float32) * other.astype(jnp.float32)  98.5 us
    all_to_all x1, starting transfers between devices, per_device(): lax.all_to_all(state, 'orient', split_axis=0, concat_axis=2, tiled=True)  89.2 us
    slice x2, local copies, waits for them, and re-layouts, upwind_padded(): fore_x = jnp.roll(center, -1, axis=-1) - center  87.4 us
    all_to_all x2, local copies, waits for them, and re-layouts, per_device(): lax.all_to_all(q_init, 'orient', split_axis=2, concat_axis=0, tiled=True)  52.2 us
  transfers between devices with their start and end apart: 11, of which 7 were waited for; matrix products, arithmetic and copies ran while one was open for 24% of the time, Pallas kernels for 0%

commit v1 on v0

v1 whole, which is shorter than its diff:
```python
import functools

import jax
import jax.numpy as jnp
from jax import lax
from jax.experimental import pallas as pl
from jax.experimental.pallas import tpu as pltpu
from jax.sharding import PartitionSpec as P

SHARES = (3, 3, 8, 2)

step_length = 0.3
relax_rate = 0.5
coupling = 8.0


F32 = jnp.float32
BF16 = jnp.bfloat16


def ring(count, shift):
    return [(i, (i + shift) % count) for i in range(count)]


def angle_tables(orientations):
    along_x = orientations[0]
    along_y = orientations[1]
    along_z = orientations[2]
    field_terms = jnp.stack(
        [
            along_x * along_x,
            along_y * along_y,
            along_z * along_z,
            2.0 * along_x * along_y,
            2.0 * along_x * along_z,
            2.0 * along_y * along_z,
        ]
    )
    tensor_terms = jnp.stack(
        [
            along_x * along_x - 1.0 / 3.0,
            along_y * along_y - 1.0 / 3.0,
            along_z * along_z - 1.0 / 3.0,
            along_x * along_y,
            along_x * along_z,
            along_y * along_z,
        ]
    )
    return (field_terms, tensor_terms)


def stencil_weights(orientations):
    low = step_length * jnp.maximum(orientations, 0.0)
    high = -step_length * jnp.minimum(orientations, 0.0)
    middle = 1.0 - jnp.sum(low + high, axis=0)
    return jnp.stack([low[0], high[0], low[1], high[1], low[2], high[2], middle])


def advect_kernel(has_low, has_high, *refs):
    refs = list(refs)
    coef, below, centre, above = refs[:4]
    rest = refs[4:]
    low = rest.pop(0) if has_low else None
    high = rest.pop(0) if has_high else None
    field, out, staged = rest
    z = pl.program_id(0)
    last = pl.num_programs(0) - 1
    count, width = staged.shape[0], staged.shape[1]
    owners, rows = out.shape[0], out.shape[2]

    def one(o, carry):
        f = centre[o, 0].astype(F32)
        zm = below[o, 0].astype(F32)
        if has_low:
            zm = jnp.where(z == 0, low[o, 0].astype(F32), zm)
        zp = above[o, 0].astype(F32)
        if has_high:
            zp = jnp.where(z == last, high[o, 0].astype(F32), zp)
        lanes = f.shape[1]
        moved = coef[6, o] * f
        moved += coef[0, o] * pltpu.roll(f, 1, 1) + coef[1, o] * pltpu.roll(f, lanes - 1, 1)
        moved += coef[2, o] * pltpu.roll(f, 1, 0) + coef[3, o] * pltpu.roll(f, width - 1, 0)
        moved += coef[4, o] * zm + coef[5, o] * zp
        exponent = coef[7, o] * field[0, 0].astype(F32)
        for c in range(1, 6):
            exponent += coef[7 + c, o] * field[c, 0].astype(F32)
        staged[o] = moved * jnp.exp(exponent)
        return carry

    lax.fori_loop(0, count, one, 0)
    for owner in range(owners):
        part = staged[:, owner * rows : (owner + 1) * rows, :]
        out[owner, 0] = jnp.swapaxes(part, 0, 1).astype(BF16)


def advect(coef, q, low, high, field, start, depth, owners):
    count, layers, width, lanes = q.shape
    rows = width // owners
    block = (count, 1, width, lanes)
    in_specs = [
        pl.BlockSpec(memory_space=pltpu.SMEM),
        pl.BlockSpec(block, lambda z: (0, jnp.maximum(start + z - 1, 0), 0, 0)),
        pl.BlockSpec(block, lambda z: (0, start + z, 0, 0)),
        pl.BlockSpec(block, lambda z: (0, jnp.minimum(start + z + 1, layers - 1), 0, 0)),
    ]
    operands = [coef, q, q, q]
    for halo in (low, high):
        if halo is not None:
            in_specs.append(pl.BlockSpec(block, lambda z: (0, 0, 0, 0)))
            operands.append(halo)
    in_specs.append(pl.BlockSpec((6, 1, width, lanes), lambda z: (0, start + z, 0, 0)))
    operands.append(field)
    cells = count * depth * width * lanes
    return pl.pallas_call(
        functools.partial(advect_kernel, low is not None, high is not None),
        grid=(depth,),
        in_specs=in_specs,
        out_specs=pl.BlockSpec((owners, 1, rows, count, lanes), lambda z: (0, z, 0, 0, 0)),
        out_shape=jax.ShapeDtypeStruct((owners, depth, rows, count, lanes), BF16),
        scratch_shapes=[pltpu.VMEM((count, width, lanes), F32)],
        cost_estimate=pl.CostEstimate(
            flops=30 * cells, transcendentals=cells, bytes_accessed=8 * cells
        ),
        name="advect_first",
    )(*operands)


def turn_kernel(rotation, block, out):
    owners, rows, count, lanes = block.shape[0], block.shape[2], block.shape[3], block.shape[4]
    total = owners * count
    pair = 2 if rows % 2 == 0 else 1

    def one(step, carry):
        columns = []
        for j in range(pair):
            y = step * pair + j
            columns.append(block[:, 0, y].astype(F32).reshape(total, lanes).astype(BF16))
        wide = jnp.concatenate(columns, axis=1) if pair > 1 else columns[0]
        turned = jnp.dot(rotation[...], wide, preferred_element_type=F32).astype(BF16)
        for j in range(pair):
            out[0, step * pair + j] = turned[:, j * lanes : (j + 1) * lanes]
        return carry

    lax.fori_loop(0, rows // pair, one, 0)


def turn(rotation, block):
    owners, depth, rows, count, lanes = block.shape
    total = owners * count
    cells = total * depth * rows * lanes
    return pl.pallas_call(
        turn_kernel,
        grid=(depth,),
        in_specs=[
            pl.BlockSpec((total, total), lambda z: (0, 0)),
            pl.BlockSpec((owners, 1, rows, count, lanes), lambda z: (0, z, 0, 0, 0)),
        ],
        out_specs=pl.BlockSpec((1, rows, total, lanes), lambda z: (z, 0, 0, 0)),
        out_shape=jax.ShapeDtypeStruct((depth, rows, total, lanes), BF16),
        cost_estimate=pl.CostEstimate(
            flops=2 * total * cells, transcendentals=0, bytes_accessed=4 * cells
        ),
        name="turn_first",
    )(rotation, block)


def advect_turn_kernel(
    rotation, weights, terms, below, centre, above, low, high, south, north, field, out, mixed, powers
):
    z = pl.program_id(0)
    last = pl.num_programs(0) - 1
    rows, total, lanes = centre.shape[1:]
    owners, count = out.shape[0], out.shape[3]
    pair = 2 if rows % 2 == 0 else 1
    piece = 64 if total % 64 == 0 else total

    def one(step, carry):
        for j in range(pair):
            y = step * pair + j
            powers[...] = jnp.dot(terms[...], field[0, y], preferred_element_type=F32)
            for base in range(0, total, piece):
                part = pl.ds(base, piece)
                f = centre[0, y, part].astype(F32)
                ym = centre[0, jnp.maximum(y - 1, 0), part].astype(F32)
                ym = jnp.where(y == 0, south[0, 0, part].astype(F32), ym)
                yp = centre[0, jnp.minimum(y + 1, rows - 1), part].astype(F32)
                yp = jnp.where(y == rows - 1, north[0, 0, part].astype(F32), yp)
                zm = below[0, y, part].astype(F32)
                zm = jnp.where(z == 0, low[0, y, part].astype(F32), zm)
                zp = above[0, y, part].astype(F32)
                zp = jnp.where(z == last, high[0, y, part].astype(F32), zp)
                moved = weights[6, part] * f
                moved += weights[0, part] * pltpu.roll(f, 1, 1)
                moved += weights[1, part] * pltpu.roll(f, lanes - 1, 1)
                moved += weights[2, part] * ym + weights[3, part] * yp
                moved += weights[4, part] * zm + weights[5, part] * zp
                mixed[part, j * lanes : (j + 1) * lanes] = (
                    moved * jnp.exp(powers[part])
                ).astype(BF16)
        turned = jnp.dot(rotation[...], mixed[...], preferred_element_type=F32)
        for j in range(pair):
            column = turned[:, j * lanes : (j + 1) * lanes]
            out[:, 0, step * pair + j] = column.reshape(owners, count, lanes).astype(BF16)
        return carry

    lax.fori_loop(0, rows // pair, one, 0)


def advect_turn(rotation, weights, terms, state, low, high, south, north, field, owners):
    depth, rows, total, lanes = state.shape
    count = total // owners
    layer = (1, rows, total, lanes)
    edge = (1, 1, total, lanes)
    pair = 2 if rows % 2 == 0 else 1
    cells = total * depth * rows * lanes
    fixed = lambda z: (0, 0, 0, 0)
    here = lambda z: (z, 0, 0, 0)
    return pl.pallas_call(
        advect_turn_kernel,
        grid=(depth,),
        in_specs=[
            pl.BlockSpec((total, total), lambda z: (0, 0)),
            pl.BlockSpec(weights.shape, lambda z: (0, 0, 0)),
            pl.BlockSpec(terms.shape, lambda z: (0, 0)),
            pl.BlockSpec(layer, lambda z: (jnp.maximum(z - 1, 0), 0, 0, 0)),
            pl.BlockSpec(layer, here),
            pl.BlockSpec(layer, lambda z: (jnp.minimum(z + 1, depth - 1), 0, 0, 0)),
            pl.BlockSpec(layer, fixed),
            pl.BlockSpec(layer, fixed),
            pl.BlockSpec(edge, here),
            pl.BlockSpec(edge, here),
            pl.BlockSpec((1,) + field.shape[1:], here),
        ],
        out_specs=pl.BlockSpec((owners, 1, rows, count, lanes), lambda z: (0, z, 0, 0, 0)),
        out_shape=jax.ShapeDtypeStruct((owners, depth, rows, count, lanes), BF16),
        scratch_shapes=[
            pltpu.VMEM((total, pair * lanes), BF16),
            pltpu.VMEM((total, lanes), F32),
        ],
        cost_estimate=pl.CostEstimate(
            flops=2 * total * cells, transcendentals=cells, bytes_accessed=8 * cells
        ),
        name="advect_turn",
    )(rotation, weights, terms, state, state, state, low, high, south, north, field)


def gather_kernel(*refs):
    coef, block, partner = refs[:3]
    state, partial = refs[-2:]
    owners, rows, count = block.shape[0], block.shape[2], block.shape[3]
    for owner in range(owners):
        part = pl.ds(owner * rows, rows)
        mine = jnp.swapaxes(block[owner, 0].astype(F32), 0, 1)
        state[:, 0, part, :] = mine.astype(BF16)
        sums = [None] * 6
        for o in range(count):
            product = mine[o] * partner[o, 0, part, :].astype(F32)
            for c in range(6):
                term = coef[c, o] * product
                sums[c] = term if sums[c] is None else sums[c] + term
        for c in range(6):
            partial[owner, c, 0] = sums[c].astype(partial.dtype)


def gather(coef, block, partner, state, start, kind):
    owners, depth, rows, count, lanes = block.shape
    width = partner.shape[2]
    cells = owners * depth * rows * count * lanes
    slab = pl.BlockSpec((count, 1, width, lanes), lambda z: (0, start + z, 0, 0))
    operands = [coef, block, partner]
    in_specs = [
        pl.BlockSpec(memory_space=pltpu.SMEM),
        pl.BlockSpec((owners, 1, rows, count, lanes), lambda z: (0, z, 0, 0, 0)),
        slab,
    ]
    aliases = {}
    if state is not None:
        aliases = {3: 0}
        operands.append(state)
        in_specs.append(pl.BlockSpec(memory_space=pl.ANY))
    return pl.pallas_call(
        gather_kernel,
        grid=(depth,),
        in_specs=in_specs,
        out_specs=[
            slab,
            pl.BlockSpec((owners, 6, 1, rows, lanes), lambda z: (0, 0, z, 0, 0)),
        ],
        out_shape=[
            jax.ShapeDtypeStruct(partner.shape, BF16),
            jax.ShapeDtypeStruct((owners, 6, depth, rows, lanes), kind),
        ],
        input_output_aliases=aliases,
        cost_estimate=pl.CostEstimate(
            flops=14 * cells, transcendentals=0, bytes_accessed=6 * cells
        ),
        name="gather_last",
    )(*operands)


def exchange(block):
    return lax.all_to_all(block, "orient", split_axis=0, concat_axis=0, tiled=True)


def halve(block):
    owners = lax.axis_size("orient")
    me = lax.axis_index("orient")
    rest = block.shape[1:]
    stride = 1
    held = block
    kept = owners
    while kept > 1:
        bit = (me // stride) % 2
        pairs = held.reshape((kept // 2, 2) + rest)
        mine = lax.dynamic_index_in_dim(pairs, bit, 1, keepdims=False)
        theirs = lax.dynamic_index_in_dim(pairs, 1 - bit, 1, keepdims=False)
        if kept == 2:
            theirs = theirs.astype(BF16)
        came = lax.ppermute(theirs, "orient", [(i, i ^ stride) for i in range(owners)])
        held = mine.astype(F32) + came.astype(F32)
        kept //= 2
        stride *= 2
    return held[0]


def chunk_sizes(layers):
    whole = sum(SHARES)
    sizes = [max(1, layers * share // whole) for share in SHARES]
    sizes[2] += layers - sum(sizes)
    return sizes


def staged_device(q_init, partner, field, orientations, orient_weight, rotation):
    owners = lax.axis_size("orient")
    slabs = lax.axis_size("space")
    me = lax.axis_index("orient")
    count, layers, width, lanes = q_init.shape
    rows = width // owners
    sizes = chunk_sizes(layers)
    chunks = len(sizes)
    starts = [sum(sizes[:c]) for c in range(chunks)]

    first = lax.ppermute(q_init[:, layers - 1 :], "space", ring(slabs, 1))
    final = lax.ppermute(q_init[:, :1], "space", ring(slabs, -1))

    field_terms, tensor_terms = angle_tables(orientations)
    weights = stencil_weights(orientations)
    exponent_terms = -step_length * field_terms
    local_coef = lax.dynamic_slice_in_dim(
        jnp.concatenate([weights, exponent_terms]), me * count, count, 1
    )
    local_tensor = lax.dynamic_slice_in_dim(
        tensor_terms * orient_weight[None, :], me * count, count, 1
    )
    wide_weights = jnp.broadcast_to(weights[:, :, None], weights.shape + (lanes,))
    top = lax.reduce_precision(exponent_terms, 8, 7)
    left = exponent_terms - top
    centre = lax.reduce_precision(left, 8, 7)
    split_terms = jnp.concatenate([top, centre, left - centre]).astype(BF16).T
    own_field = lax.dynamic_slice_in_dim(field, me * rows, rows, 2)
    row_field = jnp.transpose(own_field, (1, 2, 0, 3))
    row_field = jnp.concatenate([row_field] * 3, axis=2)
    padding = 32 - split_terms.shape[1]
    split_terms = jnp.pad(split_terms, ((0, 0), (0, padding)))
    row_field = jnp.pad(row_field, ((0, 0), (0, 0), (0, padding), (0, 0)))

    turned = {}
    souths = {}
    norths = {}
    for c in ORDER:
        sent = advect(
            local_coef,
            q_init,
            first if c == 0 else None,
            final if c == chunks - 1 else None,
            field,
            starts[c],
            sizes[c],
            owners,
        )
        got = exchange(sent)
        turned[c] = turn(rotation, got)
        souths[c] = lax.ppermute(turned[c][:, rows - 1 :], "orient", ring(owners, 1))
        norths[c] = lax.ppermute(turned[c][:, :1], "orient", ring(owners, -1))
    under = lax.ppermute(turned[chunks - 1][-1:], "space", ring(slabs, 1))
    over = lax.ppermute(turned[0][:1], "space", ring(slabs, -1))

    state = None
    sums = {}
    for c in ORDER:
        low = under if c == 0 else turned[c - 1][-1:]
        high = over if c == chunks - 1 else turned[c + 1][:1]
        sent = advect_turn(
            rotation,
            wide_weights,
            split_terms,
            turned[c],
            low,
            high,
            souths[c],
            norths[c],
            row_field[starts[c] : starts[c] + sizes[c]],
            owners,
        )
        got = exchange(sent)
        closing = c == ORDER[-1]
        state, partial = gather(
            local_tensor, got, partner, state, starts[c], BF16 if closing else F32
        )
        if closing or owners & (owners - 1):
            sums[c] = jnp.sum(exchange(partial).astype(F32), axis=0)
        else:
            sums[c] = halve(partial)
    tensor = jnp.concatenate([sums[c] for c in range(chunks)], axis=1)
    new_field = (1.0 - relax_rate) * own_field.astype(F32) + relax_rate * coupling * tensor
    return (state, new_field)


ORDER = (1, 2, 0, 3)


def solution(mesh):
    in_specs = (
        P("orient", "space", None, None),
        P("orient", "space", None, None),
        P(None, "space", None, None),
        P(),
        P(),
        P(),
    )
    out_specs = (P("orient", "space", None, None), P(None, "space", "orient", None))
    return jax.shard_map(
        staged_device, mesh=mesh, in_specs=in_specs, out_specs=out_specs, check_vma=False
    )
```

time: 1680 us -> 1010 us (0.60)
  waiting for transfers between devices: 912 us -> 592 us
  local copies, waits for them, and re-layouts: 317 us -> 45.2 us
  Pallas kernels: 0 us -> 228 us
  other arithmetic: 230 us -> 11.2 us
  matrix products: 96 us -> 0 us
  starting transfers between devices: 115 us -> 134 us
    all_to_all x3 -> x9, waiting for transfers between devices: 679 us -> 167 us  [exchange(): lax.all_to_all(block, 'orient', split_axis=0, concat_axis=0, tiled=True)]
    pallas_call x0 -> x16, Pallas kernels: none -> 228 us  [the longest x4 81.5 us: advect_turn(): pl.pallas_call(advect_turn_kernel, grid=(depth,), in_specs=[pl.BlockSpec(...]
    convert_element_type x4 -> x0, other arithmetic: 219 us -> none  [the longest x2 176 us: per_device(): block_in = (moved * damping).astype(jnp.bfloat16)]
    ppermute x8 -> x21, waiting for transfers between devices: 233 us -> 425 us  [the longest x4 335 us: staged_device(): souths[c] = lax.ppermute(turned[c][:, rows - 1:], 'orient', ring(owners, 1))]
    convert_element_type x3, local copies, waits for them, and re-layouts: 98.5 us -> 0.11 us  [halve(): theirs = theirs.astype(BF16)]
    dot_general x3 -> x0, matrix products: 75.6 us -> none  [the longest x2 44.9 us: per_device(): jnp.dot(rotation, flat, preferred_element_type=jnp.float32)]
    slice x4 -> x13, local copies, waits for them, and re-layouts: 91.8 us -> 22.5 us  [the longest x2 6.15 us: staged_device(): high = over if c == chunks - 1 else turned[c + 1][:1]]
    all_to_all x3 -> x0, local copies, waits for them, and re-layouts: 67.5 us -> none  [the longest x2 52.2 us: per_device(): lax.all_to_all(q_init, 'orient', split_axis=2, concat_axis=0, tiled=True)]
  transfers between devices with their start and end apart: 11 -> 30, of which waited for: 7 -> 17; matrix products, arithmetic and copies ran while one was open for 24% -> 4% of each run, Pallas kernels for 0% -> 21%
where the time goes in v1:
time: 1010 us
  waiting for transfers between devices  592 us (59%)
  Pallas kernels  228 us (23%)
  starting transfers between devices  134 us (13%)
  local copies, waits for them, and re-layouts  45.2 us (4%)
  other arithmetic  11.2 us (1%)
    ppermute x4, waiting for transfers between devices, staged_device(): souths[c] = lax.ppermute(turned[c][:, rows - 1:], 'orient', ring(owners, 1))  335 us
    all_to_all x9, waiting for transfers between devices, exchange(): lax.all_to_all(block, 'orient', split_axis=0, concat_axis=0, tiled=True)  167 us
    all_to_all x9, starting transfers between devices, exchange(): lax.all_to_all(block, 'orient', split_axis=0, concat_axis=0, tiled=True)  99.3 us
    pallas_call x4, Pallas kernels, advect_turn(): pl.pallas_call(advect_turn_kernel, grid=(depth,), in_specs=[pl.BlockSpec(...  81.5 us
    pallas_call x4, Pallas kernels, advect(): pl.pallas_call(functools.partial(advect_kernel, low is not None, high is...  71.9 us
    ppermute x9, waiting for transfers between devices, halve(): lax.ppermute(theirs, 'orient', [(i, i ^ stride) for i in range(owners)])  65 us
    pallas_call x4, Pallas kernels, gather(): pl.pallas_call(gather_kernel, grid=(depth,), in_specs=in_specs, out_specs...  39.7 us
    pallas_call x4, Pallas kernels, turn(): pl.pallas_call(turn_kernel, grid=(depth,), in_specs=[pl.BlockSpec((total,...  34.8 us
  transfers between devices with their start and end apart: 30, of which 17 were waited for; matrix products, arithmetic and copies ran while one was open for 4% of the time, Pallas kernels for 21%

profile of v1, /device:TPU:0, one launch (start us, length us, event | category | flops | bytes accessed | tf_op | source)
XLA Modules:
  0.0 1010.9 jit_solution(1216723530038623717)
XLA Ops:
  0.6 2.7 fusion.8
  3.4 2.4 collective-permute-start
  7.9 10.2 %collective-permute-done.refs_4_ = bf16[32,1,128,128]{3,2,1,0:T(8,128)(2,1)S(1)} collective-permute-done((bf16[32,1,128,128]{3,2,1,0:T(8,128)(2,1)S(1)}, bf16[32,1,128,128]{3,2,1,0:T(8,128)(2,1)S(1)}, u32[]{:S(2)}, u32[]{:S(2)}) %collective-permute-start) | collective-permute-done | bytes 1048608 | tf_op jit(solution)/shard_map/ppermute | solution.py:344
  19.1 11.0 %advect_first.4 = bf16[8,2,16,32,128]{4,3,2,1,0:T(8,128)(2,1)} custom-call(f32[13,32]{1,0:T(8,128)} %constant_dynamic-slice_fusion.6.refs_0_, bf16[32,16,128,128]{3,2,1,0:T(8,128)(2,1)} %refs_3_.7, bf16[32,16,128,128]{3,2,1,0:T(8,128)(2,1)} %refs_3_.7, bf16[32,16,128,128]{3,2,1,0:T(8,128)(2,1)} %refs_3_.7, bf16[32,1,128,128]{3,2,1,0:T(8,128)(2,1)} %copy-done.7, ...), custom_call_target="tpu_custom_call" | custom-call | flops 31457280 | bytes 8388608 | tf_op jit(solution)/shard_map/advect_first/pallas_call | solution.py:114
  30.1 5.8 all-to-all-start
  35.9 13.8 %advect_first.7 = bf16[8,3,16,32,128]{4,3,2,1,0:T(8,128)(2,1)} custom-call(f32[13,32]{1,0:T(8,128)} %constant_dynamic-slice_fusion.6.refs_0_, bf16[32,16,128,128]{3,2,1,0:T(8,128)(2,1)} %refs_3_.7, bf16[32,16,128,128]{3,2,1,0:T(8,128)(2,1)} %refs_3_.7, bf16[32,16,128,128]{3,2,1,0:T(8,128)(2,1)} %refs_3_.7, bf16[6,16,128,128]{3,2,1,0:T(8,128)(2,1)} %refs_4_.3), custom_call_target="tpu_custom_call" | custom-call | flops 47185920 | bytes 12582912 | tf_op jit(solution)/shard_map/advect_first/pallas_call | solution.py:114
  49.7 35.5 %all-to-all-done.block = bf16[8,2,16,32,128]{4,3,2,1,0:T(8,128)(2,1)S(1)} async-done(((bf16[8,2,16,32,128]{4,3,2,1,0:T(8,128)(2,1)}), bf16[8,2,16,32,128]{4,3,2,1,0:T(8,128)(2,1)S(1)}, u32[]{:S(2)}, u32[]{:S(2)}) %all-to-all-start) | async-done | bytes 2097184 | tf_op jit(solution)/shard_map/all_to_all | solution.py:302
  86.5 3.7 all-to-all-start.4
  90.2 14.5 %collective-permute-done.1.refs_4_ = bf16[32,1,128,128]{3,2,1,0:T(8,128)(2,1)} collective-permute-done((bf16[32,1,128,128]{3,2,1,0:T(8,128)(2,1)}, bf16[32,1,128,128]{3,2,1,0:T(8,128)(2,1)}, u32[]{:S(2)}, u32[]{:S(2)}) %collective-permute-start.1) | collective-permute-done | bytes 1048608 | tf_op jit(solution)/shard_map/ppermute | solution.py:343
  104.7 15.0 %advect_first.6 = bf16[8,3,16,32,128]{4,3,2,1,0:T(8,128)(2,1)} custom-call(f32[13,32]{1,0:T(8,128)} %constant_dynamic-slice_fusion.6.refs_0_, bf16[32,16,128,128]{3,2,1,0:T(8,128)(2,1)} %refs_3_.7, bf16[32,16,128,128]{3,2,1,0:T(8,128)(2,1)} %refs_3_.7, bf16[32,16,128,128]{3,2,1,0:T(8,128)(2,1)} %refs_3_.7, ...), custom_call_target="tpu_custom_call" | custom-call | flops 47185920 | bytes 12582912 | tf_op jit(solution)/shard_map/advect_first/pallas_call | solution.py:114
  119.8 41.3 %all-to-all-done.4.block = bf16[8,3,16,32,128]{4,3,2,1,0:T(8,128)(2,1)S(1)} async-done(((bf16[8,3,16,32,128]{4,3,2,1,0:T(8,128)(2,1)}), bf16[8,3,16,32,128]{4,3,2,1,0:T(8,128)(2,1)S(1)}, u32[]{:S(2)}, u32[]{:S(2)}) %all-to-all-start.4) | async-done | bytes 3145760 | tf_op jit(solution)/shard_map/all_to_all | solution.py:302
  162.7 4.5 all-to-all-start.2
  167.2 32.1 %advect_first.5 = bf16[8,8,16,32,128]{4,3,2,1,0:T(8,128)(2,1)} custom-call(f32[13,32]{1,0:T(8,128)} %constant_dynamic-slice_fusion.6.refs_0_, bf16[32,16,128,128]{3,2,1,0:T(8,128)(2,1)} %refs_3_.7, bf16[32,16,128,128]{3,2,1,0:T(8,128)(2,1)} %refs_3_.7, bf16[32,16,128,128]{3,2,1,0:T(8,128)(2,1)} %refs_3_.7, bf16[6,16,128,128]{3,2,1,0:T(8,128)(2,1)} %refs_4_.3), custom_call_target="tpu_custom_call" | custom-call | flops 125829120 | bytes 33554432 | tf_op jit(solution)/shard_map/advect_first/pallas_call | solution.py:114
  199.3 38.1 %all-to-all-done.2.block = bf16[8,3,16,32,128]{4,3,2,1,0:T(8,128)(2,1)} async-done(((bf16[8,3,16,32,128]{4,3,2,1,0:T(8,128)(2,1)}), bf16[8,3,16,32,128]{4,3,2,1,0:T(8,128)(2,1)}, u32[]{:S(2)}, u32[]{:S(2)}) %all-to-all-start.2) | async-done | bytes 3145760 | tf_op jit(solution)/shard_map/all_to_all | solution.py:302
  237.4 5.0 all-to-all-start.1
  244.6 6.1 turn_first.4.below.centre.above
  250.7 3.1 fusion.16
  255.5 6.9 turn_first.7.below.centre.above
  262.4 7.0 turn_first.6.below.centre.above
  270.5 1.9 collective-permute-start.6
  272.4 2.8 collective-permute-start.7
  276.8 108.8 %collective-permute-done.6.south = bf16[3,1,256,128]{3,2,1,0:T(8,128)(2,1)} collective-permute-done((bf16[3,1,256,128]{3,2,1,0:T(8,128)(2,1)S(1)}, bf16[3,1,256,128]{3,2,1,0:T(8,128)(2,1)}, u32[]{:S(2)}, u32[]{:S(2)}) %collective-permute-start.6) | collective-permute-done | bytes 196640 | tf_op jit(solution)/shard_map/ppermute | solution.py:383
  386.8 16.3 %advect_turn.5 = bf16[8,3,16,32,128]{4,3,2,1,0:T(8,128)(2,1)} custom-call(bf16[256,256]{1,0:T(8,128)(2,1)} %rotation.15, f32[7,256,128]{2,1,0:T(8,128)} %broadcast_in_dim.2.weights, bf16[256,32]{1,0:T(8,128)(2,1)} %pad.8.clone.terms, bf16[3,16,256,128]{3,2,1,0:T(8,128)(2,1)} %turn_first.6.below.centre.above, ...), custom_call_target="tpu_custom_call" | custom-call | flops 805306368 | bytes 12582912 | tf_op jit(solution)/shard_map/advect_turn/pallas_call | solution.py:218
  403.2 23.3 %all-to-all-done.1.block = bf16[8,8,16,32,128]{4,3,2,1,0:T(8,128)(2,1)} async-done(((bf16[8,8,16,32,128]{4,3,2,1,0:T(8,128)(2,1)}), bf16[8,8,16,32,128]{4,3,2,1,0:T(8,128)(2,1)}, u32[]{:S(2)}, u32[]{:S(2)}) %all-to-all-start.1) | async-done | bytes 8388640 | tf_op jit(solution)/shard_map/all_to_all | solution.py:302
  426.5 22.4 %all-to-all-start.5 = ((bf16[8,3,16,32,128]{4,3,2,1,0:T(8,128)(2,1)}), bf16[8,3,16,32,128]{4,3,2,1,0:T(8,128)(2,1)}, u32[]{:S(2)}, u32[]{:S(2)}) async-start(bf16[8,3,16,32,128]{4,3,2,1,0:T(8,128)(2,1)} %advect_turn.5), calls=%async_computation.5 | async-start | bytes 6291456 | tf_op jit(solution)/shard_map/all_to_all | solution.py:302
  449.7 2.0 collective-permute-start.10
  451.7 2.7 collective-permute-start.11
  454.4 3.1 fusion.12
  457.5 14.7 %turn_first.5.below.centre.above = bf16[8,16,256,128]{3,2,1,0:T(8,128)(2,1)} custom-call(bf16[256,256]{1,0:T(8,128)(2,1)} %rotation.15, bf16[8,8,16,32,128]{4,3,2,1,0:T(8,128)(2,1)} %all-to-all-done.1.block), custom_call_target="tpu_custom_call" | custom-call | flops 2147483648 | bytes 16777216 | tf_op jit(solution)/shard_map/turn_first/pallas_call | solution.py:151
  472.3 3.1 fusion.9
  475.4 33.4 %collective-permute-done.10.south = bf16[3,1,256,128]{3,2,1,0:T(8,128)(2,1)S(1)} collective-permute-done((bf16[3,1,256,128]{3,2,1,0:T(8,128)(2,1)}, bf16[3,1,256,128]{3,2,1,0:T(8,128)(2,1)S(1)}, u32[]{:S(2)}, u32[]{:S(2)}) %collective-permute-start.10) | collective-permute-done | bytes 196640 | tf_op jit(solution)/shard_map/ppermute | solution.py:383
  509.6 16.3 %advect_turn.7 = bf16[8,3,16,32,128]{4,3,2,1,0:T(8,128)(2,1)} custom-call(bf16[256,256]{1,0:T(8,128)(2,1)} %rotation.15, f32[7,256,128]{2,1,0:T(8,128)} %broadcast_in_dim.2.weights, bf16[256,32]{1,0:T(8,128)(2,1)} %pad.8.clone.terms, bf16[3,16,256,128]{3,2,1,0:T(8,128)(2,1)} %turn_first.7.below.centre.above, ...), custom_call_target="tpu_custom_call" | custom-call | flops 805306368 | bytes 12582912 | tf_op jit(solution)/shard_map/advect_turn/pallas_call | solution.py:218
  525.9 18.6 %all-to-all-start.7 = ((bf16[8,3,16,32,128]{4,3,2,1,0:T(8,128)(2,1)}), bf16[8,3,16,32,128]{4,3,2,1,0:T(8,128)(2,1)S(1)}, u32[]{:S(2)}, u32[]{:S(2)}) async-start(bf16[8,3,16,32,128]{4,3,2,1,0:T(8,128)(2,1)} %advect_turn.7), calls=%async_computation.7 | async-start | bytes 6291456 | tf_op jit(solution)/shard_map/all_to_all | solution.py:302
  545.8 2.1 collective-permute-start.8
  547.9 2.8 collective-permute-start.9
  550.6 2.3 slice.144.field
  552.9 58.1 %collective-permute-done.8.south = bf16[8,1,256,128]{3,2,1,0:T(8,128)(2,1)} collective-permute-done((bf16[8,1,256,128]{3,2,1,0:T(8,128)(2,1)S(1)}, bf16[8,1,256,128]{3,2,1,0:T(8,128)(2,1)}, u32[]{:S(2)}, u32[]{:S(2)}) %collective-permute-start.8) | collective-permute-done | bytes 524320 | tf_op jit(solution)/shard_map/ppermute | solution.py:383
  611.0 36.6 %advect_turn.6 = bf16[8,8,16,32,128]{4,3,2,1,0:T(8,128)(2,1)} custom-call(bf16[256,256]{1,0:T(8,128)(2,1)} %rotation.15, f32[7,256,128]{2,1,0:T(8,128)} %broadcast_in_dim.2.weights, bf16[256,32]{1,0:T(8,128)(2,1)} %pad.8.clone.terms, bf16[8,16,256,128]{3,2,1,0:T(8,128)(2,1)} %turn_first.5.below.centre.above, ...), custom_call_target="tpu_custom_call" | custom-call | flops 2147483648 | bytes 33554432 | tf_op jit(solution)/shard_map/advect_turn/pallas_call | solution.py:218
  647.6 1.7 copy-done.2
  649.3 17.6 %all-to-all-start.6 = ((bf16[8,8,16,32,128]{4,3,2,1,0:T(8,128)(2,1)}), bf16[8,8,16,32,128]{4,3,2,1,0:T(8,128)(2,1)}, u32[]{:S(2)}, u32[]{:S(2)}) async-start(bf16[8,8,16,32,128]{4,3,2,1,0:T(8,128)(2,1)} %advect_turn.6), calls=%async_computation.6 | async-start | bytes 16777216 | tf_op jit(solution)/shard_map/all_to_all | solution.py:302
  669.0 1.8 collective-permute-start.3
  670.8 3.0 collective-permute-start.4
  675.4 134.6 %collective-permute-done.3.south = bf16[2,1,256,128]{3,2,1,0:T(8,128)(2,1)S(1)} collective-permute-done((bf16[2,1,256,128]{3,2,1,0:T(8,128)(2,1)S(1)}, bf16[2,1,256,128]{3,2,1,0:T(8,128)(2,1)S(1)}, u32[]{:S(2)}, u32[]{:S(2)}) %collective-permute-start.3) | collective-permute-done | bytes 131104 | tf_op jit(solution)/shard_map/ppermute | solution.py:383
  811.0 12.3 %advect_turn.4 = bf16[8,2,16,32,128]{4,3,2,1,0:T(8,128)(2,1)} custom-call(bf16[256,256]{1,0:T(8,128)(2,1)} %rotation.15, f32[7,256,128]{2,1,0:T(8,128)} %broadcast_in_dim.2.weights, bf16[256,32]{1,0:T(8,128)(2,1)} %pad.8.clone.terms, bf16[2,16,256,128]{3,2,1,0:T(8,128)(2,1)} %turn_first.4.below.centre.above, ...), custom_call_target="tpu_custom_call" | custom-call | flops 536870912 | bytes 8388608 | tf_op jit(solution)/shard_map/advect_turn/pallas_call | solution.py:218
  823.4 29.0 %all-to-all-done.6.refs_1_ = bf16[8,8,16,32,128]{4,3,2,1,0:T(8,128)(2,1)} async-done(((bf16[8,8,16,32,128]{4,3,2,1,0:T(8,128)(2,1)}), bf16[8,8,16,32,128]{4,3,2,1,0:T(8,128)(2,1)}, u32[]{:S(2)}, u32[]{:S(2)}) %all-to-all-start.6) | async-done | bytes 8388640 | tf_op jit(solution)/shard_map/all_to_all | solution.py:302
  852.4 18.2 %all-to-all-start.3 = ((bf16[8,2,16,32,128]{4,3,2,1,0:T(8,128)(2,1)}), bf16[8,2,16,32,128]{4,3,2,1,0:T(8,128)(2,1)S(1)}, u32[]{:S(2)}, u32[]{:S(2)}) async-start(bf16[8,2,16,32,128]{4,3,2,1,0:T(8,128)(2,1)} %advect_turn.4), calls=%async_computation.3 | async-start | bytes 4194304 | tf_op jit(solution)/shard_map/all_to_all | solution.py:302
  871.4 8.1 gather_last.4
  880.6 2.1 collective-permute-start.15
  882.7 17.5 %gather_last.5 = (bf16[32,16,128,128]{3,2,1,0:T(8,128)(2,1)}, f32[8,6,8,16,128]{4,3,2,1,0:T(8,128)}) custom-call(f32[6,32]{1,0:T(8,128)} %fusion.7.refs_0_, bf16[8,8,16,32,128]{4,3,2,1,0:T(8,128)(2,1)} %all-to-all-done.6.refs_1_, bf16[32,16,128,128]{3,2,1,0:T(8,128)(2,1)} %refs_2_.15, ...), custom_call_target="tpu_custom_call", output_to_operand_aliasing={{0}: (3, {})} | custom-call | flops 58720256 | bytes 25165824 | tf_op jit(solution)/shard_map/gather_last/pallas_call | solution.py:281
  900.2 2.7 dynamic-slice_bitcast_fusion
  903.0 5.8 collective-permute-done.15
  911.0 8.1 gather_last.6
  919.1 1.9 dynamic-slice_bitcast_fusion.3
  921.0 2.0 collective-permute-start.12
  923.0 3.9 collective-permute-done.16
  931.5 6.0 gather_last.7
  937.5 3.5 all-to-all-start.8
  940.9 17.3 %collective-permute-done.12 = f32[4,6,3,16,128]{4,3,2,1,0:T(8,128)} collective-permute-done((f32[4,6,3,16,128]{4,3,2,1,0:T(8,128)}, f32[4,6,3,16,128]{4,3,2,1,0:T(8,128)}, u32[]{:S(2)}, u32[]{:S(2)}) %collective-permute-start.12) | collective-permute-done | bytes 589856 | tf_op jit(solution)/shard_map/ppermute | solution.py:319
  959.6 2.1 bitcast_add_fusion
  962.7 2.3 collective-permute-start.19
  965.4 25.2 %collective-permute-done.13 = f32[2,6,3,16,128]{4,1,3,2,0:T(8,128)S(1)} collective-permute-done((f32[2,6,3,16,128]{4,1,3,2,0:T(8,128)S(1)}, f32[2,6,3,16,128]{4,1,3,2,0:T(8,128)S(1)}, u32[]{:S(2)}, u32[]{:S(2)}) %collective-permute-start.13) | collective-permute-done | bytes 294944 | tf_op jit(solution)/shard_map/ppermute | solution.py:319
  990.8 3.7 collective-permute-start.14
  994.4 2.0 bitcast_add_fusion.1
  997.7 11.8 %collective-permute-done.20 = bf16[1,6,8,16,128]{4,1,3,2,0:T(8,128)(2,1)S(1)} collective-permute-done((bf16[1,6,8,16,128]{4,1,3,2,0:T(8,128)(2,1)S(1)}, bf16[1,6,8,16,128]{4,1,3,2,0:T(8,128)(2,1)S(1)}, u32[]{:S(2)}, u32[]{:S(2)}) %collective-permute-start.20) | collective-permute-done | bytes 196640 | tf_op jit(solution)/shard_map/ppermute | solution.py:319
  (111 shorter events, 35.5 us)
Async XLA Ops:
  0.6 5.2 copy-start.14
  3.4 14.7 %collective-permute-start = (bf16[32,1,128,128]{3,2,1,0:T(8,128)(2,1)S(1)}, bf16[32,1,128,128]{3,2,1,0:T(8,128)(2,1)S(1)}, u32[]{:S(2)}, u32[]{:S(2)}) collective-permute-start(bf16[32,1,128,128]{3,2,1,0:T(8,128)(2,1)S(1)} %get-tuple-element.25), channel_id=1, source_target_pairs={{0,24},{8,0},{16,8},{24,16},{1,25},{9,1},{17,9},{25,17},{2,26},{10... | collective-permute-start | bytes 3145736 | tf_op jit(solution)/shard_map/ppermute | solution.py:344
  18.1 1.0 copy-start.7
  30.1 55.1 %all-to-all-start = ((bf16[8,2,16,32,128]{4,3,2,1,0:T(8,128)(2,1)}), bf16[8,2,16,32,128]{4,3,2,1,0:T(8,128)(2,1)S(1)}, u32[]{:S(2)}, u32[]{:S(2)}) async-start(bf16[8,2,16,32,128]{4,3,2,1,0:T(8,128)(2,1)} %advect_first.4), calls=%async_computation | async-start | bytes 4194304 | tf_op jit(solution)/shard_map/all_to_all | solution.py:302
  85.2 1.3 copy-start.5
  86.5 74.6 %all-to-all-start.4 = ((bf16[8,3,16,32,128]{4,3,2,1,0:T(8,128)(2,1)}), bf16[8,3,16,32,128]{4,3,2,1,0:T(8,128)(2,1)S(1)}, u32[]{:S(2)}, u32[]{:S(2)}) async-start(bf16[8,3,16,32,128]{4,3,2,1,0:T(8,128)(2,1)} %advect_first.7), calls=%async_computation.4 | async-start | bytes 6291456 | tf_op jit(solution)/shard_map/all_to_all | solution.py:302
  90.2 14.6 %collective-permute-start.1 = (bf16[32,1,128,128]{3,2,1,0:T(8,128)(2,1)}, bf16[32,1,128,128]{3,2,1,0:T(8,128)(2,1)}, u32[]{:S(2)}, u32[]{:S(2)}) collective-permute-start(bf16[32,1,128,128]{3,2,1,0:T(8,128)(2,1)} %get-tuple-element.24), channel_id=1, source_target_pairs={{0,8},{8,16},{16,24},{24,0},{1,9},{9,17},{17,25},{25,1},{2,10},{10... | collective-permute-start | bytes 3145736 | tf_op jit(solution)/shard_map/ppermute | solution.py:343
  161.1 1.6 copy-start.1
  162.7 74.6 %all-to-all-start.2 = ((bf16[8,3,16,32,128]{4,3,2,1,0:T(8,128)(2,1)}), bf16[8,3,16,32,128]{4,3,2,1,0:T(8,128)(2,1)}, u32[]{:S(2)}, u32[]{:S(2)}) async-start(bf16[8,3,16,32,128]{4,3,2,1,0:T(8,128)(2,1)} %advect_first.6), calls=%async_computation.2 | async-start | bytes 6291456 | tf_op jit(solution)/shard_map/all_to_all | solution.py:302
  237.4 189.1 %all-to-all-start.1 = ((bf16[8,8,16,32,128]{4,3,2,1,0:T(8,128)(2,1)}), bf16[8,8,16,32,128]{4,3,2,1,0:T(8,128)(2,1)}, u32[]{:S(2)}, u32[]{:S(2)}) async-start(bf16[8,8,16,32,128]{4,3,2,1,0:T(8,128)(2,1)} %advect_first.5), calls=%async_computation.1 | async-start | bytes 16777216 | tf_op jit(solution)/shard_map/all_to_all | solution.py:302
  244.5 10.0 copy-start.4
  250.7 3.1 copy-start.13
  253.8 23.0 %collective-permute-start.5 = (bf16[1,16,256,128]{3,2,1,0:T(8,128)(2,1)}, bf16[1,16,256,128]{3,2,1,0:T(8,128)(2,1)}, u32[]{:S(2)}, u32[]{:S(2)}) collective-permute-start(bf16[1,16,256,128]{3,2,1,0:T(8,128)(2,1)} %get-tuple-element.41), channel_id=1, source_target_pairs={{0,8},{8,16},{16,24},{24,0},{1,9},{9,17},{17,25},{25,1},{2,10},{10... | collective-permute-start | bytes 3145736 | tf_op jit(solution)/shard_map/ppermute | solution.py:385
  262.4 12.9 %copy-start = (bf16[3,16,256,128]{3,2,1,0:T(8,128)(2,1)S(1)}, bf16[3,16,256,128]{3,2,1,0:T(8,128)(2,1)}, u32[]{:S(2)}) copy-start(bf16[3,16,256,128]{3,2,1,0:T(8,128)(2,1)} %turn_first.7.below.centre.above) | copy-start | bytes 9437188
  270.5 115.1 %collective-permute-start.6 = (bf16[3,1,256,128]{3,2,1,0:T(8,128)(2,1)S(1)}, bf16[3,1,256,128]{3,2,1,0:T(8,128)(2,1)}, u32[]{:S(2)}, u32[]{:S(2)}) collective-permute-start(bf16[3,1,256,128]{3,2,1,0:T(8,128)(2,1)S(1)} %get-tuple-element.37), channel_id=1, source_target_pairs={{0,1},{1,2},{2,3},{3,4},{4,5},{5,6},{6,7},{7,0},{8,9},{9,10},{10,1... | collective-permute-start | bytes 589832 | tf_op jit(solution)/shard_map/ppermute | solution.py:383
  272.4 113.2 %collective-permute-start.7 = (bf16[3,1,256,128]{3,2,1,0:T(8,128)(2,1)S(1)}, bf16[3,1,256,128]{3,2,1,0:T(8,128)(2,1)}, u32[]{:S(2)}, u32[]{:S(2)}) collective-permute-start(bf16[3,1,256,128]{3,2,1,0:T(8,128)(2,1)S(1)} %get-tuple-element.36), channel_id=1, source_target_pairs={{0,7},{1,0},{2,1},{3,2},{4,3},{5,4},{6,5},{7,6},{8,15},{9,8},{10,9... | collective-permute-start | bytes 589832 | tf_op jit(solution)/shard_map/ppermute | solution.py:384
  426.5 99.4 %all-to-all-start.5 = ((bf16[8,3,16,32,128]{4,3,2,1,0:T(8,128)(2,1)}), bf16[8,3,16,32,128]{4,3,2,1,0:T(8,128)(2,1)}, u32[]{:S(2)}, u32[]{:S(2)}) async-start(bf16[8,3,16,32,128]{4,3,2,1,0:T(8,128)(2,1)} %advect_turn.5), calls=%async_computation.5 | async-start | bytes 6291456 | tf_op jit(solution)/shard_map/all_to_all | solution.py:302
  449.7 59.1 %collective-permute-start.10 = (bf16[3,1,256,128]{3,2,1,0:T(8,128)(2,1)}, bf16[3,1,256,128]{3,2,1,0:T(8,128)(2,1)S(1)}, u32[]{:S(2)}, u32[]{:S(2)}) collective-permute-start(bf16[3,1,256,128]{3,2,1,0:T(8,128)(2,1)} %get-tuple-element.31), channel_id=1, source_target_pairs={{0,1},{1,2},{2,3},{3,4},{4,5},{5,6},{6,7},{7,0},{8,9},{9,10},{10,1... | collective-permute-start | bytes 589832 | tf_op jit(solution)/shard_map/ppermute | solution.py:383
  451.7 57.1 %collective-permute-start.11 = (bf16[3,1,256,128]{3,2,1,0:T(8,128)(2,1)}, bf16[3,1,256,128]{3,2,1,0:T(8,128)(2,1)S(1)}, u32[]{:S(2)}, u32[]{:S(2)}) collective-permute-start(bf16[3,1,256,128]{3,2,1,0:T(8,128)(2,1)} %get-tuple-element.30), channel_id=1, source_target_pairs={{0,7},{1,0},{2,1},{3,2},{4,3},{5,4},{6,5},{7,6},{8,15},{9,8},{10,9... | collective-permute-start | bytes 589832 | tf_op jit(solution)/shard_map/ppermute | solution.py:384
  508.8 0.7 copy-start.9
  508.8 0.8 copy-start.10
  525.9 121.7 %all-to-all-start.7 = ((bf16[8,3,16,32,128]{4,3,2,1,0:T(8,128)(2,1)}), bf16[8,3,16,32,128]{4,3,2,1,0:T(8,128)(2,1)S(1)}, u32[]{:S(2)}, u32[]{:S(2)}) async-start(bf16[8,3,16,32,128]{4,3,2,1,0:T(8,128)(2,1)} %advect_turn.7), calls=%async_computation.7 | async-start | bytes 6291456 | tf_op jit(solution)/shard_map/all_to_all | solution.py:302
  545.8 65.2 %collective-permute-start.8 = (bf16[8,1,256,128]{3,2,1,0:T(8,128)(2,1)S(1)}, bf16[8,1,256,128]{3,2,1,0:T(8,128)(2,1)}, u32[]{:S(2)}, u32[]{:S(2)}) collective-permute-start(bf16[8,1,256,128]{3,2,1,0:T(8,128)(2,1)S(1)} %get-tuple-element.29), channel_id=1, source_target_pairs={{0,1},{1,2},{2,3},{3,4},{4,5},{5,6},{6,7},{7,0},{8,9},{9,10},{10,1... | collective-permute-start | bytes 1572872 | tf_op jit(solution)/shard_map/ppermute | solution.py:383
  547.9 63.2 %collective-permute-start.9 = (bf16[8,1,256,128]{3,2,1,0:T(8,128)(2,1)S(1)}, bf16[8,1,256,128]{3,2,1,0:T(8,128)(2,1)}, u32[]{:S(2)}, u32[]{:S(2)}) collective-permute-start(bf16[8,1,256,128]{3,2,1,0:T(8,128)(2,1)S(1)} %get-tuple-element.28), channel_id=1, source_target_pairs={{0,7},{1,0},{2,1},{3,2},{4,3},{5,4},{6,5},{7,6},{8,15},{9,8},{10,9... | collective-permute-start | bytes 1572872 | tf_op jit(solution)/shard_map/ppermute | solution.py:384
  647.6 1.7 copy-start.2
  649.3 203.2 %all-to-all-start.6 = ((bf16[8,8,16,32,128]{4,3,2,1,0:T(8,128)(2,1)}), bf16[8,8,16,32,128]{4,3,2,1,0:T(8,128)(2,1)}, u32[]{:S(2)}, u32[]{:S(2)}) async-start(bf16[8,8,16,32,128]{4,3,2,1,0:T(8,128)(2,1)} %advect_turn.6), calls=%async_computation.6 | async-start | bytes 16777216 | tf_op jit(solution)/shard_map/all_to_all | solution.py:302
  666.9 143.1 %collective-permute-start.2 = (bf16[1,16,256,128]{3,2,1,0:T(8,128)(2,1)}, bf16[1,16,256,128]{3,2,1,0:T(8,128)(2,1)S(1)}, u32[]{:S(2)}, u32[]{:S(2)}) collective-permute-start(bf16[1,16,256,128]{3,2,1,0:T(8,128)(2,1)} %get-tuple-element.33), channel_id=1, source_target_pairs={{0,24},{8,0},{16,8},{24,16},{1,25},{9,1},{17,9},{25,17},{2,26},{10... | collective-permute-start | bytes 3145736 | tf_op jit(solution)/shard_map/ppermute | solution.py:386
  669.0 141.0 %collective-permute-start.3 = (bf16[2,1,256,128]{3,2,1,0:T(8,128)(2,1)S(1)}, bf16[2,1,256,128]{3,2,1,0:T(8,128)(2,1)S(1)}, u32[]{:S(2)}, u32[]{:S(2)}) collective-permute-start(bf16[2,1,256,128]{3,2,1,0:T(8,128)(2,1)S(1)} %get-tuple-element.43), channel_id=1, source_target_pairs={{0,1},{1,2},{2,3},{3,4},{4,5},{5,6},{6,7},{7,0},{8,9},{9,10},{10,1... | collective-permute-start | bytes 393224 | tf_op jit(solution)/shard_map/ppermute | solution.py:383
  670.8 139.2 %collective-permute-start.4 = (bf16[2,1,256,128]{3,2,1,0:T(8,128)(2,1)S(1)}, bf16[2,1,256,128]{3,2,1,0:T(8,128)(2,1)S(1)}, u32[]{:S(2)}, u32[]{:S(2)}) collective-permute-start(bf16[2,1,256,128]{3,2,1,0:T(8,128)(2,1)S(1)} %get-tuple-element.42), channel_id=1, source_target_pairs={{0,7},{1,0},{2,1},{3,2},{4,3},{5,4},{6,5},{7,6},{8,15},{9,8},{10,9... | collective-permute-start | bytes 393224 | tf_op jit(solution)/shard_map/ppermute | solution.py:384
  810.0 0.6 copy-start.11
  810.0 0.7 copy-start.12
  810.0 1.0 copy-start.6
  823.3 47.3 %copy-start.21 = (f32[256]{0:T(256)S(1)}, f32[256]{0:T(256)}, u32[]{:S(2)}) copy-start(f32[256]{0:T(256)} %param.10) | copy-start | bytes 3076
  823.3 47.4 %copy-start.15 = (f32[1,256]{1,0:T(1,128)S(1)}, f32[1,256]{1,0:T(1,128)}, u32[]{:S(2)}) copy-start(f32[1,256]{1,0:T(1,128)} %get-tuple-element.55) | copy-start | bytes 3076
  823.4 47.3 %copy-start.16 = (f32[1,256]{1,0:T(1,128)S(1)}, f32[1,256]{1,0:T(1,128)}, u32[]{:S(2)}) copy-start(f32[1,256]{1,0:T(1,128)} %get-tuple-element.56) | copy-start | bytes 3076
  823.4 47.3 %copy-start.17 = (f32[1,256]{1,0:T(1,128)S(1)}, f32[1,256]{1,0:T(1,128)}, u32[]{:S(2)}) copy-start(f32[1,256]{1,0:T(1,128)} %get-tuple-element.58) | copy-start | bytes 3076
  823.4 47.3 %copy-start.18 = (f32[1,256]{1,0:T(1,128)S(1)}, f32[1,256]{1,0:T(1,128)}, u32[]{:S(2)}) copy-start(f32[1,256]{1,0:T(1,128)} %get-tuple-element.59) | copy-start | bytes 3076
  823.4 47.3 %copy-start.19 = (f32[1,256]{1,0:T(1,128)S(1)}, f32[1,256]{1,0:T(1,128)}, u32[]{:S(2)}) copy-start(f32[1,256]{1,0:T(1,128)} %get-tuple-element.60) | copy-start | bytes 3076
  823.4 47.3 %copy-start.20 = (f32[1,256]{1,0:T(1,128)S(1)}, f32[1,256]{1,0:T(1,128)}, u32[]{:S(2)}) copy-start(f32[1,256]{1,0:T(1,128)} %get-tuple-element.62) | copy-start | bytes 3076
  852.4 77.8 %all-to-all-start.3 = ((bf16[8,2,16,32,128]{4,3,2,1,0:T(8,128)(2,1)}), bf16[8,2,16,32,128]{4,3,2,1,0:T(8,128)(2,1)S(1)}, u32[]{:S(2)}, u32[]{:S(2)}) async-start(bf16[8,2,16,32,128]{4,3,2,1,0:T(8,128)(2,1)} %advect_turn.4), calls=%async_computation.3 | async-start | bytes 4194304 | tf_op jit(solution)/shard_map/all_to_all | solution.py:302
  880.6 28.1 %collective-permute-start.15 = (f32[4,6,3,16,128]{4,3,2,1,0:T(8,128)S(1)}, f32[4,6,3,16,128]{4,3,2,1,0:T(8,128)}, u32[]{:S(2)}, u32[]{:S(2)}) collective-permute-start(f32[4,6,3,16,128]{4,3,2,1,0:T(8,128)S(1)} %dynamic-slice_bitcast_fusion.2), channel_id=1, source_target_pairs={{0,1},{1,0},{2,3},{3,2},{4,5},{5,4},{6,7},{7,6},{8,9},{9,8},{10,11... | collective-permute-start | bytes 1769480 | tf_op jit(solution)/shard_map/ppermute | solution.py:319
  902.9 56.6 %collective-permute-start.18 = (f32[4,6,8,16,128]{4,3,2,1,0:T(8,128)}, f32[4,6,8,16,128]{4,3,2,1,0:T(8,128)}, u32[]{:S(2)}, u32[]{:S(2)}) collective-permute-start(f32[4,6,8,16,128]{4,3,2,1,0:T(8,128)} %dynamic-slice_bitcast_fusion), channel_id=1, source_target_pairs={{0,1},{1,0},{2,3},{3,2},{4,5},{5,4},{6,7},{7,6},{8,9},{9,8},{10,11... | collective-permute-start | bytes 4718600 | tf_op jit(solution)/shard_map/ppermute | solution.py:319
  911.0 15.9 %collective-permute-start.16 = (f32[2,6,3,16,128]{4,1,3,2,0:T(8,128)}, f32[2,6,3,16,128]{4,1,3,2,0:T(8,128)S(1)}, u32[]{:S(2)}, u32[]{:S(2)}) collective-permute-start(f32[2,6,3,16,128]{4,1,3,2,0:T(8,128)} %bitcast.42), channel_id=1, source_target_pairs={{0,2},{1,3},{2,0},{3,1},{4,6},{5,7},{6,4},{7,5},{8,10},{9,11},{10,... | collective-permute-start | bytes 884744 | tf_op jit(solution)/shard_map/ppermute | solution.py:319
  921.0 37.2 %collective-permute-start.12 = (f32[4,6,3,16,128]{4,3,2,1,0:T(8,128)}, f32[4,6,3,16,128]{4,3,2,1,0:T(8,128)}, u32[]{:S(2)}, u32[]{:S(2)}) collective-permute-start(f32[4,6,3,16,128]{4,3,2,1,0:T(8,128)} %dynamic-slice_bitcast_fusion.3), channel_id=1, source_target_pairs={{0,1},{1,0},{2,3},{3,2},{4,5},{5,4},{6,7},{7,6},{8,9},{9,8},{10,11... | collective-permute-start | bytes 1769480 | tf_op jit(solution)/shard_map/ppermute | solution.py:319
  926.9 0.8 copy-start.8
  928.8 36.4 %collective-permute-start.17 = (bf16[1,6,3,16,128]{4,1,3,2,0:T(8,128)(2,1)S(1)}, bf16[1,6,3,16,128]{4,1,3,2,0:T(8,128)(2,1)S(1)}, u32[]{:S(2)}, u32[]{:S(2)}) collective-permute-start(bf16[1,6,3,16,128]{4,1,3,2,0:T(8,128)(2,1)S(1)} %dynamic-slice_convert_fusion.1), channel_id=1, source_target_pairs={{0,4},{1,5},{2,6},{3,7},{4,0},{5,1},{6,2},{7,3},{8,12},{9,13},{10,... | collective-permute-start | bytes 221192 | tf_op jit(solution)/shard_map/ppermute | solution.py:319
  930.2 1.3 copy-start.3
  937.5 27.8 %all-to-all-start.8 = ((bf16[8,6,2,16,128]{4,3,2,1,0:T(8,128)(2,1)}), bf16[8,6,2,16,128]{4,3,2,1,0:T(8,128)(2,1)S(1)}, u32[]{:S(2)}, u32[]{:S(2)}) async-start(bf16[8,6,2,16,128]{4,3,2,1,0:T(8,128)(2,1)} %get-tuple-element.17), calls=%async_computation.8 | async-start | bytes 786432 | tf_op jit(solution)/shard_map/all_to_all | solution.py:302
  962.7 31.8 %collective-permute-start.19 = (f32[2,6,8,16,128]{4,3,2,1,0:T(8,128)}, f32[2,6,8,16,128]{4,3,2,1,0:T(8,128)}, u32[]{:S(2)}, u32[]{:S(2)}) collective-permute-start(f32[2,6,8,16,128]{4,3,2,1,0:T(8,128)} %get-tuple-element.45), channel_id=1, source_target_pairs={{0,2},{1,3},{2,0},{3,1},{4,6},{5,7},{6,4},{7,5},{8,10},{9,11},{10,... | collective-permute-start | bytes 2359304 | tf_op jit(solution)/shard_map/ppermute | solution.py:319
  965.1 25.5 %collective-permute-start.13 = (f32[2,6,3,16,128]{4,1,3,2,0:T(8,128)S(1)}, f32[2,6,3,16,128]{4,1,3,2,0:T(8,128)S(1)}, u32[]{:S(2)}, u32[]{:S(2)}) collective-permute-start(f32[2,6,3,16,128]{4,1,3,2,0:T(8,128)S(1)} %bitcast.54), channel_id=1, source_target_pairs={{0,2},{1,3},{2,0},{3,1},{4,6},{5,7},{6,4},{7,5},{8,10},{9,11},{10,... | collective-permute-start | bytes 884744 | tf_op jit(solution)/shard_map/ppermute | solution.py:319
  990.8 6.9 collective-permute-start.14
  996.5 12.9 %collective-permute-start.20 = (bf16[1,6,8,16,128]{4,1,3,2,0:T(8,128)(2,1)S(1)}, bf16[1,6,8,16,128]{4,1,3,2,0:T(8,128)(2,1)S(1)}, u32[]{:S(2)}, u32[]{:S(2)}) collective-permute-start(bf16[1,6,8,16,128]{4,1,3,2,0:T(8,128)(2,1)S(1)} %dynamic-slice_convert_fusion), channel_id=1, source_target_pairs={{0,4},{1,5},{2,6},{3,7},{4,0},{5,1},{6,2},{7,3},{8,12},{9,13},{10,... | collective-permute-start | bytes 589832 | tf_op jit(solution)/shard_map/ppermute | solution.py:319

commit v2 on v1

--- a/solution.py
+++ b/solution.py
@@ -7,7 +7,10 @@
 from jax.experimental.pallas import tpu as pltpu
 from jax.sharding import PartitionSpec as P
 
-SHARES = (3, 3, 8, 2)
+SHARES = (2, 2, 6, 4, 2)
+SENDING = (1, 2, 0, 3, 4)
+RETURNING = (1, 2, 3, 0, 4)
+DISTANCES = (2, 3, 1, 6, 7, 4, 5)
 
 step_length = 0.3
 relax_rate = 0.5
@@ -56,17 +59,33 @@
     return jnp.stack([low[0], high[0], low[1], high[1], low[2], high[2], middle])
 
 
-def advect_kernel(has_low, has_high, *refs):
+def paired(owners):
+    return owners == len(DISTANCES) + 1
+
+
+def block_count(owners):
+    return owners if paired(owners) else 1
+
+
+def owner_rows(place, index, rows):
+    if place is None:
+        return pl.ds(index * rows, rows)
+    return pl.ds(pl.multiple_of(jnp.bitwise_xor(place, index) * rows, rows), rows)
+
+
+def advect_kernel(has_low, has_high, pieces, *refs):
     refs = list(refs)
-    coef, below, centre, above = refs[:4]
-    rest = refs[4:]
+    coef, place, below, centre, above = refs[:5]
+    rest = refs[5:]
     low = rest.pop(0) if has_low else None
     high = rest.pop(0) if has_high else None
-    field, out, staged = rest
+    field = rest[0]
+    outs = rest[1 : 1 + pieces]
+    staged = rest[-1]
     z = pl.program_id(0)
     last = pl.num_programs(0) - 1
     count, width = staged.shape[0], staged.shape[1]
-    owners, rows = out.shape[0], out.shape[2]
+    group, rows = outs[0].shape[0], outs[0].shape[2]
 
     def one(o, carry):
         f = centre[o, 0].astype(F32)
@@ -88,22 +107,26 @@
         return carry
 
     lax.fori_loop(0, count, one, 0)
-    for owner in range(owners):
-        part = staged[:, owner * rows : (owner + 1) * rows, :]
-        out[owner, 0] = jnp.swapaxes(part, 0, 1).astype(BF16)
-
-
-def advect(coef, q, low, high, field, start, depth, owners):
+    base = place[0] if pieces > 1 else None
+    for index in range(pieces * group):
+        part = staged[:, owner_rows(base, index, rows), :]
+        outs[index // group][index % group, 0] = jnp.swapaxes(part, 0, 1).astype(BF16)
+
+
+def advect(coef, place, q, low, high, field, start, depth, owners):
     count, layers, width, lanes = q.shape
     rows = width // owners
+    pieces = block_count(owners)
+    group = owners // pieces
     block = (count, 1, width, lanes)
     in_specs = [
+        pl.BlockSpec(memory_space=pltpu.SMEM),
         pl.BlockSpec(memory_space=pltpu.SMEM),
         pl.BlockSpec(block, lambda z: (0, jnp.maximum(start + z - 1, 0), 0, 0)),
         pl.BlockSpec(block, lambda z: (0, start + z, 0, 0)),
         pl.BlockSpec(block, lambda z: (0, jnp.minimum(start + z + 1, layers - 1), 0, 0)),
     ]
-    operands = [coef, q, q, q]
+    operands = [coef, place, q, q, q]
     for halo in (low, high):
         if halo is not None:
             in_specs.append(pl.BlockSpec(block, lambda z: (0, 0, 0, 0)))
@@ -112,11 +135,12 @@
     operands.append(field)
     cells = count * depth * width * lanes
     return pl.pallas_call(
-        functools.partial(advect_kernel, low is not None, high is not None),
+        functools.partial(advect_kernel, low is not None, high is not None, pieces),
         grid=(depth,),
         in_specs=in_specs,
-        out_specs=pl.BlockSpec((owners, 1, rows, count, lanes), lambda z: (0, z, 0, 0, 0)),
-        out_shape=jax.ShapeDtypeStruct((owners, depth, rows, count, lanes), BF16),
+        out_specs=[pl.BlockSpec((group, 1, rows, count, lanes), lambda z: (0, z, 0, 0, 0))]
+        * pieces,
+        out_shape=[jax.ShapeDtypeStruct((group, depth, rows, count, lanes), BF16)] * pieces,
         scratch_shapes=[pltpu.VMEM((count, width, lanes), F32)],
         cost_estimate=pl.CostEstimate(
             flops=30 * cells, transcendentals=cells, bytes_accessed=8 * cells
@@ -125,16 +149,19 @@
     )(*operands)
 
 
-def turn_kernel(rotation, block, out):
-    owners, rows, count, lanes = block.shape[0], block.shape[2], block.shape[3], block.shape[4]
-    total = owners * count
+def turn_kernel(pieces, rotation, *refs):
+    blocks = refs[:pieces]
+    out, south, north = refs[pieces:]
+    group, rows, count, lanes = (blocks[0].shape[i] for i in (0, 2, 3, 4))
     pair = 2 if rows % 2 == 0 else 1
 
     def one(step, carry):
         columns = []
         for j in range(pair):
             y = step * pair + j
-            columns.append(block[:, 0, y].astype(F32).reshape(total, lanes).astype(BF16))
+            parts = [b[:, 0, y].astype(F32).reshape(group * count, lanes) for b in blocks]
+            column = jnp.concatenate(parts, axis=0) if pieces > 1 else parts[0]
+            columns.append(column.astype(BF16))
         wide = jnp.concatenate(columns, axis=1) if pair > 1 else columns[0]
         turned = jnp.dot(rotation[...], wide, preferred_element_type=F32).astype(BF16)
         for j in range(pair):
@@ -142,35 +169,44 @@
         return carry
 
     lax.fori_loop(0, rows // pair, one, 0)
-
-
-def turn(rotation, block):
-    owners, depth, rows, count, lanes = block.shape
-    total = owners * count
+    south[0, 0] = out[0, rows - 1]
+    north[0, 0] = out[0, 0]
+
+
+def turn(rotation, blocks):
+    pieces = len(blocks)
+    group, depth, rows, count, lanes = blocks[0].shape
+    total = pieces * group * count
     cells = total * depth * rows * lanes
+    edge = pl.BlockSpec((1, 1, total, lanes), lambda z: (z, 0, 0, 0))
+    edge_shape = jax.ShapeDtypeStruct((depth, 1, total, lanes), BF16)
     return pl.pallas_call(
-        turn_kernel,
+        functools.partial(turn_kernel, pieces),
         grid=(depth,),
-        in_specs=[
-            pl.BlockSpec((total, total), lambda z: (0, 0)),
-            pl.BlockSpec((owners, 1, rows, count, lanes), lambda z: (0, z, 0, 0, 0)),
+        in_specs=[pl.BlockSpec((total, total), lambda z: (0, 0))]
+        + [pl.BlockSpec((group, 1, rows, count, lanes), lambda z: (0, z, 0, 0, 0))] * pieces,
+        out_specs=[pl.BlockSpec((1, rows, total, lanes), lambda z: (z, 0, 0, 0)), edge, edge],
+        out_shape=[
+            jax.ShapeDtypeStruct((depth, rows, total, lanes), BF16),
+            edge_shape,
+            edge_shape,
         ],
-        out_specs=pl.BlockSpec((1, rows, total, lanes), lambda z: (z, 0, 0, 0)),
-        out_shape=jax.ShapeDtypeStruct((depth, rows, total, lanes), BF16),
         cost_estimate=pl.CostEstimate(
             flops=2 * total * cells, transcendentals=0, bytes_accessed=4 * cells
         ),
         name="turn_first",
-    )(rotation, block)
+    )(rotation, *blocks)
 
 
 def advect_turn_kernel(
-    rotation, weights, terms, below, centre, above, low, high, south, north, field, out, mixed, powers
+    pieces, rotation, weights, terms, below, centre, above, low, high, south, north, field, *refs
 ):
+    outs = refs[:pieces]
+    mixed, powers = refs[pieces:]
     z = pl.program_id(0)
     last = pl.num_programs(0) - 1
     rows, total, lanes = centre.shape[1:]
-    owners, count = out.shape[0], out.shape[3]
+    group, count = outs[0].shape[0], outs[0].shape[3]
     pair = 2 if rows % 2 == 0 else 1
     piece = 64 if total % 64 == 0 else total
 
@@ -198,25 +234,32 @@
                     moved * jnp.exp(powers[part])
                 ).astype(BF16)
         turned = jnp.dot(rotation[...], mixed[...], preferred_element_type=F32)
+        span = group * count
         for j in range(pair):
             column = turned[:, j * lanes : (j + 1) * lanes]
-            out[:, 0, step * pair + j] = column.reshape(owners, count, lanes).astype(BF16)
+            for p in range(pieces):
+                mine = column[p * span : (p + 1) * span]
+                outs[p][:, 0, step * pair + j] = mine.reshape(group, count, lanes).astype(BF16)
         return carry
 
     lax.fori_loop(0, rows // pair, one, 0)
 
 
-def advect_turn(rotation, weights, terms, state, low, high, south, north, field, owners):
+def advect_turn(
+    rotation, weights, terms, state, low, high, south, north, field, start, owners
+):
     depth, rows, total, lanes = state.shape
     count = total // owners
+    pieces = block_count(owners)
+    group = owners // pieces
     layer = (1, rows, total, lanes)
     edge = (1, 1, total, lanes)
     pair = 2 if rows % 2 == 0 else 1
     cells = total * depth * rows * lanes
-    fixed = lambda z: (0, 0, 0, 0)
+    low_last = low.shape[0] - 1
     here = lambda z: (z, 0, 0, 0)
     return pl.pallas_call(
-        advect_turn_kernel,
+        functools.partial(advect_turn_kernel, pieces),
         grid=(depth,),
         in_specs=[
             pl.BlockSpec((total, total), lambda z: (0, 0)),
@@ -225,14 +268,15 @@
             pl.BlockSpec(layer, lambda z: (jnp.maximum(z - 1, 0), 0, 0, 0)),
             pl.BlockSpec(layer, here),
             pl.BlockSpec(layer, lambda z: (jnp.minimum(z + 1, depth - 1), 0, 0, 0)),
-            pl.BlockSpec(layer, fixed),
-            pl.BlockSpec(layer, fixed),
+            pl.BlockSpec(layer, lambda z: (low_last, 0, 0, 0)),
+            pl.BlockSpec(layer, lambda z: (0, 0, 0, 0)),
             pl.BlockSpec(edge, here),
             pl.BlockSpec(edge, here),
-            pl.BlockSpec((1,) + field.shape[1:], here),
+            pl.BlockSpec((1,) + field.shape[1:], lambda z: (start + z, 0, 0, 0)),
         ],
-        out_specs=pl.BlockSpec((owners, 1, rows, count, lanes), lambda z: (0, z, 0, 0, 0)),
-        out_shape=jax.ShapeDtypeStruct((owners, depth, rows, count, lanes), BF16),
+        out_specs=[pl.BlockSpec((group, 1, rows, count, lanes), lambda z: (0, z, 0, 0, 0))]
+        * pieces,
+        out_shape=[jax.ShapeDtypeStruct((group, depth, rows, count, lanes), BF16)] * pieces,
         scratch_shapes=[
             pltpu.VMEM((total, pair * lanes), BF16),
             pltpu.VMEM((total, lanes), F32),
@@ -244,13 +288,17 @@
     )(rotation, weights, terms, state, state, state, low, high, south, north, field)
 
 
-def gather_kernel(*refs):
-    coef, block, partner = refs[:3]
+def gather_kernel(pieces, by_owner, coef, place, *refs):
+    blocks = refs[:pieces]
+    partner = refs[pieces]
     state, partial = refs[-2:]
-    owners, rows, count = block.shape[0], block.shape[2], block.shape[3]
-    for owner in range(owners):
-        part = pl.ds(owner * rows, rows)
-        mine = jnp.swapaxes(block[owner, 0].astype(F32), 0, 1)
+    group, rows, count = (blocks[0].shape[i] for i in (0, 2, 3))
+    base = place[0] if pieces > 1 else None
+    for index in range(pieces * group):
+        part = owner_rows(base, index, rows)
+        slot = jnp.bitwise_xor(base, index) if by_owner and pieces > 1 else index
+        block = blocks[index // group]
+        mine = jnp.swapaxes(block[index % group, 0].astype(F32), 0, 1)
         state[:, 0, part, :] = mine.astype(BF16)
         sums = [None] * 6
         for o in range(count):
@@ -259,27 +307,29 @@
                 term = coef[c, o] * product
                 sums[c] = term if sums[c] is None else sums[c] + term
         for c in range(6):
-            partial[owner, c, 0] = sums[c].astype(partial.dtype)
-
-
-def gather(coef, block, partner, state, start, kind):
-    owners, depth, rows, count, lanes = block.shape
+            partial[slot, c, 0] = sums[c].astype(partial.dtype)
+
+
+def gather(coef, place, blocks, partner, state, start, closing):
+    pieces = len(blocks)
+    group, depth, rows, count, lanes = blocks[0].shape
+    owners = pieces * group
     width = partner.shape[2]
     cells = owners * depth * rows * count * lanes
     slab = pl.BlockSpec((count, 1, width, lanes), lambda z: (0, start + z, 0, 0))
-    operands = [coef, block, partner]
-    in_specs = [
-        pl.BlockSpec(memory_space=pltpu.SMEM),
-        pl.BlockSpec((owners, 1, rows, count, lanes), lambda z: (0, z, 0, 0, 0)),
-        slab,
-    ]
+    operands = [coef, place, *blocks, partner]
+    in_specs = (
+        [pl.BlockSpec(memory_space=pltpu.SMEM)] * 2
+        + [pl.BlockSpec((group, 1, rows, count, lanes), lambda z: (0, z, 0, 0, 0))] * pieces
+        + [slab]
+    )
     aliases = {}
     if state is not None:
-        aliases = {3: 0}
+        aliases = {len(operands): 0}
         operands.append(state)
         in_specs.append(pl.BlockSpec(memory_space=pl.ANY))
     return pl.pallas_call(
-        gather_kernel,
+        functools.partial(gather_kernel, pieces, closing),
         grid=(depth,),
         in_specs=in_specs,
         out_specs=[
@@ -288,7 +338,9 @@
         ],
         out_shape=[
             jax.ShapeDtypeStruct(partner.shape, BF16),
-            jax.ShapeDtypeStruct((owners, 6, depth, rows, lanes), kind),
+            jax.ShapeDtypeStruct(
+                (owners, 6, depth, rows, lanes), BF16 if closing else F32
+            ),
         ],
         input_output_aliases=aliases,
         cost_estimate=pl.CostEstimate(
@@ -298,27 +350,34 @@
     )(*operands)
 
 
+def swapped(block, distance):
+    owners = lax.axis_size("orient")
+    return lax.ppermute(block, "orient", [(i, i ^ distance) for i in range(owners)])
+
+
 def exchange(block):
     return lax.all_to_all(block, "orient", split_axis=0, concat_axis=0, tiled=True)
 
 
-def halve(block):
-    owners = lax.axis_size("orient")
-    me = lax.axis_index("orient")
-    rest = block.shape[1:]
+def exchange_blocks(blocks):
+    if len(blocks) == 1:
+        return [exchange(blocks[0])]
+    came = list(blocks)
+    for distance in DISTANCES:
+        came[distance] = swapped(blocks[distance], distance)
+    return came
+
+
+def halve(held):
     stride = 1
-    held = block
-    kept = owners
-    while kept > 1:
-        bit = (me // stride) % 2
-        pairs = held.reshape((kept // 2, 2) + rest)
-        mine = lax.dynamic_index_in_dim(pairs, bit, 1, keepdims=False)
-        theirs = lax.dynamic_index_in_dim(pairs, 1 - bit, 1, keepdims=False)
-        if kept == 2:
+    while held.shape[0] > 1:
+        half = held.shape[0] // 2
+        pairs = held.reshape((half, 2) + held.shape[1:])
+        theirs = pairs[:, 1]
+        if half == 1:
             theirs = theirs.astype(BF16)
-        came = lax.ppermute(theirs, "orient", [(i, i ^ stride) for i in range(owners)])
-        held = mine.astype(F32) + came.astype(F32)
-        kept //= 2
+        came = swapped(theirs, stride)
+        held = pairs[:, 0] + came.astype(F32)
         stride *= 2
     return held[0]
 
@@ -335,10 +394,12 @@
     slabs = lax.axis_size("space")
     me = lax.axis_index("orient")
     count, layers, width, lanes = q_init.shape
+    total = rotation.shape[0]
     rows = width // owners
     sizes = chunk_sizes(layers)
     chunks = len(sizes)
     starts = [sum(sizes[:c]) for c in range(chunks)]
+    place = me.astype(jnp.int32).reshape(1)
 
     first = lax.ppermute(q_init[:, layers - 1 :], "space", ring(slabs, 1))
     final = lax.ppermute(q_init[:, :1], "space", ring(slabs, -1))
@@ -363,13 +424,22 @@
     padding = 32 - split_terms.shape[1]
     split_terms = jnp.pad(split_terms, ((0, 0), (0, padding)))
     row_field = jnp.pad(row_field, ((0, 0), (0, 0), (0, padding), (0, 0)))
+    enter = rotation
+    leave = rotation
+    if paired(owners):
+        into = lax.broadcasted_iota(jnp.int32, (total, total), 1)
+        source = ((into // count) ^ me) * count + into % count
+        chosen = (lax.broadcasted_iota(jnp.int32, (total, total), 0) == source).astype(BF16)
+        enter = jnp.dot(rotation, chosen, preferred_element_type=F32).astype(BF16)
+        leave = jnp.dot(chosen.T, rotation, preferred_element_type=F32).astype(BF16)
 
     turned = {}
     souths = {}
     norths = {}
-    for c in ORDER:
+    for c in SENDING:
         sent = advect(
             local_coef,
+            place,
             q_init,
             first if c == 0 else None,
             final if c == chunks - 1 else None,
@@ -378,45 +448,41 @@
             sizes[c],
             owners,
         )
-        got = exchange(sent)
-        turned[c] = turn(rotation, got)
-        souths[c] = lax.ppermute(turned[c][:, rows - 1 :], "orient", ring(owners, 1))
-        norths[c] = lax.ppermute(turned[c][:, :1], "orient", ring(owners, -1))
+        got = exchange_blocks(sent)
+        turned[c], top_rows, end_rows = turn(enter, got)
+        souths[c] = lax.ppermute(top_rows, "orient", ring(owners, 1))
+        norths[c] = lax.ppermute(end_rows, "orient", ring(owners, -1))
     under = lax.ppermute(turned[chunks - 1][-1:], "space", ring(slabs, 1))
     over = lax.ppermute(turned[0][:1], "space", ring(slabs, -1))
 
     state = None
     sums = {}
-    for c in ORDER:
-        low = under if c == 0 else turned[c - 1][-1:]
-        high = over if c == chunks - 1 else turned[c + 1][:1]
+    for c in RETURNING:
         sent = advect_turn(
-            rotation,
+            leave,
             wide_weights,
             split_terms,
             turned[c],
-            low,
-            high,
+            under if c == 0 else turned[c - 1],
+            over if c == chunks - 1 else turned[c + 1],
             souths[c],
             norths[c],
-            row_field[starts[c] : starts[c] + sizes[c]],
+            row_field,
+            starts[c],
             owners,
         )
-        got = exchange(sent)
-        closing = c == ORDER[-1]
+        got = exchange_blocks(sent)
+        closing = c == RETURNING[-1] or not paired(owners)
         state, partial = gather(
-            local_tensor, got, partner, state, starts[c], BF16 if closing else F32
+            local_tensor, place, got, partner, state, starts[c], closing
         )
-        if closing or owners & (owners - 1):
+        if closing:
             sums[c] = jnp.sum(exchange(partial).astype(F32), axis=0)
         else:
             sums[c] = halve(partial)
     tensor = jnp.concatenate([sums[c] for c in range(chunks)], axis=1)
     new_field = (1.0 - relax_rate) * own_field.astype(F32) + relax_rate * coupling * tensor
     return (state, new_field)
-
-
-ORDER = (1, 2, 0, 3)
 
 
 def solution(mesh):
@@ -429,6 +495,9 @@
         P(),
     )
     out_specs = (P("orient", "space", None, None), P(None, "space", "orient", None))
-    return jax.shard_map(
+    mapped = jax.shard_map(
         staged_device, mesh=mesh, in_specs=in_specs, out_specs=out_specs, check_vma=False
     )
+    if not paired(mesh.shape["orient"]):
+        return mapped
+    return mapped

time: 1010 us -> 954 us (0.945)
  waiting for transfers between devices: 592 us -> 386 us
  starting transfers between devices: 134 us -> 283 us
  local copies, waits for them, and re-layouts: 45.2 us -> 23.3 us
  Pallas kernels: 228 us -> 245 us
    ppermute x17 -> x92, starting transfers between devices: 30.8 us -> 268 us  [the longest x82 250 us: swapped(): lax.ppermute(block, 'orient', [(i, i ^ distance) for i in range(owners)])]
    all_to_all x9 -> x1, waiting for transfers between devices: 167 us -> 0.01 us  [exchange(): lax.all_to_all(block, 'orient', split_axis=0, concat_axis=0, tiled=True)]
    all_to_all x9 -> x1, starting transfers between devices: 99.3 us -> 14.6 us  [exchange(): lax.all_to_all(block, 'orient', split_axis=0, concat_axis=0, tiled=True)]
    slice x11 -> x5, local copies, waits for them, and re-layouts: 19.7 us -> 2.18 us  [the longest x1 1.04 us: staged_device(): over = lax.ppermute(turned[0][:1], 'space', ring(slabs, -1))]
    ppermute x1, waiting for transfers between devices: 14.5 us -> 0.01 us  [staged_device(): first = lax.ppermute(q_init[:, layers - 1:], 'space', ring(slabs, 1))]
    ppermute x17 -> x92, waiting for transfers between devices: 400 us -> 386 us  [the longest x82 337 us: swapped(): lax.ppermute(block, 'orient', [(i, i ^ distance) for i in range(owners)])]
    pallas_call x12 -> x15, Pallas kernels: 156 us -> 170 us  [the longest x5 86.8 us: advect_turn(): pl.pallas_call(functools.partial(advect_turn_kernel, pieces), grid=(depth...]
    ppermute x1, waiting for transfers between devices: 10.2 us -> 0.01 us  [staged_device(): final = lax.ppermute(q_init[:, :1], 'space', ring(slabs, -1))]
  transfers between devices with their start and end apart: 30 -> 97, of which waited for: 17 -> 29; matrix products, arithmetic and copies ran while one was open for 4% -> 3% of each run, Pallas kernels for 21% -> 25%
where the time goes in v2:
time: 954 us; the launch traced here: 953 us
  waiting for transfers between devices  386 us (40%)
  starting transfers between devices  283 us (30%)
  Pallas kernels  245 us (26%)
  local copies, waits for them, and re-layouts  23.3 us (2%)
  other arithmetic  12.5 us (1%)
    ppermute x82, waiting for transfers between devices, swapped(): lax.ppermute(block, 'orient', [(i, i ^ distance) for i in range(owners)])  337 us
    ppermute x82, starting transfers between devices, swapped(): lax.ppermute(block, 'orient', [(i, i ^ distance) for i in range(owners)])  250 us
    pallas_call x5, Pallas kernels, advect_turn(): pl.pallas_call(functools.partial(advect_turn_kernel, pieces), grid=(depth...  86.8 us
    pallas_call x5, Pallas kernels, advect(): pl.pallas_call(functools.partial(advect_kernel, low is not None, high is...  75 us
    pallas_call x5, Pallas kernels, gather(): pl.pallas_call(functools.partial(gather_kernel, pieces, closing), grid=(d...  44.6 us
    pallas_call x5, Pallas kernels, turn(): pl.pallas_call(functools.partial(turn_kernel, pieces), grid=(depth,), in_...  38 us
    ppermute x5, waiting for transfers between devices, staged_device(): souths[c] = lax.ppermute(top_rows, 'orient', ring(owners, 1))  30.8 us
  transfers between devices with their start and end apart: 97, of which 29 were waited for; matrix products, arithmetic and copies ran while one was open for 3% of the time, Pallas kernels for 25%

profile of v2, /device:TPU:0, one launch (start us, length us, event | category | flops | bytes accessed | tf_op | source)
XLA Modules:
  0.0 953.2 jit_solution(1921374819850190194)
XLA Ops:
  3.7 10.1 %advect_first.8 = (bf16[1,2,16,32,128]{4,3,2,1,0:T(8,128)(2,1)}, bf16[1,2,16,32,128]{4,3,2,1,0:T(8,128)(2,1)}, bf16[1,2,16,32,128]{4,3,2,1,0:T(8,128)(2,1)}, bf1...) custom-call(f32[13,32]{1,0:T(8,128)} %constant_dynamic-slice_fusion., ...), custom_call_target="tpu_custom_call" | custom-call | flops 31457280 | bytes 8388608 | tf_op jit(solution)/shard_map/advect_first/pallas_call | solution.py:137
  27.3 17.6 %advect_first.6 = (bf16[1,4,16,32,128]{4,3,2,1,0:T(8,128)(2,1)}, bf16[1,4,16,32,128]{4,3,2,1,0:T(8,128)(2,1)}, bf16[1,4,16,32,128]{4,3,2,1,0:T(8,128)(2,1)}, bf1...) custom-call(f32[13,32]{1,0:T(8,128)} %constant_dynamic-slice_fusion., ...), custom_call_target="tpu_custom_call" | custom-call | flops 62914560 | bytes 16777216 | tf_op jit(solution)/shard_map/advect_first/pallas_call | solution.py:137
  46.7 11.6 %collective-permute-done.38.refs_5_ = bf16[1,2,16,32,128]{4,3,2,1,0:T(8,128)(2,1)S(1)} collective-permute-done((bf16[1,2,16,32,128]{4,3,2,1,0:T(8,128)(2,1)}, bf16[1,2,16,32,128]{4,3,2,1,0:T(8,128)(2,1)S(1)}, u32[]{:S(2)}, u32[]{:S(2)}) %collective-permute-start.38) | collective-permute-done | bytes 262176 | tf_op jit(solution)/shard_map/ppermute | solution.py:355
  59.2 6.5 collective-permute-start.11
  67.3 5.7 turn_first.8
  74.5 19.5 %collective-permute-done.75.south = bf16[2,1,256,128]{3,2,1,0:T(8,128)(2,1)S(1)} collective-permute-done((bf16[2,1,256,128]{3,2,1,0:T(8,128)(2,1)}, bf16[2,1,256,128]{3,2,1,0:T(8,128)(2,1)S(1)}, u32[]{:S(2)}, u32[]{:S(2)}) %collective-permute-start.75) | collective-permute-done | bytes 131104 | tf_op jit(solution)/shard_map/ppermute | solution.py:453
  96.5 4.2 collective-permute-start.14
  104.0 25.2 %advect_first.9 = (bf16[1,6,16,32,128]{4,3,2,1,0:T(8,128)(2,1)}, bf16[1,6,16,32,128]{4,3,2,1,0:T(8,128)(2,1)}, bf16[1,6,16,32,128]{4,3,2,1,0:T(8,128)(2,1)}, bf1...) custom-call(f32[13,32]{1,0:T(8,128)} %constant_dynamic-slice_fusion., ...), custom_call_target="tpu_custom_call" | custom-call | flops 94371840 | bytes 25165824 | tf_op jit(solution)/shard_map/advect_first/pallas_call | solution.py:137
  129.3 12.3 %collective-permute-done.12.refs_5_ = bf16[1,4,16,32,128]{4,3,2,1,0:T(8,128)(2,1)} collective-permute-done((bf16[1,4,16,32,128]{4,3,2,1,0:T(8,128)(2,1)}, bf16[1,4,16,32,128]{4,3,2,1,0:T(8,128)(2,1)}, u32[]{:S(2)}, u32[]{:S(2)}) %collective-permute-start.12) | collective-permute-done | bytes 524320 | tf_op jit(solution)/shard_map/ppermute | solution.py:355
  141.6 11.8 %collective-permute-start.52 = (bf16[1,6,16,32,128]{4,3,2,1,0:T(8,128)(2,1)}, bf16[1,6,16,32,128]{4,3,2,1,0:T(8,128)(2,1)}, u32[]{:S(2)}, u32[]{:S(2)}) collective-permute-start(bf16[1,6,16,32,128]{4,3,2,1,0:T(8,128)(2,1)} %get-tuple-element.166), channel_id=1, source_target_pairs={{0,3},{1,2},{2,1},{3,0},{4,7},{5,6},{6,5},{7,4},{8,11},{9,10},{10,... | collective-permute-start | bytes 2359304 | tf_op jit(solution)/shard_map/ppermute | solution.py:355
  156.1 8.9 turn_first.6
  165.0 17.8 %collective-permute-done.76.north = bf16[2,1,256,128]{3,2,1,0:T(8,128)(2,1)S(1)} collective-permute-done((bf16[2,1,256,128]{3,2,1,0:T(8,128)(2,1)S(1)}, bf16[2,1,256,128]{3,2,1,0:T(8,128)(2,1)S(1)}, u32[]{:S(2)}, u32[]{:S(2)}) %collective-permute-start.76) | collective-permute-done | bytes 131104 | tf_op jit(solution)/shard_map/ppermute | solution.py:454
  183.5 11.2 %collective-permute-done.57.south = bf16[4,1,256,128]{3,2,1,0:T(8,128)(2,1)S(1)} collective-permute-done((bf16[4,1,256,128]{3,2,1,0:T(8,128)(2,1)}, bf16[4,1,256,128]{3,2,1,0:T(8,128)(2,1)S(1)}, u32[]{:S(2)}, u32[]{:S(2)}) %collective-permute-start.57) | collective-permute-done | bytes 262176 | tf_op jit(solution)/shard_map/ppermute | solution.py:453
  202.4 11.0 %advect_first.7 = (bf16[1,2,16,32,128]{4,3,2,1,0:T(8,128)(2,1)}, bf16[1,2,16,32,128]{4,3,2,1,0:T(8,128)(2,1)}, bf16[1,2,16,32,128]{4,3,2,1,0:T(8,128)(2,1)}, bf1...) custom-call(f32[13,32]{1,0:T(8,128)} %constant_dynamic-slice_fusion., ...), custom_call_target="tpu_custom_call" | custom-call | flops 31457280 | bytes 8388608 | tf_op jit(solution)/shard_map/advect_first/pallas_call | solution.py:137
  213.5 68.7 %collective-permute-done.53.refs_4_ = bf16[1,6,16,32,128]{4,3,2,1,0:T(8,128)(2,1)} collective-permute-done((bf16[1,6,16,32,128]{4,3,2,1,0:T(8,128)(2,1)}, bf16[1,6,16,32,128]{4,3,2,1,0:T(8,128)(2,1)}, u32[]{:S(2)}, u32[]{:S(2)}) %collective-permute-start.53) | collective-permute-done | bytes 786464 | tf_op jit(solution)/shard_map/ppermute | solution.py:355
  282.1 15.7 %collective-permute-done.54.refs_5_ = bf16[1,6,16,32,128]{4,3,2,1,0:T(8,128)(2,1)} collective-permute-done((bf16[1,6,16,32,128]{4,3,2,1,0:T(8,128)(2,1)}, bf16[1,6,16,32,128]{4,3,2,1,0:T(8,128)(2,1)}, u32[]{:S(2)}, u32[]{:S(2)}) %collective-permute-start.54) | collective-permute-done | bytes 786464 | tf_op jit(solution)/shard_map/ppermute | solution.py:355
  297.8 17.4 %collective-permute-start.18 = (bf16[1,2,16,32,128]{4,3,2,1,0:T(8,128)(2,1)}, bf16[1,2,16,32,128]{4,3,2,1,0:T(8,128)(2,1)S(1)}, u32[]{:S(2)}, u32[]{:S(2)}) collective-permute-start(bf16[1,2,16,32,128]{4,3,2,1,0:T(8,128)(2,1)} %get-tuple-element.128), channel_id=1, source_target_pairs={{0,3},{1,2},{2,1},{3,0},{4,7},{5,6},{6,5},{7,4},{8,11},{9,10},{10,... | collective-permute-start | bytes 786440 | tf_op jit(solution)/shard_map/ppermute | solution.py:355
  315.3 23.8 %collective-permute-start.19 = (bf16[1,2,16,32,128]{4,3,2,1,0:T(8,128)(2,1)}, bf16[1,2,16,32,128]{4,3,2,1,0:T(8,128)(2,1)S(1)}, u32[]{:S(2)}, u32[]{:S(2)}) collective-permute-start(bf16[1,2,16,32,128]{4,3,2,1,0:T(8,128)(2,1)} %get-tuple-element.129), channel_id=1, source_target_pairs={{0,4},{1,5},{2,6},{3,7},{4,0},{5,1},{6,2},{7,3},{8,12},{9,13},{10,... | collective-permute-start | bytes 786440 | tf_op jit(solution)/shard_map/ppermute | solution.py:355
  343.5 11.1 %advect_first.5 = (bf16[1,2,16,32,128]{4,3,2,1,0:T(8,128)(2,1)}, bf16[1,2,16,32,128]{4,3,2,1,0:T(8,128)(2,1)}, bf16[1,2,16,32,128]{4,3,2,1,0:T(8,128)(2,1)}, bf1...) custom-call(f32[13,32]{1,0:T(8,128)} %constant_dynamic-slice_fusion., ...), custom_call_target="tpu_custom_call" | custom-call | flops 31457280 | bytes 8388608 | tf_op jit(solution)/shard_map/advect_first/pallas_call | solution.py:137
  357.2 10.4 %collective-permute-done.19.refs_4_ = bf16[1,2,16,32,128]{4,3,2,1,0:T(8,128)(2,1)S(1)} collective-permute-done((bf16[1,2,16,32,128]{4,3,2,1,0:T(8,128)(2,1)}, bf16[1,2,16,32,128]{4,3,2,1,0:T(8,128)(2,1)S(1)}, u32[]{:S(2)}, u32[]{:S(2)}) %collective-permute-start.19) | collective-permute-done | bytes 262176 | tf_op jit(solution)/shard_map/ppermute | solution.py:355
  367.6 7.3 collective-permute-done.20.refs_5_
  374.9 4.8 collective-permute-start.4
  382.6 11.0 %collective-permute-start.5 = (bf16[1,2,16,32,128]{4,3,2,1,0:T(8,128)(2,1)}, bf16[1,2,16,32,128]{4,3,2,1,0:T(8,128)(2,1)S(1)}, u32[]{:S(2)}, u32[]{:S(2)}) collective-permute-start(bf16[1,2,16,32,128]{4,3,2,1,0:T(8,128)(2,1)} %get-tuple-element.112), channel_id=1, source_target_pairs={{0,5},{1,4},{2,7},{3,6},{4,1},{5,0},{6,3},{7,2},{8,13},{9,12},{10,... | collective-permute-start | bytes 786440 | tf_op jit(solution)/shard_map/ppermute | solution.py:355
  393.6 12.1 %turn_first.9 = (bf16[6,16,256,128]{3,2,1,0:T(8,128)(2,1)}, bf16[6,1,256,128]{3,2,1,0:T(8,128)(2,1)}, bf16[6,1,256,128]{3,2,1,0:T(8,128)(2,1)}) custom-call(bf16[256,256]{1,0:T(8,128)(2,1)} %fusion.6.rotation, bf16[1,6,16,32,128]{4,3,2,1,0:T(8,128)(2,1)} %get-tuple-element.163.refs_0_, bf16[1,6,16,32,128]{4,3,2,1,0:T(8,128)(2,1)} %collective-permute-done.50.refs_1_, ...), custom_call_target="tpu_custom_call" | custom-call | flops 1610612736 | bytes 12582912 | tf_op jit(solution)/shard_map/turn_first/pallas_call | solution.py:183
  416.6 11.7 %collective-permute-done.5.refs_5_ = bf16[1,2,16,32,128]{4,3,2,1,0:T(8,128)(2,1)S(1)} collective-permute-done((bf16[1,2,16,32,128]{4,3,2,1,0:T(8,128)(2,1)}, bf16[1,2,16,32,128]{4,3,2,1,0:T(8,128)(2,1)S(1)}, u32[]{:S(2)}, u32[]{:S(2)}) %collective-permute-start.5) | collective-permute-done | bytes 262176 | tf_op jit(solution)/shard_map/ppermute | solution.py:355
  429.1 5.7 turn_first.7
  436.0 12.4 %advect_turn.9 = (bf16[1,2,16,32,128]{4,3,2,1,0:T(8,128)(2,1)}, bf16[1,2,16,32,128]{4,3,2,1,0:T(8,128)(2,1)}, bf16[1,2,16,32,128]{4,3,2,1,0:T(8,128)(2,1)}, bf16...) custom-call(bf16[256,256]{1,0:T(8,128)(2,1)} %convolution_convert_fu, ...), custom_call_target="tpu_custom_call" | custom-call | flops 536870912 | bytes 8388608 | tf_op jit(solution)/shard_map/advect_turn/pallas_call | solution.py:261
  451.3 5.6 turn_first.5
  457.0 4.3 collective-permute-start.42
  461.4 20.7 %advect_turn.7 = (bf16[1,4,16,32,128]{4,3,2,1,0:T(8,128)(2,1)}, bf16[1,4,16,32,128]{4,3,2,1,0:T(8,128)(2,1)}, bf16[1,4,16,32,128]{4,3,2,1,0:T(8,128)(2,1)}, bf16...) custom-call(bf16[256,256]{1,0:T(8,128)(2,1)} %convolution_convert_fu, ...), custom_call_target="tpu_custom_call" | custom-call | flops 1073741824 | bytes 16777216 | tf_op jit(solution)/shard_map/advect_turn/pallas_call | solution.py:261
  488.6 4.6 collective-permute-start.83
  493.2 16.2 %collective-permute-done.80.refs_4_ = bf16[1,2,16,32,128]{4,3,2,1,0:T(8,128)(2,1)S(1)} collective-permute-done((bf16[1,2,16,32,128]{4,3,2,1,0:T(8,128)(2,1)S(1)}, bf16[1,2,16,32,128]{4,3,2,1,0:T(8,128)(2,1)S(1)}, u32[]{:S(2)}, u32[]{:S(2)}) %collective-permute-start.80) | collective-permute-done | bytes 262176 | tf_op jit(solution)/shard_map/ppermute | solution.py:355
  509.4 6.3 collective-permute-done.81.refs_5_
  515.7 6.5 collective-permute-start.62
  522.2 9.9 %collective-permute-start.63 = (bf16[1,4,16,32,128]{4,3,2,1,0:T(8,128)(2,1)}, bf16[1,4,16,32,128]{4,3,2,1,0:T(8,128)(2,1)}, u32[]{:S(2)}, u32[]{:S(2)}) collective-permute-start(bf16[1,4,16,32,128]{4,3,2,1,0:T(8,128)(2,1)} %get-tuple-element.179), channel_id=1, source_target_pairs={{0,5},{1,4},{2,7},{3,6},{4,1},{5,0},{6,3},{7,2},{8,13},{9,12},{10,... | collective-permute-start | bytes 1572872 | tf_op jit(solution)/shard_map/ppermute | solution.py:355
  533.3 28.9 %advect_turn.8 = (bf16[1,6,16,32,128]{4,3,2,1,0:T(8,128)(2,1)}, bf16[1,6,16,32,128]{4,3,2,1,0:T(8,128)(2,1)}, bf16[1,6,16,32,128]{4,3,2,1,0:T(8,128)(2,1)}, bf16...) custom-call(bf16[256,256]{1,0:T(8,128)(2,1)} %convolution_convert_fu, ...), custom_call_target="tpu_custom_call" | custom-call | flops 1610612736 | bytes 25165824 | tf_op jit(solution)/shard_map/advect_turn/pallas_call | solution.py:261
  565.5 7.3 collective-permute-done.62.refs_4_
  576.7 19.4 %collective-permute-done.63.refs_5_ = bf16[1,4,16,32,128]{4,3,2,1,0:T(8,128)(2,1)} collective-permute-done((bf16[1,4,16,32,128]{4,3,2,1,0:T(8,128)(2,1)}, bf16[1,4,16,32,128]{4,3,2,1,0:T(8,128)(2,1)}, u32[]{:S(2)}, u32[]{:S(2)}) %collective-permute-start.63) | collective-permute-done | bytes 524320 | tf_op jit(solution)/shard_map/ppermute | solution.py:355
  596.3 11.6 %collective-permute-start.70 = (bf16[1,6,16,32,128]{4,3,2,1,0:T(8,128)(2,1)}, bf16[1,6,16,32,128]{4,3,2,1,0:T(8,128)(2,1)}, u32[]{:S(2)}, u32[]{:S(2)}) collective-permute-start(bf16[1,6,16,32,128]{4,3,2,1,0:T(8,128)(2,1)} %get-tuple-element.187), channel_id=1, source_target_pairs={{0,3},{1,2},{2,1},{3,0},{4,7},{5,6},{6,5},{7,4},{8,11},{9,10},{10,... | collective-permute-start | bytes 2359304 | tf_op jit(solution)/shard_map/ppermute | solution.py:355
  608.6 6.7 gather_last.5
  617.1 9.9 %collective-permute-start.71 = (bf16[1,6,16,32,128]{4,3,2,1,0:T(8,128)(2,1)}, bf16[1,6,16,32,128]{4,3,2,1,0:T(8,128)(2,1)}, u32[]{:S(2)}, u32[]{:S(2)}) collective-permute-start(bf16[1,6,16,32,128]{4,3,2,1,0:T(8,128)(2,1)} %get-tuple-element.188), channel_id=1, source_target_pairs={{0,4},{1,5},{2,6},{3,7},{4,0},{5,1},{6,2},{7,3},{8,12},{9,13},{10,... | collective-permute-start | bytes 2359304 | tf_op jit(solution)/shard_map/ppermute | solution.py:355
  628.0 11.5 %collective-permute-done.70.refs_3_ = bf16[1,6,16,32,128]{4,3,2,1,0:T(8,128)(2,1)} collective-permute-done((bf16[1,6,16,32,128]{4,3,2,1,0:T(8,128)(2,1)}, bf16[1,6,16,32,128]{4,3,2,1,0:T(8,128)(2,1)}, u32[]{:S(2)}, u32[]{:S(2)}) %collective-permute-start.70) | collective-permute-done | bytes 786464 | tf_op jit(solution)/shard_map/ppermute | solution.py:355
  639.5 4.3 collective-permute-start.72
  646.9 12.4 %advect_turn.6 = (bf16[1,2,16,32,128]{4,3,2,1,0:T(8,128)(2,1)}, bf16[1,2,16,32,128]{4,3,2,1,0:T(8,128)(2,1)}, bf16[1,2,16,32,128]{4,3,2,1,0:T(8,128)(2,1)}, bf16...) custom-call(bf16[256,256]{1,0:T(8,128)(2,1)} %convolution_convert_fu, ...), custom_call_target="tpu_custom_call" | custom-call | flops 536870912 | bytes 8388608 | tf_op jit(solution)/shard_map/advect_turn/pallas_call | solution.py:261
  659.3 53.8 %collective-permute-done.71.refs_4_ = bf16[1,6,16,32,128]{4,3,2,1,0:T(8,128)(2,1)} collective-permute-done((bf16[1,6,16,32,128]{4,3,2,1,0:T(8,128)(2,1)}, bf16[1,6,16,32,128]{4,3,2,1,0:T(8,128)(2,1)}, u32[]{:S(2)}, u32[]{:S(2)}) %collective-permute-start.71) | collective-permute-done | bytes 786464 | tf_op jit(solution)/shard_map/ppermute | solution.py:355
  713.3 16.1 %collective-permute-done.72.refs_5_ = bf16[1,6,16,32,128]{4,3,2,1,0:T(8,128)(2,1)} collective-permute-done((bf16[1,6,16,32,128]{4,3,2,1,0:T(8,128)(2,1)}, bf16[1,6,16,32,128]{4,3,2,1,0:T(8,128)(2,1)}, u32[]{:S(2)}, u32[]{:S(2)}) %collective-permute-start.72) | collective-permute-done | bytes 786464 | tf_op jit(solution)/shard_map/ppermute | solution.py:355
  734.2 14.7 %gather_last.6 = (bf16[32,16,128,128]{3,2,1,0:T(8,128)(2,1)}, f32[8,6,6,16,128]{4,3,2,1,0:T(8,128)}) custom-call(f32[6,32]{1,0:T(8,128)} %dynamic-slice_multiply_fusion.coef, s32[1]{0:T(128)} %bitcast.refs_1_.place, bf16[1,6,16,32,128]{4,3,2,1,0:T(8,128)(2,1)} %get-tuple-element.184.refs_0_, ...), custom_call_target="tpu_custom_call", output_to_operand_aliasing={{0}: (11, {})} | custom-call | flops 44040192 | bytes 18874368 | tf_op jit(solution)/shard_map/gather_last/pallas_call | solution.py:331
  748.9 10.6 %gather_last.7 = (bf16[32,16,128,128]{3,2,1,0:T(8,128)(2,1)}, f32[8,6,4,16,128]{4,3,2,1,0:T(8,128)}) custom-call(f32[6,32]{1,0:T(8,128)} %dynamic-slice_multiply_fusion.coef, s32[1]{0:T(128)} %bitcast.refs_1_.place, bf16[1,4,16,32,128]{4,3,2,1,0:T(8,128)(2,1)} %get-tuple-element.174.refs_0_, ...), custom_call_target="tpu_custom_call", output_to_operand_aliasing={{0}: (11, {})} | custom-call | flops 29360128 | bytes 12582912 | tf_op jit(solution)/shard_map/gather_last/pallas_call | solution.py:331
  759.5 33.2 %collective-permute-start.44 = (bf16[1,2,16,32,128]{4,3,2,1,0:T(8,128)(2,1)}, bf16[1,2,16,32,128]{4,3,2,1,0:T(8,128)(2,1)}, u32[]{:S(2)}, u32[]{:S(2)}) collective-permute-start(bf16[1,2,16,32,128]{4,3,2,1,0:T(8,128)(2,1)} %get-tuple-element.157), channel_id=1, source_target_pairs={{0,2},{1,3},{2,0},{3,1},{4,6},{5,7},{6,4},{7,5},{8,10},{9,11},{10,... | collective-permute-start | bytes 786440 | tf_op jit(solution)/shard_map/ppermute | solution.py:355
  801.1 12.5 %advect_turn.5 = (bf16[1,2,16,32,128]{4,3,2,1,0:T(8,128)(2,1)}, bf16[1,2,16,32,128]{4,3,2,1,0:T(8,128)(2,1)}, bf16[1,2,16,32,128]{4,3,2,1,0:T(8,128)(2,1)}, bf16...) custom-call(bf16[256,256]{1,0:T(8,128)(2,1)} %convolution_convert_fu, ...), custom_call_target="tpu_custom_call" | custom-call | flops 536870912 | bytes 8388608 | tf_op jit(solution)/shard_map/advect_turn/pallas_call | solution.py:261
  817.1 10.0 %collective-permute-done.46.refs_4_ = bf16[1,2,16,32,128]{4,3,2,1,0:T(8,128)(2,1)} collective-permute-done((bf16[1,2,16,32,128]{4,3,2,1,0:T(8,128)(2,1)}, bf16[1,2,16,32,128]{4,3,2,1,0:T(8,128)(2,1)}, u32[]{:S(2)}, u32[]{:S(2)}) %collective-permute-start.46) | collective-permute-done | bytes 262176 | tf_op jit(solution)/shard_map/ppermute | solution.py:355
  827.7 5.0 collective-permute-done.47.refs_5_
  832.7 6.2 collective-permute-start.28
  840.0 4.1 collective-permute-start.29
  844.1 6.5 collective-permute-done.26.refs_1_
  858.5 6.5 gather_last.8
  865.1 5.6 collective-permute-done.29.refs_4_
  872.2 5.0 collective-permute-done.30.refs_5_
  877.2 6.2 gather_last.9
  883.4 14.6 %all-to-all-start = ((bf16[8,6,2,16,128]{4,3,2,1,0:T(8,128)(2,1)}), bf16[8,6,2,16,128]{4,3,2,1,0:T(8,128)(2,1)}, u32[]{:S(2)}, u32[]{:S(2)}) async-start(bf16[8,6,2,16,128]{4,3,2,1,0:T(8,128)(2,1)} %get-tuple-element.211), calls=%async_computation | async-start | bytes 786432 | tf_op jit(solution)/shard_map/all_to_all | solution.py:359
  904.5 8.0 collective-permute-done.84
  927.5 8.0 collective-permute-done.86
  935.5 4.5 collective-permute-done.91
  942.8 8.0 collective-permute-done.92
  (382 shorter events, 141.1 us)
Async XLA Ops:
  21.5 36.8 %collective-permute-start.38 = (bf16[1,2,16,32,128]{4,3,2,1,0:T(8,128)(2,1)}, bf16[1,2,16,32,128]{4,3,2,1,0:T(8,128)(2,1)S(1)}, u32[]{:S(2)}, u32[]{:S(2)}) collective-permute-start(bf16[1,2,16,32,128]{4,3,2,1,0:T(8,128)(2,1)} %get-tuple-element.149), channel_id=1, source_target_pairs={{0,5},{1,4},{2,7},{3,6},{4,1},{5,0},{6,3},{7,2},{8,13},{9,12},{10,... | collective-permute-start | bytes 786440 | tf_op jit(solution)/shard_map/ppermute | solution.py:355
  23.4 35.7 %collective-permute-start.39 = (bf16[1,2,16,32,128]{4,3,2,1,0:T(8,128)(2,1)}, bf16[1,2,16,32,128]{4,3,2,1,0:T(8,128)(2,1)S(1)}, u32[]{:S(2)}, u32[]{:S(2)}) collective-permute-start(bf16[1,2,16,32,128]{4,3,2,1,0:T(8,128)(2,1)} %get-tuple-element.150), channel_id=1, source_target_pairs={{0,6},{1,7},{2,4},{3,5},{4,2},{5,3},{6,0},{7,1},{8,14},{9,15},{10,... | collective-permute-start | bytes 786440 | tf_op jit(solution)/shard_map/ppermute | solution.py:355
  46.2 48.4 %collective-permute-start.8 = (bf16[1,4,16,32,128]{4,3,2,1,0:T(8,128)(2,1)}, bf16[1,4,16,32,128]{4,3,2,1,0:T(8,128)(2,1)S(1)}, u32[]{:S(2)}, u32[]{:S(2)}) collective-permute-start(bf16[1,4,16,32,128]{4,3,2,1,0:T(8,128)(2,1)} %get-tuple-element.117), channel_id=1, source_target_pairs={{0,1},{1,0},{2,3},{3,2},{4,5},{5,4},{6,7},{7,6},{8,9},{9,8},{10,11... | collective-permute-start | bytes 1572872 | tf_op jit(solution)/shard_map/ppermute | solution.py:355
  46.6 49.9 %collective-permute-start.9 = (bf16[1,4,16,32,128]{4,3,2,1,0:T(8,128)(2,1)}, bf16[1,4,16,32,128]{4,3,2,1,0:T(8,128)(2,1)S(1)}, u32[]{:S(2)}, u32[]{:S(2)}) collective-permute-start(bf16[1,4,16,32,128]{4,3,2,1,0:T(8,128)(2,1)} %get-tuple-element.118), channel_id=1, source_target_pairs={{0,2},{1,3},{2,0},{3,1},{4,6},{5,7},{6,4},{7,5},{8,10},{9,11},{10,... | collective-permute-start | bytes 1572872 | tf_op jit(solution)/shard_map/ppermute | solution.py:355
  58.3 45.5 %collective-permute-start.10 = (bf16[1,4,16,32,128]{4,3,2,1,0:T(8,128)(2,1)}, bf16[1,4,16,32,128]{4,3,2,1,0:T(8,128)(2,1)S(1)}, u32[]{:S(2)}, u32[]{:S(2)}) collective-permute-start(bf16[1,4,16,32,128]{4,3,2,1,0:T(8,128)(2,1)} %get-tuple-element.119), channel_id=1, source_target_pairs={{0,3},{1,2},{2,1},{3,0},{4,7},{5,6},{6,5},{7,4},{8,11},{9,10},{10,... | collective-permute-start | bytes 1572872 | tf_op jit(solution)/shard_map/ppermute | solution.py:355
  59.2 70.0 %collective-permute-start.11 = (bf16[1,4,16,32,128]{4,3,2,1,0:T(8,128)(2,1)}, bf16[1,4,16,32,128]{4,3,2,1,0:T(8,128)(2,1)}, u32[]{:S(2)}, u32[]{:S(2)}) collective-permute-start(bf16[1,4,16,32,128]{4,3,2,1,0:T(8,128)(2,1)} %get-tuple-element.120), channel_id=1, source_target_pairs={{0,4},{1,5},{2,6},{3,7},{4,0},{5,1},{6,2},{7,3},{8,12},{9,13},{10,... | collective-permute-start | bytes 1572872 | tf_op jit(solution)/shard_map/ppermute | solution.py:355
  94.1 47.5 %collective-permute-start.12 = (bf16[1,4,16,32,128]{4,3,2,1,0:T(8,128)(2,1)}, bf16[1,4,16,32,128]{4,3,2,1,0:T(8,128)(2,1)}, u32[]{:S(2)}, u32[]{:S(2)}) collective-permute-start(bf16[1,4,16,32,128]{4,3,2,1,0:T(8,128)(2,1)} %get-tuple-element.121), channel_id=1, source_target_pairs={{0,5},{1,4},{2,7},{3,6},{4,1},{5,0},{6,3},{7,2},{8,13},{9,12},{10,... | collective-permute-start | bytes 1572872 | tf_op jit(solution)/shard_map/ppermute | solution.py:355
  94.6 47.0 %collective-permute-start.13 = (bf16[1,4,16,32,128]{4,3,2,1,0:T(8,128)(2,1)}, bf16[1,4,16,32,128]{4,3,2,1,0:T(8,128)(2,1)}, u32[]{:S(2)}, u32[]{:S(2)}) collective-permute-start(bf16[1,4,16,32,128]{4,3,2,1,0:T(8,128)(2,1)} %get-tuple-element.122), channel_id=1, source_target_pairs={{0,6},{1,7},{2,4},{3,5},{4,2},{5,3},{6,0},{7,1},{8,14},{9,15},{10,... | collective-permute-start | bytes 1572872 | tf_op jit(solution)/shard_map/ppermute | solution.py:355
  96.5 56.8 %collective-permute-start.14 = (bf16[1,4,16,32,128]{4,3,2,1,0:T(8,128)(2,1)}, bf16[1,4,16,32,128]{4,3,2,1,0:T(8,128)(2,1)}, u32[]{:S(2)}, u32[]{:S(2)}) collective-permute-start(bf16[1,4,16,32,128]{4,3,2,1,0:T(8,128)(2,1)} %get-tuple-element.123), channel_id=1, source_target_pairs={{0,7},{1,6},{2,5},{3,4},{4,3},{5,2},{6,1},{7,0},{8,15},{9,14},{10,... | collective-permute-start | bytes 1572872 | tf_op jit(solution)/shard_map/ppermute | solution.py:355
  103.9 95.5 %collective-permute-start.15 = (bf16[32,1,128,128]{3,2,1,0:T(8,128)(2,1)}, bf16[32,1,128,128]{3,2,1,0:T(8,128)(2,1)S(1)}, u32[]{:S(2)}, u32[]{:S(2)}) collective-permute-start(bf16[32,1,128,128]{3,2,1,0:T(8,128)(2,1)} %get-tuple-element.218), channel_id=1, source_target_pairs={{0,8},{8,16},{16,24},{24,0},{1,9},{9,17},{17,25},{25,1},{2,10},{10... | collective-permute-start | bytes 3145736 | tf_op jit(solution)/shard_map/ppermute | solution.py:404
  129.2 65.4 %collective-permute-start.50 = (bf16[1,6,16,32,128]{4,3,2,1,0:T(8,128)(2,1)}, bf16[1,6,16,32,128]{4,3,2,1,0:T(8,128)(2,1)}, u32[]{:S(2)}, u32[]{:S(2)}) collective-permute-start(bf16[1,6,16,32,128]{4,3,2,1,0:T(8,128)(2,1)} %get-tuple-element.164), channel_id=1, source_target_pairs={{0,1},{1,0},{2,3},{3,2},{4,5},{5,4},{6,7},{7,6},{8,9},{9,8},{10,11... | collective-permute-start | bytes 2359304 | tf_op jit(solution)/shard_map/ppermute | solution.py:355
  141.6 54.2 %collective-permute-start.51 = (bf16[1,6,16,32,128]{4,3,2,1,0:T(8,128)(2,1)}, bf16[1,6,16,32,128]{4,3,2,1,0:T(8,128)(2,1)}, u32[]{:S(2)}, u32[]{:S(2)}) collective-permute-start(bf16[1,6,16,32,128]{4,3,2,1,0:T(8,128)(2,1)} %get-tuple-element.165), channel_id=1, source_target_pairs={{0,2},{1,3},{2,0},{3,1},{4,6},{5,7},{6,4},{7,5},{8,10},{9,11},{10,... | collective-permute-start | bytes 2359304 | tf_op jit(solution)/shard_map/ppermute | solution.py:355
  141.6 54.2 %collective-permute-start.52 = (bf16[1,6,16,32,128]{4,3,2,1,0:T(8,128)(2,1)}, bf16[1,6,16,32,128]{4,3,2,1,0:T(8,128)(2,1)}, u32[]{:S(2)}, u32[]{:S(2)}) collective-permute-start(bf16[1,6,16,32,128]{4,3,2,1,0:T(8,128)(2,1)} %get-tuple-element.166), channel_id=1, source_target_pairs={{0,3},{1,2},{2,1},{3,0},{4,7},{5,6},{6,5},{7,4},{8,11},{9,10},{10,... | collective-permute-start | bytes 2359304 | tf_op jit(solution)/shard_map/ppermute | solution.py:355
  194.7 144.4 %collective-permute-start = (bf16[32,1,128,128]{3,2,1,0:T(8,128)(2,1)}, bf16[32,1,128,128]{3,2,1,0:T(8,128)(2,1)S(1)}, u32[]{:S(2)}, u32[]{:S(2)}) collective-permute-start(bf16[32,1,128,128]{3,2,1,0:T(8,128)(2,1)} %get-tuple-element.219), channel_id=1, source_target_pairs={{0,24},{8,0},{16,8},{24,16},{1,25},{9,1},{17,9},{25,17},{2,26},{10... | collective-permute-start | bytes 3145736 | tf_op jit(solution)/shard_map/ppermute | solution.py:405
  194.7 87.4 %collective-permute-start.53 = (bf16[1,6,16,32,128]{4,3,2,1,0:T(8,128)(2,1)}, bf16[1,6,16,32,128]{4,3,2,1,0:T(8,128)(2,1)}, u32[]{:S(2)}, u32[]{:S(2)}) collective-permute-start(bf16[1,6,16,32,128]{4,3,2,1,0:T(8,128)(2,1)} %get-tuple-element.167), channel_id=1, source_target_pairs={{0,4},{1,5},{2,6},{3,7},{4,0},{5,1},{6,2},{7,3},{8,12},{9,13},{10,... | collective-permute-start | bytes 2359304 | tf_op jit(solution)/shard_map/ppermute | solution.py:355
  195.8 102.1 %collective-permute-start.54 = (bf16[1,6,16,32,128]{4,3,2,1,0:T(8,128)(2,1)}, bf16[1,6,16,32,128]{4,3,2,1,0:T(8,128)(2,1)}, u32[]{:S(2)}, u32[]{:S(2)}) collective-permute-start(bf16[1,6,16,32,128]{4,3,2,1,0:T(8,128)(2,1)} %get-tuple-element.168), channel_id=1, source_target_pairs={{0,5},{1,4},{2,7},{3,6},{4,1},{5,0},{6,3},{7,2},{8,13},{9,12},{10,... | collective-permute-start | bytes 2359304 | tf_op jit(solution)/shard_map/ppermute | solution.py:355
  195.8 102.1 %collective-permute-start.55 = (bf16[1,6,16,32,128]{4,3,2,1,0:T(8,128)(2,1)}, bf16[1,6,16,32,128]{4,3,2,1,0:T(8,128)(2,1)}, u32[]{:S(2)}, u32[]{:S(2)}) collective-permute-start(bf16[1,6,16,32,128]{4,3,2,1,0:T(8,128)(2,1)} %get-tuple-element.169), channel_id=1, source_target_pairs={{0,6},{1,7},{2,4},{3,5},{4,2},{5,3},{6,0},{7,1},{8,14},{9,15},{10,... | collective-permute-start | bytes 2359304 | tf_op jit(solution)/shard_map/ppermute | solution.py:355
  199.4 115.8 %collective-permute-start.56 = (bf16[1,6,16,32,128]{4,3,2,1,0:T(8,128)(2,1)}, bf16[1,6,16,32,128]{4,3,2,1,0:T(8,128)(2,1)}, u32[]{:S(2)}, u32[]{:S(2)}) collective-permute-start(bf16[1,6,16,32,128]{4,3,2,1,0:T(8,128)(2,1)} %get-tuple-element.170), channel_id=1, source_target_pairs={{0,7},{1,6},{2,5},{3,4},{4,3},{5,2},{6,1},{7,0},{8,15},{9,14},{10,... | collective-permute-start | bytes 2359304 | tf_op jit(solution)/shard_map/ppermute | solution.py:355
  282.1 57.3 %collective-permute-start.16 = (bf16[1,2,16,32,128]{4,3,2,1,0:T(8,128)(2,1)}, bf16[1,2,16,32,128]{4,3,2,1,0:T(8,128)(2,1)S(1)}, u32[]{:S(2)}, u32[]{:S(2)}) collective-permute-start(bf16[1,2,16,32,128]{4,3,2,1,0:T(8,128)(2,1)} %get-tuple-element.126), channel_id=1, source_target_pairs={{0,1},{1,0},{2,3},{3,2},{4,5},{5,4},{6,7},{7,6},{8,9},{9,8},{10,11... | collective-permute-start | bytes 786440 | tf_op jit(solution)/shard_map/ppermute | solution.py:355
  297.8 56.7 %collective-permute-start.17 = (bf16[1,2,16,32,128]{4,3,2,1,0:T(8,128)(2,1)}, bf16[1,2,16,32,128]{4,3,2,1,0:T(8,128)(2,1)S(1)}, u32[]{:S(2)}, u32[]{:S(2)}) collective-permute-start(bf16[1,2,16,32,128]{4,3,2,1,0:T(8,128)(2,1)} %get-tuple-element.127), channel_id=1, source_target_pairs={{0,2},{1,3},{2,0},{3,1},{4,6},{5,7},{6,4},{7,5},{8,10},{9,11},{10,... | collective-permute-start | bytes 786440 | tf_op jit(solution)/shard_map/ppermute | solution.py:355
  297.8 58.6 %collective-permute-start.18 = (bf16[1,2,16,32,128]{4,3,2,1,0:T(8,128)(2,1)}, bf16[1,2,16,32,128]{4,3,2,1,0:T(8,128)(2,1)S(1)}, u32[]{:S(2)}, u32[]{:S(2)}) collective-permute-start(bf16[1,2,16,32,128]{4,3,2,1,0:T(8,128)(2,1)} %get-tuple-element.128), channel_id=1, source_target_pairs={{0,3},{1,2},{2,1},{3,0},{4,7},{5,6},{6,5},{7,4},{8,11},{9,10},{10,... | collective-permute-start | bytes 786440 | tf_op jit(solution)/shard_map/ppermute | solution.py:355
  315.3 52.4 %collective-permute-start.19 = (bf16[1,2,16,32,128]{4,3,2,1,0:T(8,128)(2,1)}, bf16[1,2,16,32,128]{4,3,2,1,0:T(8,128)(2,1)S(1)}, u32[]{:S(2)}, u32[]{:S(2)}) collective-permute-start(bf16[1,2,16,32,128]{4,3,2,1,0:T(8,128)(2,1)} %get-tuple-element.129), channel_id=1, source_target_pairs={{0,4},{1,5},{2,6},{3,7},{4,0},{5,1},{6,2},{7,3},{8,12},{9,13},{10,... | collective-permute-start | bytes 786440 | tf_op jit(solution)/shard_map/ppermute | solution.py:355
  339.1 35.8 %collective-permute-start.20 = (bf16[1,2,16,32,128]{4,3,2,1,0:T(8,128)(2,1)}, bf16[1,2,16,32,128]{4,3,2,1,0:T(8,128)(2,1)S(1)}, u32[]{:S(2)}, u32[]{:S(2)}) collective-permute-start(bf16[1,2,16,32,128]{4,3,2,1,0:T(8,128)(2,1)} %get-tuple-element.130), channel_id=1, source_target_pairs={{0,5},{1,4},{2,7},{3,6},{4,1},{5,0},{6,3},{7,2},{8,13},{9,12},{10,... | collective-permute-start | bytes 786440 | tf_op jit(solution)/shard_map/ppermute | solution.py:355
  339.4 35.5 %collective-permute-start.21 = (bf16[1,2,16,32,128]{4,3,2,1,0:T(8,128)(2,1)}, bf16[1,2,16,32,128]{4,3,2,1,0:T(8,128)(2,1)}, u32[]{:S(2)}, u32[]{:S(2)}) collective-permute-start(bf16[1,2,16,32,128]{4,3,2,1,0:T(8,128)(2,1)} %get-tuple-element.131), channel_id=1, source_target_pairs={{0,6},{1,7},{2,4},{3,5},{4,2},{5,3},{6,0},{7,1},{8,14},{9,15},{10,... | collective-permute-start | bytes 786440 | tf_op jit(solution)/shard_map/ppermute | solution.py:355
  356.4 49.3 %collective-permute-start.1 = (bf16[1,2,16,32,128]{4,3,2,1,0:T(8,128)(2,1)}, bf16[1,2,16,32,128]{4,3,2,1,0:T(8,128)(2,1)S(1)}, u32[]{:S(2)}, u32[]{:S(2)}) collective-permute-start(bf16[1,2,16,32,128]{4,3,2,1,0:T(8,128)(2,1)} %get-tuple-element.108), channel_id=1, source_target_pairs={{0,1},{1,0},{2,3},{3,2},{4,5},{5,4},{6,7},{7,6},{8,9},{9,8},{10,11... | collective-permute-start | bytes 786440 | tf_op jit(solution)/shard_map/ppermute | solution.py:355
  367.6 41.3 %collective-permute-start.2 = (bf16[1,2,16,32,128]{4,3,2,1,0:T(8,128)(2,1)}, bf16[1,2,16,32,128]{4,3,2,1,0:T(8,128)(2,1)S(1)}, u32[]{:S(2)}, u32[]{:S(2)}) collective-permute-start(bf16[1,2,16,32,128]{4,3,2,1,0:T(8,128)(2,1)} %get-tuple-element.109), channel_id=1, source_target_pairs={{0,2},{1,3},{2,0},{3,1},{4,6},{5,7},{6,4},{7,5},{8,10},{9,11},{10,... | collective-permute-start | bytes 786440 | tf_op jit(solution)/shard_map/ppermute | solution.py:355
  374.9 35.6 %collective-permute-start.3 = (bf16[1,2,16,32,128]{4,3,2,1,0:T(8,128)(2,1)}, bf16[1,2,16,32,128]{4,3,2,1,0:T(8,128)(2,1)S(1)}, u32[]{:S(2)}, u32[]{:S(2)}) collective-permute-start(bf16[1,2,16,32,128]{4,3,2,1,0:T(8,128)(2,1)} %get-tuple-element.110), channel_id=1, source_target_pairs={{0,3},{1,2},{2,1},{3,0},{4,7},{5,6},{6,5},{7,4},{8,11},{9,10},{10,... | collective-permute-start | bytes 786440 | tf_op jit(solution)/shard_map/ppermute | solution.py:355
  374.9 37.4 %collective-permute-start.4 = (bf16[1,2,16,32,128]{4,3,2,1,0:T(8,128)(2,1)}, bf16[1,2,16,32,128]{4,3,2,1,0:T(8,128)(2,1)S(1)}, u32[]{:S(2)}, u32[]{:S(2)}) collective-permute-start(bf16[1,2,16,32,128]{4,3,2,1,0:T(8,128)(2,1)} %get-tuple-element.111), channel_id=1, source_target_pairs={{0,4},{1,5},{2,6},{3,7},{4,0},{5,1},{6,2},{7,3},{8,12},{9,13},{10,... | collective-permute-start | bytes 786440 | tf_op jit(solution)/shard_map/ppermute | solution.py:355
  382.6 45.7 %collective-permute-start.5 = (bf16[1,2,16,32,128]{4,3,2,1,0:T(8,128)(2,1)}, bf16[1,2,16,32,128]{4,3,2,1,0:T(8,128)(2,1)S(1)}, u32[]{:S(2)}, u32[]{:S(2)}) collective-permute-start(bf16[1,2,16,32,128]{4,3,2,1,0:T(8,128)(2,1)} %get-tuple-element.112), channel_id=1, source_target_pairs={{0,5},{1,4},{2,7},{3,6},{4,1},{5,0},{6,3},{7,2},{8,13},{9,12},{10,... | collective-permute-start | bytes 786440 | tf_op jit(solution)/shard_map/ppermute | solution.py:355
  405.7 55.5 %collective-permute-start.66 = (bf16[6,1,256,128]{3,2,1,0:T(8,128)(2,1)}, bf16[6,1,256,128]{3,2,1,0:T(8,128)(2,1)S(1)}, u32[]{:S(2)}, u32[]{:S(2)}) collective-permute-start(bf16[6,1,256,128]{3,2,1,0:T(8,128)(2,1)} %get-tuple-element.182), channel_id=1, source_target_pairs={{0,1},{1,2},{2,3},{3,4},{4,5},{5,6},{6,7},{7,0},{8,9},{9,10},{10,1... | collective-permute-start | bytes 1179656 | tf_op jit(solution)/shard_map/ppermute | solution.py:453
  409.0 52.2 %collective-permute-start.67 = (bf16[6,1,256,128]{3,2,1,0:T(8,128)(2,1)}, bf16[6,1,256,128]{3,2,1,0:T(8,128)(2,1)S(1)}, u32[]{:S(2)}, u32[]{:S(2)}) collective-permute-start(bf16[6,1,256,128]{3,2,1,0:T(8,128)(2,1)} %get-tuple-element.183), channel_id=1, source_target_pairs={{0,7},{1,0},{2,1},{3,2},{4,3},{5,4},{6,5},{7,6},{8,15},{9,8},{10,9... | collective-permute-start | bytes 1179656 | tf_op jit(solution)/shard_map/ppermute | solution.py:454
  410.5 37.9 %collective-permute-start.6 = (bf16[1,2,16,32,128]{4,3,2,1,0:T(8,128)(2,1)}, bf16[1,2,16,32,128]{4,3,2,1,0:T(8,128)(2,1)S(1)}, u32[]{:S(2)}, u32[]{:S(2)}) collective-permute-start(bf16[1,2,16,32,128]{4,3,2,1,0:T(8,128)(2,1)} %get-tuple-element.113), channel_id=1, source_target_pairs={{0,6},{1,7},{2,4},{3,5},{4,2},{5,3},{6,0},{7,1},{8,14},{9,15},{10,... | collective-permute-start | bytes 786440 | tf_op jit(solution)/shard_map/ppermute | solution.py:355
  412.3 38.3 %collective-permute-start.7 = (bf16[1,2,16,32,128]{4,3,2,1,0:T(8,128)(2,1)}, bf16[1,2,16,32,128]{4,3,2,1,0:T(8,128)(2,1)S(1)}, u32[]{:S(2)}, u32[]{:S(2)}) collective-permute-start(bf16[1,2,16,32,128]{4,3,2,1,0:T(8,128)(2,1)} %get-tuple-element.114), channel_id=1, source_target_pairs={{0,7},{1,6},{2,5},{3,4},{4,3},{5,2},{6,1},{7,0},{8,15},{9,14},{10,... | collective-permute-start | bytes 786440 | tf_op jit(solution)/shard_map/ppermute | solution.py:355
  448.5 37.0 %collective-permute-start.77 = (bf16[1,2,16,32,128]{4,3,2,1,0:T(8,128)(2,1)}, bf16[1,2,16,32,128]{4,3,2,1,0:T(8,128)(2,1)S(1)}, u32[]{:S(2)}, u32[]{:S(2)}) collective-permute-start(bf16[1,2,16,32,128]{4,3,2,1,0:T(8,128)(2,1)} %get-tuple-element.195), channel_id=1, source_target_pairs={{0,1},{1,0},{2,3},{3,2},{4,5},{5,4},{6,7},{7,6},{8,9},{9,8},{10,11... | collective-permute-start | bytes 786440 | tf_op jit(solution)/shard_map/ppermute | solution.py:355
  450.6 31.5 %collective-permute-start.41 = (bf16[2,1,256,128]{3,2,1,0:T(8,128)(2,1)}, bf16[2,1,256,128]{3,2,1,0:T(8,128)(2,1)S(1)}, u32[]{:S(2)}, u32[]{:S(2)}) collective-permute-start(bf16[2,1,256,128]{3,2,1,0:T(8,128)(2,1)} %get-tuple-element.153), channel_id=1, source_target_pairs={{0,1},{1,2},{2,3},{3,4},{4,5},{5,6},{6,7},{7,0},{8,9},{9,10},{10,1... | collective-permute-start | bytes 393224 | tf_op jit(solution)/shard_map/ppermute | solution.py:453
  482.1 50.0 %collective-permute-start.59 = (bf16[1,4,16,32,128]{4,3,2,1,0:T(8,128)(2,1)}, bf16[1,4,16,32,128]{4,3,2,1,0:T(8,128)(2,1)S(1)}, u32[]{:S(2)}, u32[]{:S(2)}) collective-permute-start(bf16[1,4,16,32,128]{4,3,2,1,0:T(8,128)(2,1)} %get-tuple-element.175), channel_id=1, source_target_pairs={{0,1},{1,0},{2,3},{3,2},{4,5},{5,4},{6,7},{7,6},{8,9},{9,8},{10,11... | collective-permute-start | bytes 1572872 | tf_op jit(solution)/shard_map/ppermute | solution.py:355
  488.6 33.6 %collective-permute-start.83 = (bf16[1,2,16,32,128]{4,3,2,1,0:T(8,128)(2,1)}, bf16[1,2,16,32,128]{4,3,2,1,0:T(8,128)(2,1)S(1)}, u32[]{:S(2)}, u32[]{:S(2)}) collective-permute-start(bf16[1,2,16,32,128]{4,3,2,1,0:T(8,128)(2,1)} %get-tuple-element.201), channel_id=1, source_target_pairs={{0,7},{1,6},{2,5},{3,4},{4,3},{5,2},{6,1},{7,0},{8,15},{9,14},{10,... | collective-permute-start | bytes 786440 | tf_op jit(solution)/shard_map/ppermute | solution.py:355
  509.4 52.8 %collective-permute-start.60 = (bf16[1,4,16,32,128]{4,3,2,1,0:T(8,128)(2,1)}, bf16[1,4,16,32,128]{4,3,2,1,0:T(8,128)(2,1)S(1)}, u32[]{:S(2)}, u32[]{:S(2)}) collective-permute-start(bf16[1,4,16,32,128]{4,3,2,1,0:T(8,128)(2,1)} %get-tuple-element.176), channel_id=1, source_target_pairs={{0,2},{1,3},{2,0},{3,1},{4,6},{5,7},{6,4},{7,5},{8,10},{9,11},{10,... | collective-permute-start | bytes 1572872 | tf_op jit(solution)/shard_map/ppermute | solution.py:355
  515.7 49.8 %collective-permute-start.61 = (bf16[1,4,16,32,128]{4,3,2,1,0:T(8,128)(2,1)}, bf16[1,4,16,32,128]{4,3,2,1,0:T(8,128)(2,1)}, u32[]{:S(2)}, u32[]{:S(2)}) collective-permute-start(bf16[1,4,16,32,128]{4,3,2,1,0:T(8,128)(2,1)} %get-tuple-element.177), channel_id=1, source_target_pairs={{0,3},{1,2},{2,1},{3,0},{4,7},{5,6},{6,5},{7,4},{8,11},{9,10},{10,... | collective-permute-start | bytes 1572872 | tf_op jit(solution)/shard_map/ppermute | solution.py:355
  515.7 57.0 %collective-permute-start.62 = (bf16[1,4,16,32,128]{4,3,2,1,0:T(8,128)(2,1)}, bf16[1,4,16,32,128]{4,3,2,1,0:T(8,128)(2,1)}, u32[]{:S(2)}, u32[]{:S(2)}) collective-permute-start(bf16[1,4,16,32,128]{4,3,2,1,0:T(8,128)(2,1)} %get-tuple-element.178), channel_id=1, source_target_pairs={{0,4},{1,5},{2,6},{3,7},{4,0},{5,1},{6,2},{7,3},{8,12},{9,13},{10,... | collective-permute-start | bytes 1572872 | tf_op jit(solution)/shard_map/ppermute | solution.py:355
  522.2 73.9 %collective-permute-start.63 = (bf16[1,4,16,32,128]{4,3,2,1,0:T(8,128)(2,1)}, bf16[1,4,16,32,128]{4,3,2,1,0:T(8,128)(2,1)}, u32[]{:S(2)}, u32[]{:S(2)}) collective-permute-start(bf16[1,4,16,32,128]{4,3,2,1,0:T(8,128)(2,1)} %get-tuple-element.179), channel_id=1, source_target_pairs={{0,5},{1,4},{2,7},{3,6},{4,1},{5,0},{6,3},{7,2},{8,13},{9,12},{10,... | collective-permute-start | bytes 1572872 | tf_op jit(solution)/shard_map/ppermute | solution.py:355
  532.9 63.3 %collective-permute-start.64 = (bf16[1,4,16,32,128]{4,3,2,1,0:T(8,128)(2,1)}, bf16[1,4,16,32,128]{4,3,2,1,0:T(8,128)(2,1)}, u32[]{:S(2)}, u32[]{:S(2)}) collective-permute-start(bf16[1,4,16,32,128]{4,3,2,1,0:T(8,128)(2,1)} %get-tuple-element.180), channel_id=1, source_target_pairs={{0,6},{1,7},{2,4},{3,5},{4,2},{5,3},{6,0},{7,1},{8,14},{9,15},{10,... | collective-permute-start | bytes 1572872 | tf_op jit(solution)/shard_map/ppermute | solution.py:355
  563.1 54.0 %collective-permute-start.68 = (bf16[1,6,16,32,128]{4,3,2,1,0:T(8,128)(2,1)}, bf16[1,6,16,32,128]{4,3,2,1,0:T(8,128)(2,1)S(1)}, u32[]{:S(2)}, u32[]{:S(2)}) collective-permute-start(bf16[1,6,16,32,128]{4,3,2,1,0:T(8,128)(2,1)} %get-tuple-element.185), channel_id=1, source_target_pairs={{0,1},{1,0},{2,3},{3,2},{4,5},{5,4},{6,7},{7,6},{8,9},{9,8},{10,11... | collective-permute-start | bytes 2359304 | tf_op jit(solution)/shard_map/ppermute | solution.py:355
  565.5 80.2 %collective-permute-start.33 = (bf16[1,16,256,128]{3,2,1,0:T(8,128)(2,1)}, bf16[1,16,256,128]{3,2,1,0:T(8,128)(2,1)}, u32[]{:S(2)}, u32[]{:S(2)}) collective-permute-start(bf16[1,16,256,128]{3,2,1,0:T(8,128)(2,1)} %slice.127), channel_id=1, source_target_pairs={{0,8},{8,16},{16,24},{24,0},{1,9},{9,17},{17,25},{25,1},{2,10},{10... | collective-permute-start | bytes 3145736 | tf_op jit(solution)/shard_map/ppermute | solution.py:455
  572.8 43.6 %collective-permute-start.65 = (bf16[1,4,16,32,128]{4,3,2,1,0:T(8,128)(2,1)}, bf16[1,4,16,32,128]{4,3,2,1,0:T(8,128)(2,1)}, u32[]{:S(2)}, u32[]{:S(2)}) collective-permute-start(bf16[1,4,16,32,128]{4,3,2,1,0:T(8,128)(2,1)} %get-tuple-element.181), channel_id=1, source_target_pairs={{0,7},{1,6},{2,5},{3,4},{4,3},{5,2},{6,1},{7,0},{8,15},{9,14},{10,... | collective-permute-start | bytes 1572872 | tf_op jit(solution)/shard_map/ppermute | solution.py:355
  596.1 31.9 %collective-permute-start.69 = (bf16[1,6,16,32,128]{4,3,2,1,0:T(8,128)(2,1)}, bf16[1,6,16,32,128]{4,3,2,1,0:T(8,128)(2,1)}, u32[]{:S(2)}, u32[]{:S(2)}) collective-permute-start(bf16[1,6,16,32,128]{4,3,2,1,0:T(8,128)(2,1)} %get-tuple-element.186), channel_id=1, source_target_pairs={{0,2},{1,3},{2,0},{3,1},{4,6},{5,7},{6,4},{7,5},{8,10},{9,11},{10,... | collective-permute-start | bytes 2359304 | tf_op jit(solution)/shard_map/ppermute | solution.py:355
  596.3 43.3 %collective-permute-start.70 = (bf16[1,6,16,32,128]{4,3,2,1,0:T(8,128)(2,1)}, bf16[1,6,16,32,128]{4,3,2,1,0:T(8,128)(2,1)}, u32[]{:S(2)}, u32[]{:S(2)}) collective-permute-start(bf16[1,6,16,32,128]{4,3,2,1,0:T(8,128)(2,1)} %get-tuple-element.187), channel_id=1, source_target_pairs={{0,3},{1,2},{2,1},{3,0},{4,7},{5,6},{6,5},{7,4},{8,11},{9,10},{10,... | collective-permute-start | bytes 2359304 | tf_op jit(solution)/shard_map/ppermute | solution.py:355
  617.1 96.0 %collective-permute-start.71 = (bf16[1,6,16,32,128]{4,3,2,1,0:T(8,128)(2,1)}, bf16[1,6,16,32,128]{4,3,2,1,0:T(8,128)(2,1)}, u32[]{:S(2)}, u32[]{:S(2)}) collective-permute-start(bf16[1,6,16,32,128]{4,3,2,1,0:T(8,128)(2,1)} %get-tuple-element.188), channel_id=1, source_target_pairs={{0,4},{1,5},{2,6},{3,7},{4,0},{5,1},{6,2},{7,3},{8,12},{9,13},{10,... | collective-permute-start | bytes 2359304 | tf_op jit(solution)/shard_map/ppermute | solution.py:355
  628.0 166.2 %collective-permute-start.23 = (bf16[1,16,256,128]{3,2,1,0:T(8,128)(2,1)}, bf16[1,16,256,128]{3,2,1,0:T(8,128)(2,1)S(1)}, u32[]{:S(2)}, u32[]{:S(2)}) collective-permute-start(bf16[1,16,256,128]{3,2,1,0:T(8,128)(2,1)} %slice.126), channel_id=1, source_target_pairs={{0,24},{8,0},{16,8},{24,16},{1,25},{9,1},{17,9},{25,17},{2,26},{10... | collective-permute-start | bytes 3145736 | tf_op jit(solution)/shard_map/ppermute | solution.py:456
  639.5 89.9 %collective-permute-start.72 = (bf16[1,6,16,32,128]{4,3,2,1,0:T(8,128)(2,1)}, bf16[1,6,16,32,128]{4,3,2,1,0:T(8,128)(2,1)}, u32[]{:S(2)}, u32[]{:S(2)}) collective-permute-start(bf16[1,6,16,32,128]{4,3,2,1,0:T(8,128)(2,1)} %get-tuple-element.189), channel_id=1, source_target_pairs={{0,5},{1,4},{2,7},{3,6},{4,1},{5,0},{6,3},{7,2},{8,13},{9,12},{10,... | collective-permute-start | bytes 2359304 | tf_op jit(solution)/shard_map/ppermute | solution.py:355
  643.8 85.7 %collective-permute-start.73 = (bf16[1,6,16,32,128]{4,3,2,1,0:T(8,128)(2,1)}, bf16[1,6,16,32,128]{4,3,2,1,0:T(8,128)(2,1)}, u32[]{:S(2)}, u32[]{:S(2)}) collective-permute-start(bf16[1,6,16,32,128]{4,3,2,1,0:T(8,128)(2,1)} %get-tuple-element.190), channel_id=1, source_target_pairs={{0,6},{1,7},{2,4},{3,5},{4,2},{5,3},{6,0},{7,1},{8,14},{9,15},{10,... | collective-permute-start | bytes 2359304 | tf_op jit(solution)/shard_map/ppermute | solution.py:355
  645.7 85.7 %collective-permute-start.74 = (bf16[1,6,16,32,128]{4,3,2,1,0:T(8,128)(2,1)}, bf16[1,6,16,32,128]{4,3,2,1,0:T(8,128)(2,1)}, u32[]{:S(2)}, u32[]{:S(2)}) collective-permute-start(bf16[1,6,16,32,128]{4,3,2,1,0:T(8,128)(2,1)} %get-tuple-element.191), channel_id=1, source_target_pairs={{0,7},{1,6},{2,5},{3,4},{4,3},{5,2},{6,1},{7,0},{8,15},{9,14},{10,... | collective-permute-start | bytes 2359304 | tf_op jit(solution)/shard_map/ppermute | solution.py:355
  713.1 84.1 %collective-permute-start.43 = (bf16[1,2,16,32,128]{4,3,2,1,0:T(8,128)(2,1)}, bf16[1,2,16,32,128]{4,3,2,1,0:T(8,128)(2,1)S(1)}, u32[]{:S(2)}, u32[]{:S(2)}) collective-permute-start(bf16[1,2,16,32,128]{4,3,2,1,0:T(8,128)(2,1)} %get-tuple-element.156), channel_id=1, source_target_pairs={{0,1},{1,0},{2,3},{3,2},{4,5},{5,4},{6,7},{7,6},{8,9},{9,8},{10,11... | collective-permute-start | bytes 786440 | tf_op jit(solution)/shard_map/ppermute | solution.py:355
  729.4 64.8 %collective-permute-start.88 = (f32[2,6,2,16,128]{4,1,3,2,0:T(8,128)S(1)}, f32[2,6,2,16,128]{4,1,3,2,0:T(8,128)S(1)}, u32[]{:S(2)}, u32[]{:S(2)}) collective-permute-start(f32[2,6,2,16,128]{4,1,3,2,0:T(8,128)S(1)} %bitcast.172), channel_id=1, source_target_pairs={{0,2},{1,3},{2,0},{3,1},{4,6},{5,7},{6,4},{7,5},{8,10},{9,11},{10,... | collective-permute-start | bytes 589832 | tf_op jit(solution)/shard_map/ppermute | solution.py:355
  731.5 61.2 %collective-permute-start.25 = (bf16[2,1,256,128]{3,2,1,0:T(8,128)(2,1)S(1)}, bf16[2,1,256,128]{3,2,1,0:T(8,128)(2,1)S(1)}, u32[]{:S(2)}, u32[]{:S(2)}) collective-permute-start(bf16[2,1,256,128]{3,2,1,0:T(8,128)(2,1)S(1)} %copy-done.80), channel_id=1, source_target_pairs={{0,7},{1,0},{2,1},{3,2},{4,3},{5,4},{6,5},{7,6},{8,15},{9,8},{10,9... | collective-permute-start | bytes 393224 | tf_op jit(solution)/shard_map/ppermute | solution.py:454
  759.5 54.0 %collective-permute-start.44 = (bf16[1,2,16,32,128]{4,3,2,1,0:T(8,128)(2,1)}, bf16[1,2,16,32,128]{4,3,2,1,0:T(8,128)(2,1)}, u32[]{:S(2)}, u32[]{:S(2)}) collective-permute-start(bf16[1,2,16,32,128]{4,3,2,1,0:T(8,128)(2,1)} %get-tuple-element.157), channel_id=1, source_target_pairs={{0,2},{1,3},{2,0},{3,1},{4,6},{5,7},{6,4},{7,5},{8,10},{9,11},{10,... | collective-permute-start | bytes 786440 | tf_op jit(solution)/shard_map/ppermute | solution.py:355
  794.2 32.9 %collective-permute-start.46 = (bf16[1,2,16,32,128]{4,3,2,1,0:T(8,128)(2,1)}, bf16[1,2,16,32,128]{4,3,2,1,0:T(8,128)(2,1)}, u32[]{:S(2)}, u32[]{:S(2)}) collective-permute-start(bf16[1,2,16,32,128]{4,3,2,1,0:T(8,128)(2,1)} %get-tuple-element.159), channel_id=1, source_target_pairs={{0,4},{1,5},{2,6},{3,7},{4,0},{5,1},{6,2},{7,3},{8,12},{9,13},{10,... | collective-permute-start | bytes 786440 | tf_op jit(solution)/shard_map/ppermute | solution.py:355
  794.3 38.4 %collective-permute-start.47 = (bf16[1,2,16,32,128]{4,3,2,1,0:T(8,128)(2,1)}, bf16[1,2,16,32,128]{4,3,2,1,0:T(8,128)(2,1)}, u32[]{:S(2)}, u32[]{:S(2)}) collective-permute-start(bf16[1,2,16,32,128]{4,3,2,1,0:T(8,128)(2,1)} %get-tuple-element.160), channel_id=1, source_target_pairs={{0,5},{1,4},{2,7},{3,6},{4,1},{5,0},{6,3},{7,2},{8,13},{9,12},{10,... | collective-permute-start | bytes 786440 | tf_op jit(solution)/shard_map/ppermute | solution.py:355
  797.2 35.6 %collective-permute-start.48 = (bf16[1,2,16,32,128]{4,3,2,1,0:T(8,128)(2,1)}, bf16[1,2,16,32,128]{4,3,2,1,0:T(8,128)(2,1)}, u32[]{:S(2)}, u32[]{:S(2)}) collective-permute-start(bf16[1,2,16,32,128]{4,3,2,1,0:T(8,128)(2,1)} %get-tuple-element.161), channel_id=1, source_target_pairs={{0,6},{1,7},{2,4},{3,5},{4,2},{5,3},{6,0},{7,1},{8,14},{9,15},{10,... | collective-permute-start | bytes 786440 | tf_op jit(solution)/shard_map/ppermute | solution.py:355
  813.6 87.6 %collective-permute-start.93 = (f32[4,6,4,16,128]{4,3,2,1,0:T(8,128)}, f32[4,6,4,16,128]{4,3,2,1,0:T(8,128)}, u32[]{:S(2)}, u32[]{:S(2)}) collective-permute-start(f32[4,6,4,16,128]{4,3,2,1,0:T(8,128)} %slice_bitcast_fusion.2), channel_id=1, source_target_pairs={{0,1},{1,0},{2,3},{3,2},{4,5},{5,4},{6,7},{7,6},{8,9},{9,8},{10,11... | collective-permute-start | bytes 2359304 | tf_op jit(solution)/shard_map/ppermute | solution.py:355
  840.0 30.7 %collective-permute-start.29 = (bf16[1,2,16,32,128]{4,3,2,1,0:T(8,128)(2,1)}, bf16[1,2,16,32,128]{4,3,2,1,0:T(8,128)(2,1)}, u32[]{:S(2)}, u32[]{:S(2)}) collective-permute-start(bf16[1,2,16,32,128]{4,3,2,1,0:T(8,128)(2,1)} %get-tuple-element.140), channel_id=1, source_target_pairs={{0,4},{1,5},{2,6},{3,7},{4,0},{5,1},{6,2},{7,3},{8,12},{9,13},{10,... | collective-permute-start | bytes 786440 | tf_op jit(solution)/shard_map/ppermute | solution.py:355
  870.7 48.2 %collective-permute-start.90 = (f32[4,6,6,16,128]{4,3,2,1,0:T(8,128)}, f32[4,6,6,16,128]{4,3,2,1,0:T(8,128)}, u32[]{:S(2)}, u32[]{:S(2)}) collective-permute-start(f32[4,6,6,16,128]{4,3,2,1,0:T(8,128)} %slice_bitcast_fusion), channel_id=1, source_target_pairs={{0,1},{1,0},{2,3},{3,2},{4,5},{5,4},{6,7},{7,6},{8,9},{9,8},{10,11... | collective-permute-start | bytes 3538952 | tf_op jit(solution)/shard_map/ppermute | solution.py:355
  877.2 63.6 %collective-permute-start.89 = (bf16[1,6,2,16,128]{4,1,3,2,0:T(8,128)(2,1)}, bf16[1,6,2,16,128]{4,1,3,2,0:T(8,128)(2,1)}, u32[]{:S(2)}, u32[]{:S(2)}) collective-permute-start(bf16[1,6,2,16,128]{4,1,3,2,0:T(8,128)(2,1)} %fusion.33), channel_id=1, source_target_pairs={{0,4},{1,5},{2,6},{3,7},{4,0},{5,1},{6,2},{7,3},{8,12},{9,13},{10,... | collective-permute-start | bytes 147464 | tf_op jit(solution)/shard_map/ppermute | solution.py:355
  883.4 58.3 %all-to-all-start = ((bf16[8,6,2,16,128]{4,3,2,1,0:T(8,128)(2,1)}), bf16[8,6,2,16,128]{4,3,2,1,0:T(8,128)(2,1)}, u32[]{:S(2)}, u32[]{:S(2)}) async-start(bf16[8,6,2,16,128]{4,3,2,1,0:T(8,128)(2,1)} %get-tuple-element.211), calls=%async_computation | async-start | bytes 786432 | tf_op jit(solution)/shard_map/all_to_all | solution.py:359
  (120 other events, 2900.8 us)

commit v3 on v2

--- a/solution.py
+++ b/solution.py
@@ -7,9 +7,10 @@
 from jax.experimental.pallas import tpu as pltpu
 from jax.sharding import PartitionSpec as P
 
-SHARES = (2, 2, 6, 4, 2)
+SHARES = (2, 3, 5, 5, 1)
 SENDING = (1, 2, 0, 3, 4)
 RETURNING = (1, 2, 3, 0, 4)
+CLOSING = RETURNING[-2:]
 DISTANCES = (2, 3, 1, 6, 7, 4, 5)
 
 step_length = 0.3
@@ -87,6 +88,8 @@
     count, width = staged.shape[0], staged.shape[1]
     group, rows = outs[0].shape[0], outs[0].shape[2]
 
+    first = place[0] * count
+
     def one(o, carry):
         f = centre[o, 0].astype(F32)
         zm = below[o, 0].astype(F32)
@@ -96,13 +99,20 @@
         if has_high:
             zp = jnp.where(z == last, high[o, 0].astype(F32), zp)
         lanes = f.shape[1]
-        moved = coef[6, o] * f
-        moved += coef[0, o] * pltpu.roll(f, 1, 1) + coef[1, o] * pltpu.roll(f, lanes - 1, 1)
-        moved += coef[2, o] * pltpu.roll(f, 1, 0) + coef[3, o] * pltpu.roll(f, width - 1, 0)
-        moved += coef[4, o] * zm + coef[5, o] * zp
-        exponent = coef[7, o] * field[0, 0].astype(F32)
+        ux, uy, uz = (coef[axis, first + o] for axis in range(3))
+        moved = (1.0 - step_length * (jnp.abs(ux) + jnp.abs(uy) + jnp.abs(uz))) * f
+        sides = (
+            (pltpu.roll(f, 1, 1), pltpu.roll(f, lanes - 1, 1)),
+            (pltpu.roll(f, 1, 0), pltpu.roll(f, width - 1, 0)),
+            (zm, zp),
+        )
+        for u, (back, fore) in zip((ux, uy, uz), sides):
+            moved += (step_length * jnp.maximum(u, 0.0)) * back
+            moved -= (step_length * jnp.minimum(u, 0.0)) * fore
+        terms = (ux * ux, uy * uy, uz * uz, 2.0 * ux * uy, 2.0 * ux * uz, 2.0 * uy * uz)
+        exponent = (-step_length * terms[0]) * field[0, 0].astype(F32)
         for c in range(1, 6):
-            exponent += coef[7 + c, o] * field[c, 0].astype(F32)
+            exponent += (-step_length * terms[c]) * field[c, 0].astype(F32)
         staged[o] = moved * jnp.exp(exponent)
         return carry
 
@@ -368,13 +378,13 @@
     return came
 
 
-def halve(held):
+def halve(held, narrow):
     stride = 1
     while held.shape[0] > 1:
         half = held.shape[0] // 2
         pairs = held.reshape((half, 2) + held.shape[1:])
         theirs = pairs[:, 1]
-        if half == 1:
+        if narrow or half == 1:
             theirs = theirs.astype(BF16)
         came = swapped(theirs, stride)
         held = pairs[:, 0] + came.astype(F32)
@@ -407,9 +417,6 @@
     field_terms, tensor_terms = angle_tables(orientations)
     weights = stencil_weights(orientations)
     exponent_terms = -step_length * field_terms
-    local_coef = lax.dynamic_slice_in_dim(
-        jnp.concatenate([weights, exponent_terms]), me * count, count, 1
-    )
     local_tensor = lax.dynamic_slice_in_dim(
         tensor_terms * orient_weight[None, :], me * count, count, 1
     )
@@ -438,7 +445,7 @@
     norths = {}
     for c in SENDING:
         sent = advect(
-            local_coef,
+            orientations,
             place,
             q_init,
             first if c == 0 else None,
@@ -472,14 +479,14 @@
             owners,
         )
         got = exchange_blocks(sent)
-        closing = c == RETURNING[-1] or not paired(owners)
+        closing = c in CLOSING or not paired(owners)
         state, partial = gather(
             local_tensor, place, got, partner, state, starts[c], closing
         )
         if closing:
             sums[c] = jnp.sum(exchange(partial).astype(F32), axis=0)
         else:
-            sums[c] = halve(partial)
+            sums[c] = halve(partial, c == RETURNING[2])
     tensor = jnp.concatenate([sums[c] for c in range(chunks)], axis=1)
     new_field = (1.0 - relax_rate) * own_field.astype(F32) + relax_rate * coupling * tensor
     return (state, new_field)

time: 954 us -> 949 us (level)
  waiting for transfers between devices: 386 us -> 325 us
  starting transfers between devices: 283 us -> 338 us
    ppermute x5, starting transfers between devices: 6.85 us -> 40.8 us  [staged_device(): souths[c] = lax.ppermute(top_rows, 'orient', ring(owners, 1))]
    ppermute x82 -> x79, waiting for transfers between devices: 337 us -> 307 us  [swapped(): lax.ppermute(block, 'orient', [(i, i ^ distance) for i in range(owners)])]
    ppermute x5, waiting for transfers between devices: 30.8 us -> 5.79 us  [staged_device(): souths[c] = lax.ppermute(top_rows, 'orient', ring(owners, 1))]
    ppermute x82 -> x79, starting transfers between devices: 250 us -> 273 us  [swapped(): lax.ppermute(block, 'orient', [(i, i ^ distance) for i in range(owners)])]
    ppermute x5, waiting for transfers between devices: 17.8 us -> 5.26 us  [staged_device(): norths[c] = lax.ppermute(end_rows, 'orient', ring(owners, -1))]
  transfers between devices with their start and end apart: 97 -> 95, of which waited for: 29 -> 25; matrix products, arithmetic and copies ran while one was open for 3% -> 3% of each run, Pallas kernels for 25% -> 24%
where the time goes in v3:
time: 949 us; the launch traced here: 948 us
  starting transfers between devices  338 us (36%)
  waiting for transfers between devices  325 us (34%)
  Pallas kernels  245 us (26%)
  local copies, waits for them, and re-layouts  21.8 us (2%)
  other arithmetic  14.4 us (2%)
    ppermute x79, waiting for transfers between devices, swapped(): lax.ppermute(block, 'orient', [(i, i ^ distance) for i in range(owners)])  307 us
    ppermute x79, starting transfers between devices, swapped(): lax.ppermute(block, 'orient', [(i, i ^ distance) for i in range(owners)])  273 us
    pallas_call x5, Pallas kernels, advect_turn(): pl.pallas_call(functools.partial(advect_turn_kernel, pieces), grid=(depth...  86 us
    pallas_call x5, Pallas kernels, advect(): pl.pallas_call(functools.partial(advect_kernel, low is not None, high is...  76.2 us
    pallas_call x5, Pallas kernels, gather(): pl.pallas_call(functools.partial(gather_kernel, pieces, closing), grid=(d...  44.7 us
    ppermute x5, starting transfers between devices, staged_device(): souths[c] = lax.ppermute(top_rows, 'orient', ring(owners, 1))  40.8 us
    pallas_call x5, Pallas kernels, turn(): pl.pallas_call(functools.partial(turn_kernel, pieces), grid=(depth,), in_...  38 us
  transfers between devices with their start and end apart: 95, of which 25 were waited for; matrix products, arithmetic and copies ran while one was open for 3% of the time, Pallas kernels for 24%

profile of v3, /device:TPU:0, one launch (start us, length us, event | category | flops | bytes accessed | tf_op | source)
XLA Modules:
  0.0 947.8 jit_solution(5538845711787136904)
XLA Ops:
  0.7 14.3 %advect_first.8 = (bf16[1,3,16,32,128]{4,3,2,1,0:T(8,128)(2,1)}, bf16[1,3,16,32,128]{4,3,2,1,0:T(8,128)(2,1)}, bf16[1,3,16,32,128]{4,3,2,1,0:T(8,128)(2,1)}, bf1...) custom-call(f32[3,256]{1,0:T(4,128)} %refs_0_.9, ...), custom_call_target="tpu_custom_call" | custom-call | flops 47185920 | bytes 12582912 | tf_op jit(solution)/shard_map/advect_first/pallas_call | solution.py:147
  19.6 22.0 %advect_first.6 = (bf16[1,5,16,32,128]{4,3,2,1,0:T(8,128)(2,1)}, bf16[1,5,16,32,128]{4,3,2,1,0:T(8,128)(2,1)}, bf16[1,5,16,32,128]{4,3,2,1,0:T(8,128)(2,1)}, bf1...) custom-call(f32[3,256]{1,0:T(4,128)} %refs_0_.9, ...), custom_call_target="tpu_custom_call" | custom-call | flops 78643200 | bytes 20971520 | tf_op jit(solution)/shard_map/advect_first/pallas_call | solution.py:147
  46.2 3.9 collective-permute-start.39
  51.2 38.0 %collective-permute-done.37.refs_4_ = bf16[1,3,16,32,128]{4,3,2,1,0:T(8,128)(2,1)S(1)} collective-permute-done((bf16[1,3,16,32,128]{4,3,2,1,0:T(8,128)(2,1)}, bf16[1,3,16,32,128]{4,3,2,1,0:T(8,128)(2,1)S(1)}, u32[]{:S(2)}, u32[]{:S(2)}) %collective-permute-start.37) | collective-permute-done | bytes 393248 | tf_op jit(solution)/shard_map/ppermute | solution.py:365
  89.3 8.3 collective-permute-done.38.refs_5_
  97.7 10.0 %collective-permute-start.11 = (bf16[1,5,16,32,128]{4,3,2,1,0:T(8,128)(2,1)}, bf16[1,5,16,32,128]{4,3,2,1,0:T(8,128)(2,1)}, u32[]{:S(2)}, u32[]{:S(2)}) collective-permute-start(bf16[1,5,16,32,128]{4,3,2,1,0:T(8,128)(2,1)} %get-tuple-element.120), channel_id=1, source_target_pairs={{0,4},{1,5},{2,6},{3,7},{4,0},{5,1},{6,2},{7,3},{8,12},{9,13},{10,... | collective-permute-start | bytes 1966088 | tf_op jit(solution)/shard_map/ppermute | solution.py:365
  107.7 17.3 %collective-permute-start.12 = (bf16[1,5,16,32,128]{4,3,2,1,0:T(8,128)(2,1)}, bf16[1,5,16,32,128]{4,3,2,1,0:T(8,128)(2,1)}, u32[]{:S(2)}, u32[]{:S(2)}) collective-permute-start(bf16[1,5,16,32,128]{4,3,2,1,0:T(8,128)(2,1)} %get-tuple-element.121), channel_id=1, source_target_pairs={{0,5},{1,4},{2,7},{3,6},{4,1},{5,0},{6,3},{7,2},{8,13},{9,12},{10,... | collective-permute-start | bytes 1966088 | tf_op jit(solution)/shard_map/ppermute | solution.py:365
  128.0 22.1 %advect_first.9 = (bf16[1,5,16,32,128]{4,3,2,1,0:T(8,128)(2,1)}, bf16[1,5,16,32,128]{4,3,2,1,0:T(8,128)(2,1)}, bf16[1,5,16,32,128]{4,3,2,1,0:T(8,128)(2,1)}, bf1...) custom-call(f32[3,256]{1,0:T(4,128)} %refs_0_.9, ...), custom_call_target="tpu_custom_call" | custom-call | flops 78643200 | bytes 20971520 | tf_op jit(solution)/shard_map/advect_first/pallas_call | solution.py:147
  157.6 32.4 %collective-permute-done.11.refs_4_ = bf16[1,5,16,32,128]{4,3,2,1,0:T(8,128)(2,1)} collective-permute-done((bf16[1,5,16,32,128]{4,3,2,1,0:T(8,128)(2,1)}, bf16[1,5,16,32,128]{4,3,2,1,0:T(8,128)(2,1)}, u32[]{:S(2)}, u32[]{:S(2)}) %collective-permute-start.11) | collective-permute-done | bytes 655392 | tf_op jit(solution)/shard_map/ppermute | solution.py:365
  191.6 12.3 %collective-permute-done.12.refs_5_ = bf16[1,5,16,32,128]{4,3,2,1,0:T(8,128)(2,1)} collective-permute-done((bf16[1,5,16,32,128]{4,3,2,1,0:T(8,128)(2,1)}, bf16[1,5,16,32,128]{4,3,2,1,0:T(8,128)(2,1)}, u32[]{:S(2)}, u32[]{:S(2)}) %collective-permute-start.12) | collective-permute-done | bytes 655392 | tf_op jit(solution)/shard_map/ppermute | solution.py:365
  205.7 16.0 %collective-permute-start.53 = (bf16[1,5,16,32,128]{4,3,2,1,0:T(8,128)(2,1)}, bf16[1,5,16,32,128]{4,3,2,1,0:T(8,128)(2,1)}, u32[]{:S(2)}, u32[]{:S(2)}) collective-permute-start(bf16[1,5,16,32,128]{4,3,2,1,0:T(8,128)(2,1)} %get-tuple-element.167), channel_id=1, source_target_pairs={{0,4},{1,5},{2,6},{3,7},{4,0},{5,1},{6,2},{7,3},{8,12},{9,13},{10,... | collective-permute-start | bytes 1966088 | tf_op jit(solution)/shard_map/ppermute | solution.py:365
  226.4 27.7 %collective-permute-start.54 = (bf16[1,5,16,32,128]{4,3,2,1,0:T(8,128)(2,1)}, bf16[1,5,16,32,128]{4,3,2,1,0:T(8,128)(2,1)}, u32[]{:S(2)}, u32[]{:S(2)}) collective-permute-start(bf16[1,5,16,32,128]{4,3,2,1,0:T(8,128)(2,1)} %get-tuple-element.168), channel_id=1, source_target_pairs={{0,5},{1,4},{2,7},{3,6},{4,1},{5,0},{6,3},{7,2},{8,13},{9,12},{10,... | collective-permute-start | bytes 1966088 | tf_op jit(solution)/shard_map/ppermute | solution.py:365
  255.3 35.7 %collective-permute-done.53.refs_4_ = bf16[1,5,16,32,128]{4,3,2,1,0:T(8,128)(2,1)} collective-permute-done((bf16[1,5,16,32,128]{4,3,2,1,0:T(8,128)(2,1)}, bf16[1,5,16,32,128]{4,3,2,1,0:T(8,128)(2,1)}, u32[]{:S(2)}, u32[]{:S(2)}) %collective-permute-start.53) | collective-permute-done | bytes 655392 | tf_op jit(solution)/shard_map/ppermute | solution.py:365
  291.0 4.5 collective-permute-start.56
  296.4 7.3 turn_first.8
  303.7 16.3 %collective-permute-done.54.refs_5_ = bf16[1,5,16,32,128]{4,3,2,1,0:T(8,128)(2,1)} collective-permute-done((bf16[1,5,16,32,128]{4,3,2,1,0:T(8,128)(2,1)}, bf16[1,5,16,32,128]{4,3,2,1,0:T(8,128)(2,1)}, u32[]{:S(2)}, u32[]{:S(2)}) %collective-permute-start.54) | collective-permute-done | bytes 655392 | tf_op jit(solution)/shard_map/ppermute | solution.py:365
  320.5 4.2 collective-permute-start.76
  324.7 10.6 %turn_first.6 = (bf16[5,16,256,128]{3,2,1,0:T(8,128)(2,1)}, bf16[5,1,256,128]{3,2,1,0:T(8,128)(2,1)}, bf16[5,1,256,128]{3,2,1,0:T(8,128)(2,1)}) custom-call(bf16[256,256]{1,0:T(8,128)(2,1)} %fusion.5.rotation, bf16[1,5,16,32,128]{4,3,2,1,0:T(8,128)(2,1)} %get-tuple-element.116.refs_0_, bf16[1,5,16,32,128]{4,3,2,1,0:T(8,128)(2,1)} %copy-done.12, ...), custom_call_target="tpu_custom_call" | custom-call | flops 1342177280 | bytes 10485760 | tf_op jit(solution)/shard_map/turn_first/pallas_call | solution.py:193
  335.4 10.5 %turn_first.9 = (bf16[5,16,256,128]{3,2,1,0:T(8,128)(2,1)}, bf16[5,1,256,128]{3,2,1,0:T(8,128)(2,1)}, bf16[5,1,256,128]{3,2,1,0:T(8,128)(2,1)}) custom-call(bf16[256,256]{1,0:T(8,128)(2,1)} %fusion.5.rotation, bf16[1,5,16,32,128]{4,3,2,1,0:T(8,128)(2,1)} %get-tuple-element.163.refs_0_, bf16[1,5,16,32,128]{4,3,2,1,0:T(8,128)(2,1)} %collective-permute-done.50.refs_1_, ...), custom_call_target="tpu_custom_call" | custom-call | flops 1342177280 | bytes 10485760 | tf_op jit(solution)/shard_map/turn_first/pallas_call | solution.py:193
  345.9 4.8 collective-permute-start.58
  350.7 24.3 %collective-permute-start.66 = (bf16[5,1,256,128]{3,2,1,0:T(8,128)(2,1)}, bf16[5,1,256,128]{3,2,1,0:T(8,128)(2,1)}, u32[]{:S(2)}, u32[]{:S(2)}) collective-permute-start(bf16[5,1,256,128]{3,2,1,0:T(8,128)(2,1)} %get-tuple-element.182), channel_id=1, source_target_pairs={{0,1},{1,2},{2,3},{3,4},{4,5},{5,6},{6,7},{7,0},{8,9},{9,10},{10,1... | collective-permute-start | bytes 983048 | tf_op jit(solution)/shard_map/ppermute | solution.py:460
  376.0 6.6 advect_first.5
  385.5 5.9 collective-permute-start.2
  391.3 5.8 collective-permute-done.66.south
  401.3 11.3 %advect_first.7 = (bf16[1,2,16,32,128]{4,3,2,1,0:T(8,128)(2,1)}, bf16[1,2,16,32,128]{4,3,2,1,0:T(8,128)(2,1)}, bf16[1,2,16,32,128]{4,3,2,1,0:T(8,128)(2,1)}, bf1...) custom-call(f32[3,256]{1,0:T(4,128)} %refs_0_.9, ...), custom_call_target="tpu_custom_call" | custom-call | flops 31457280 | bytes 8388608 | tf_op jit(solution)/shard_map/advect_first/pallas_call | solution.py:147
  422.8 24.7 %advect_turn.8 = (bf16[1,5,16,32,128]{4,3,2,1,0:T(8,128)(2,1)}, bf16[1,5,16,32,128]{4,3,2,1,0:T(8,128)(2,1)}, bf16[1,5,16,32,128]{4,3,2,1,0:T(8,128)(2,1)}, bf16...) custom-call(bf16[256,256]{1,0:T(8,128)(2,1)} %convolution_convert_fu, ...), custom_call_target="tpu_custom_call" | custom-call | flops 1342177280 | bytes 20971520 | tf_op jit(solution)/shard_map/advect_turn/pallas_call | solution.py:271
  451.9 3.8 collective-permute-start.20
  455.7 11.3 %collective-permute-done.18.refs_3_ = bf16[1,2,16,32,128]{4,3,2,1,0:T(8,128)(2,1)S(1)} collective-permute-done((bf16[1,2,16,32,128]{4,3,2,1,0:T(8,128)(2,1)S(1)}, bf16[1,2,16,32,128]{4,3,2,1,0:T(8,128)(2,1)S(1)}, u32[]{:S(2)}, u32[]{:S(2)}) %collective-permute-start.18) | collective-permute-done | bytes 262176 | tf_op jit(solution)/shard_map/ppermute | solution.py:365
  470.7 11.0 %collective-permute-done.20.refs_5_ = bf16[1,2,16,32,128]{4,3,2,1,0:T(8,128)(2,1)S(1)} collective-permute-done((bf16[1,2,16,32,128]{4,3,2,1,0:T(8,128)(2,1)S(1)}, bf16[1,2,16,32,128]{4,3,2,1,0:T(8,128)(2,1)S(1)}, u32[]{:S(2)}, u32[]{:S(2)}) %collective-permute-start.20) | collective-permute-done | bytes 262176 | tf_op jit(solution)/shard_map/ppermute | solution.py:365
  481.7 3.5 collective-permute-start.70
  485.2 4.2 collective-permute-done.21.refs_6_
  491.6 4.4 collective-permute-done.22.refs_7_
  496.0 5.3 collective-permute-start.72
  505.4 5.7 turn_first.7
  511.0 16.4 %advect_turn.9 = (bf16[1,3,16,32,128]{4,3,2,1,0:T(8,128)(2,1)}, bf16[1,3,16,32,128]{4,3,2,1,0:T(8,128)(2,1)}, bf16[1,3,16,32,128]{4,3,2,1,0:T(8,128)(2,1)}, bf16...) custom-call(bf16[256,256]{1,0:T(8,128)(2,1)} %convolution_convert_fu, ...), custom_call_target="tpu_custom_call" | custom-call | flops 805306368 | bytes 12582912 | tf_op jit(solution)/shard_map/advect_turn/pallas_call | solution.py:271
  528.9 39.9 %collective-permute-done.71.refs_4_ = bf16[1,5,16,32,128]{4,3,2,1,0:T(8,128)(2,1)S(1)} collective-permute-done((bf16[1,5,16,32,128]{4,3,2,1,0:T(8,128)(2,1)}, bf16[1,5,16,32,128]{4,3,2,1,0:T(8,128)(2,1)S(1)}, u32[]{:S(2)}, u32[]{:S(2)}) %collective-permute-start.71) | collective-permute-done | bytes 655392 | tf_op jit(solution)/shard_map/ppermute | solution.py:365
  568.8 14.2 %collective-permute-done.72.refs_5_ = bf16[1,5,16,32,128]{4,3,2,1,0:T(8,128)(2,1)S(1)} collective-permute-done((bf16[1,5,16,32,128]{4,3,2,1,0:T(8,128)(2,1)}, bf16[1,5,16,32,128]{4,3,2,1,0:T(8,128)(2,1)S(1)}, u32[]{:S(2)}, u32[]{:S(2)}) %collective-permute-start.72) | collective-permute-done | bytes 655392 | tf_op jit(solution)/shard_map/ppermute | solution.py:365
  583.0 19.2 %collective-permute-start.80 = (bf16[1,3,16,32,128]{4,3,2,1,0:T(8,128)(2,1)}, bf16[1,3,16,32,128]{4,3,2,1,0:T(8,128)(2,1)}, u32[]{:S(2)}, u32[]{:S(2)}) collective-permute-start(bf16[1,3,16,32,128]{4,3,2,1,0:T(8,128)(2,1)} %get-tuple-element.198), channel_id=1, source_target_pairs={{0,4},{1,5},{2,6},{3,7},{4,0},{5,1},{6,2},{7,3},{8,12},{9,13},{10,... | collective-permute-start | bytes 1179656 | tf_op jit(solution)/shard_map/ppermute | solution.py:365
  602.1 27.6 %collective-permute-start.81 = (bf16[1,3,16,32,128]{4,3,2,1,0:T(8,128)(2,1)}, bf16[1,3,16,32,128]{4,3,2,1,0:T(8,128)(2,1)}, u32[]{:S(2)}, u32[]{:S(2)}) collective-permute-start(bf16[1,3,16,32,128]{4,3,2,1,0:T(8,128)(2,1)} %get-tuple-element.199), channel_id=1, source_target_pairs={{0,5},{1,4},{2,7},{3,6},{4,1},{5,0},{6,3},{7,2},{8,13},{9,12},{10,... | collective-permute-start | bytes 1179656 | tf_op jit(solution)/shard_map/ppermute | solution.py:365
  629.7 3.9 turn_first.5
  633.7 24.8 %advect_turn.7 = (bf16[1,5,16,32,128]{4,3,2,1,0:T(8,128)(2,1)}, bf16[1,5,16,32,128]{4,3,2,1,0:T(8,128)(2,1)}, bf16[1,5,16,32,128]{4,3,2,1,0:T(8,128)(2,1)}, bf16...) custom-call(bf16[256,256]{1,0:T(8,128)(2,1)} %convolution_convert_fu, ...), custom_call_target="tpu_custom_call" | custom-call | flops 1342177280 | bytes 20971520 | tf_op jit(solution)/shard_map/advect_turn/pallas_call | solution.py:271
  665.5 45.8 %collective-permute-done.83.refs_7_ = bf16[1,3,16,32,128]{4,3,2,1,0:T(8,128)(2,1)S(1)} collective-permute-done((bf16[1,3,16,32,128]{4,3,2,1,0:T(8,128)(2,1)}, bf16[1,3,16,32,128]{4,3,2,1,0:T(8,128)(2,1)S(1)}, u32[]{:S(2)}, u32[]{:S(2)}) %collective-permute-start.83) | collective-permute-done | bytes 393248 | tf_op jit(solution)/shard_map/ppermute | solution.py:365
  711.3 19.0 %collective-permute-start.63 = (bf16[1,5,16,32,128]{4,3,2,1,0:T(8,128)(2,1)}, bf16[1,5,16,32,128]{4,3,2,1,0:T(8,128)(2,1)}, u32[]{:S(2)}, u32[]{:S(2)}) collective-permute-start(bf16[1,5,16,32,128]{4,3,2,1,0:T(8,128)(2,1)} %get-tuple-element.179), channel_id=1, source_target_pairs={{0,5},{1,4},{2,7},{3,6},{4,1},{5,0},{6,3},{7,2},{8,13},{9,12},{10,... | collective-permute-start | bytes 1966088 | tf_op jit(solution)/shard_map/ppermute | solution.py:365
  739.0 8.7 gather_last.5
  747.7 12.9 %gather_last.6 = (bf16[32,16,128,128]{3,2,1,0:T(8,128)(2,1)}, f32[8,6,5,16,128]{4,3,2,1,0:T(8,128)}) custom-call(f32[6,32]{1,0:T(8,128)} %dynamic-slice_multiply_fusion.coef, s32[1]{0:T(128)} %bitcast.refs_1_.place, bf16[1,5,16,32,128]{4,3,2,1,0:T(8,128)(2,1)} %get-tuple-element.184.refs_0_, ...), custom_call_target="tpu_custom_call", output_to_operand_aliasing={{0}: (11, {})} | custom-call | flops 36700160 | bytes 15728640 | tf_op jit(solution)/shard_map/gather_last/pallas_call | solution.py:341
  761.5 7.1 collective-permute-done.63.refs_5_
  768.8 12.8 %gather_last.7 = (bf16[32,16,128,128]{3,2,1,0:T(8,128)(2,1)}, f32[8,6,5,16,128]{4,3,2,1,0:T(8,128)}) custom-call(f32[6,32]{1,0:T(8,128)} %dynamic-slice_multiply_fusion.coef, s32[1]{0:T(128)} %bitcast.refs_1_.place, bf16[1,5,16,32,128]{4,3,2,1,0:T(8,128)(2,1)} %get-tuple-element.174.refs_0_, ...), custom_call_target="tpu_custom_call", output_to_operand_aliasing={{0}: (11, {})} | custom-call | flops 36700160 | bytes 15728640 | tf_op jit(solution)/shard_map/gather_last/pallas_call | solution.py:341
  785.6 4.7 collective-permute-start.42
  790.3 5.3 collective-permute-done.42.north
  795.5 15.9 %collective-permute-start.24 = (bf16[1,1,256,128]{3,2,1,0:T(8,128)(2,1)}, bf16[1,1,256,128]{3,2,1,0:T(8,128)(2,1)S(1)}, u32[]{:S(2)}, u32[]{:S(2)}) collective-permute-start(bf16[1,1,256,128]{3,2,1,0:T(8,128)(2,1)} %get-tuple-element.134), channel_id=1, source_target_pairs={{0,1},{1,2},{2,3},{3,4},{4,5},{5,6},{6,7},{7,0},{8,9},{9,10},{10,1... | collective-permute-start | bytes 196616 | tf_op jit(solution)/shard_map/ppermute | solution.py:460
  811.5 12.5 %advect_turn.6 = (bf16[1,2,16,32,128]{4,3,2,1,0:T(8,128)(2,1)}, bf16[1,2,16,32,128]{4,3,2,1,0:T(8,128)(2,1)}, bf16[1,2,16,32,128]{4,3,2,1,0:T(8,128)(2,1)}, bf16...) custom-call(bf16[256,256]{1,0:T(8,128)(2,1)} %convolution_convert_fu, ...), custom_call_target="tpu_custom_call" | custom-call | flops 536870912 | bytes 8388608 | tf_op jit(solution)/shard_map/advect_turn/pallas_call | solution.py:271
  824.0 8.9 collective-permute-start.43
  843.7 7.7 advect_turn.5
  854.2 4.2 collective-permute-done.45.refs_3_
  858.5 7.2 collective-permute-start.26
  869.6 6.3 collective-permute-start.29
  891.0 6.1 gather_last.8
  897.6 4.4 gather_last.9
  901.9 4.0 all-to-all-start.1
  911.8 4.3 all-to-all-done.1
  916.0 3.5 all-to-all-start
  926.9 3.3 all-to-all-done
  930.3 5.8 collective-permute-done.88
  939.2 6.2 collective-permute-done.89
  (361 shorter events, 138.4 us)
Async XLA Ops:
  15.0 31.2 %collective-permute-start.34 = (bf16[1,3,16,32,128]{4,3,2,1,0:T(8,128)(2,1)}, bf16[1,3,16,32,128]{4,3,2,1,0:T(8,128)(2,1)S(1)}, u32[]{:S(2)}, u32[]{:S(2)}) collective-permute-start(bf16[1,3,16,32,128]{4,3,2,1,0:T(8,128)(2,1)} %get-tuple-element.145), channel_id=1, source_target_pairs={{0,1},{1,0},{2,3},{3,2},{4,5},{5,4},{6,7},{7,6},{8,9},{9,8},{10,11... | collective-permute-start | bytes 1179656 | tf_op jit(solution)/shard_map/ppermute | solution.py:365
  19.6 30.4 %collective-permute-start.36 = (bf16[1,3,16,32,128]{4,3,2,1,0:T(8,128)(2,1)}, bf16[1,3,16,32,128]{4,3,2,1,0:T(8,128)(2,1)S(1)}, u32[]{:S(2)}, u32[]{:S(2)}) collective-permute-start(bf16[1,3,16,32,128]{4,3,2,1,0:T(8,128)(2,1)} %get-tuple-element.147), channel_id=1, source_target_pairs={{0,3},{1,2},{2,1},{3,0},{4,7},{5,6},{6,5},{7,4},{8,11},{9,10},{10,... | collective-permute-start | bytes 1179656 | tf_op jit(solution)/shard_map/ppermute | solution.py:365
  41.6 83.5 %collective-permute-start.8 = (bf16[1,5,16,32,128]{4,3,2,1,0:T(8,128)(2,1)}, bf16[1,5,16,32,128]{4,3,2,1,0:T(8,128)(2,1)S(1)}, u32[]{:S(2)}, u32[]{:S(2)}) collective-permute-start(bf16[1,5,16,32,128]{4,3,2,1,0:T(8,128)(2,1)} %get-tuple-element.117), channel_id=1, source_target_pairs={{0,1},{1,0},{2,3},{3,2},{4,5},{5,4},{6,7},{7,6},{8,9},{9,8},{10,11... | collective-permute-start | bytes 1966088 | tf_op jit(solution)/shard_map/ppermute | solution.py:365
  43.6 45.7 %collective-permute-start.37 = (bf16[1,3,16,32,128]{4,3,2,1,0:T(8,128)(2,1)}, bf16[1,3,16,32,128]{4,3,2,1,0:T(8,128)(2,1)S(1)}, u32[]{:S(2)}, u32[]{:S(2)}) collective-permute-start(bf16[1,3,16,32,128]{4,3,2,1,0:T(8,128)(2,1)} %get-tuple-element.148), channel_id=1, source_target_pairs={{0,4},{1,5},{2,6},{3,7},{4,0},{5,1},{6,2},{7,3},{8,12},{9,13},{10,... | collective-permute-start | bytes 1179656 | tf_op jit(solution)/shard_map/ppermute | solution.py:365
  46.1 51.5 %collective-permute-start.38 = (bf16[1,3,16,32,128]{4,3,2,1,0:T(8,128)(2,1)}, bf16[1,3,16,32,128]{4,3,2,1,0:T(8,128)(2,1)S(1)}, u32[]{:S(2)}, u32[]{:S(2)}) collective-permute-start(bf16[1,3,16,32,128]{4,3,2,1,0:T(8,128)(2,1)} %get-tuple-element.149), channel_id=1, source_target_pairs={{0,5},{1,4},{2,7},{3,6},{4,1},{5,0},{6,3},{7,2},{8,13},{9,12},{10,... | collective-permute-start | bytes 1179656 | tf_op jit(solution)/shard_map/ppermute | solution.py:365
  46.2 51.5 %collective-permute-start.39 = (bf16[1,3,16,32,128]{4,3,2,1,0:T(8,128)(2,1)}, bf16[1,3,16,32,128]{4,3,2,1,0:T(8,128)(2,1)S(1)}, u32[]{:S(2)}, u32[]{:S(2)}) collective-permute-start(bf16[1,3,16,32,128]{4,3,2,1,0:T(8,128)(2,1)} %get-tuple-element.150), channel_id=1, source_target_pairs={{0,6},{1,7},{2,4},{3,5},{4,2},{5,3},{6,0},{7,1},{8,14},{9,15},{10,... | collective-permute-start | bytes 1179656 | tf_op jit(solution)/shard_map/ppermute | solution.py:365
  50.0 57.6 %collective-permute-start.40 = (bf16[1,3,16,32,128]{4,3,2,1,0:T(8,128)(2,1)}, bf16[1,3,16,32,128]{4,3,2,1,0:T(8,128)(2,1)S(1)}, u32[]{:S(2)}, u32[]{:S(2)}) collective-permute-start(bf16[1,3,16,32,128]{4,3,2,1,0:T(8,128)(2,1)} %get-tuple-element.151), channel_id=1, source_target_pairs={{0,7},{1,6},{2,5},{3,4},{4,3},{5,2},{6,1},{7,0},{8,15},{9,14},{10,... | collective-permute-start | bytes 1179656 | tf_op jit(solution)/shard_map/ppermute | solution.py:365
  89.2 63.8 %collective-permute-start.9 = (bf16[1,5,16,32,128]{4,3,2,1,0:T(8,128)(2,1)}, bf16[1,5,16,32,128]{4,3,2,1,0:T(8,128)(2,1)S(1)}, u32[]{:S(2)}, u32[]{:S(2)}) collective-permute-start(bf16[1,5,16,32,128]{4,3,2,1,0:T(8,128)(2,1)} %get-tuple-element.118), channel_id=1, source_target_pairs={{0,2},{1,3},{2,0},{3,1},{4,6},{5,7},{6,4},{7,5},{8,10},{9,11},{10,... | collective-permute-start | bytes 1966088 | tf_op jit(solution)/shard_map/ppermute | solution.py:365
  97.6 58.4 %collective-permute-start.10 = (bf16[1,5,16,32,128]{4,3,2,1,0:T(8,128)(2,1)}, bf16[1,5,16,32,128]{4,3,2,1,0:T(8,128)(2,1)S(1)}, u32[]{:S(2)}, u32[]{:S(2)}) collective-permute-start(bf16[1,5,16,32,128]{4,3,2,1,0:T(8,128)(2,1)} %get-tuple-element.119), channel_id=1, source_target_pairs={{0,3},{1,2},{2,1},{3,0},{4,7},{5,6},{6,5},{7,4},{8,11},{9,10},{10,... | collective-permute-start | bytes 1966088 | tf_op jit(solution)/shard_map/ppermute | solution.py:365
  97.7 92.3 %collective-permute-start.11 = (bf16[1,5,16,32,128]{4,3,2,1,0:T(8,128)(2,1)}, bf16[1,5,16,32,128]{4,3,2,1,0:T(8,128)(2,1)}, u32[]{:S(2)}, u32[]{:S(2)}) collective-permute-start(bf16[1,5,16,32,128]{4,3,2,1,0:T(8,128)(2,1)} %get-tuple-element.120), channel_id=1, source_target_pairs={{0,4},{1,5},{2,6},{3,7},{4,0},{5,1},{6,2},{7,3},{8,12},{9,13},{10,... | collective-permute-start | bytes 1966088 | tf_op jit(solution)/shard_map/ppermute | solution.py:365
  107.7 96.2 %collective-permute-start.12 = (bf16[1,5,16,32,128]{4,3,2,1,0:T(8,128)(2,1)}, bf16[1,5,16,32,128]{4,3,2,1,0:T(8,128)(2,1)}, u32[]{:S(2)}, u32[]{:S(2)}) collective-permute-start(bf16[1,5,16,32,128]{4,3,2,1,0:T(8,128)(2,1)} %get-tuple-element.121), channel_id=1, source_target_pairs={{0,5},{1,4},{2,7},{3,6},{4,1},{5,0},{6,3},{7,2},{8,13},{9,12},{10,... | collective-permute-start | bytes 1966088 | tf_op jit(solution)/shard_map/ppermute | solution.py:365
  125.0 80.6 %collective-permute-start.13 = (bf16[1,5,16,32,128]{4,3,2,1,0:T(8,128)(2,1)}, bf16[1,5,16,32,128]{4,3,2,1,0:T(8,128)(2,1)}, u32[]{:S(2)}, u32[]{:S(2)}) collective-permute-start(bf16[1,5,16,32,128]{4,3,2,1,0:T(8,128)(2,1)} %get-tuple-element.122), channel_id=1, source_target_pairs={{0,6},{1,7},{2,4},{3,5},{4,2},{5,3},{6,0},{7,1},{8,14},{9,15},{10,... | collective-permute-start | bytes 1966088 | tf_op jit(solution)/shard_map/ppermute | solution.py:365
  153.0 71.8 %collective-permute-start.14 = (bf16[1,5,16,32,128]{4,3,2,1,0:T(8,128)(2,1)S(1)}, bf16[1,5,16,32,128]{4,3,2,1,0:T(8,128)(2,1)S(1)}, u32[]{:S(2)}, u32[]{:S(2)}) collective-permute-start(bf16[1,5,16,32,128]{4,3,2,1,0:T(8,128)(2,1)S(1)} %copy-done.67), channel_id=1, source_target_pairs={{0,7},{1,6},{2,5},{3,4},{4,3},{5,2},{6,1},{7,0},{8,15},{9,14},{10,... | collective-permute-start | bytes 1966088 | tf_op jit(solution)/shard_map/ppermute | solution.py:365
  156.0 70.4 %collective-permute-start.50 = (bf16[1,5,16,32,128]{4,3,2,1,0:T(8,128)(2,1)S(1)}, bf16[1,5,16,32,128]{4,3,2,1,0:T(8,128)(2,1)}, u32[]{:S(2)}, u32[]{:S(2)}) collective-permute-start(bf16[1,5,16,32,128]{4,3,2,1,0:T(8,128)(2,1)S(1)} %copy-done.69), channel_id=1, source_target_pairs={{0,1},{1,0},{2,3},{3,2},{4,5},{5,4},{6,7},{7,6},{8,9},{9,8},{10,11... | collective-permute-start | bytes 1966088 | tf_op jit(solution)/shard_map/ppermute | solution.py:365
  190.0 64.0 %collective-permute-start.51 = (bf16[1,5,16,32,128]{4,3,2,1,0:T(8,128)(2,1)S(1)}, bf16[1,5,16,32,128]{4,3,2,1,0:T(8,128)(2,1)}, u32[]{:S(2)}, u32[]{:S(2)}) collective-permute-start(bf16[1,5,16,32,128]{4,3,2,1,0:T(8,128)(2,1)S(1)} %copy-done.68), channel_id=1, source_target_pairs={{0,2},{1,3},{2,0},{3,1},{4,6},{5,7},{6,4},{7,5},{8,10},{9,11},{10,... | collective-permute-start | bytes 1966088 | tf_op jit(solution)/shard_map/ppermute | solution.py:365
  203.9 51.2 %collective-permute-start.52 = (bf16[1,5,16,32,128]{4,3,2,1,0:T(8,128)(2,1)}, bf16[1,5,16,32,128]{4,3,2,1,0:T(8,128)(2,1)}, u32[]{:S(2)}, u32[]{:S(2)}) collective-permute-start(bf16[1,5,16,32,128]{4,3,2,1,0:T(8,128)(2,1)} %get-tuple-element.166), channel_id=1, source_target_pairs={{0,3},{1,2},{2,1},{3,0},{4,7},{5,6},{6,5},{7,4},{8,11},{9,10},{10,... | collective-permute-start | bytes 1966088 | tf_op jit(solution)/shard_map/ppermute | solution.py:365
  205.7 85.3 %collective-permute-start.53 = (bf16[1,5,16,32,128]{4,3,2,1,0:T(8,128)(2,1)}, bf16[1,5,16,32,128]{4,3,2,1,0:T(8,128)(2,1)}, u32[]{:S(2)}, u32[]{:S(2)}) collective-permute-start(bf16[1,5,16,32,128]{4,3,2,1,0:T(8,128)(2,1)} %get-tuple-element.167), channel_id=1, source_target_pairs={{0,4},{1,5},{2,6},{3,7},{4,0},{5,1},{6,2},{7,3},{8,12},{9,13},{10,... | collective-permute-start | bytes 1966088 | tf_op jit(solution)/shard_map/ppermute | solution.py:365
  225.6 149.3 %collective-permute-start = (bf16[32,1,128,128]{3,2,1,0:T(8,128)(2,1)}, bf16[32,1,128,128]{3,2,1,0:T(8,128)(2,1)S(1)}, u32[]{:S(2)}, u32[]{:S(2)}) collective-permute-start(bf16[32,1,128,128]{3,2,1,0:T(8,128)(2,1)} %get-tuple-element.221), channel_id=1, source_target_pairs={{0,24},{8,0},{16,8},{24,16},{1,25},{9,1},{17,9},{25,17},{2,26},{10... | collective-permute-start | bytes 3145736 | tf_op jit(solution)/shard_map/ppermute | solution.py:415
  226.4 93.6 %collective-permute-start.54 = (bf16[1,5,16,32,128]{4,3,2,1,0:T(8,128)(2,1)}, bf16[1,5,16,32,128]{4,3,2,1,0:T(8,128)(2,1)}, u32[]{:S(2)}, u32[]{:S(2)}) collective-permute-start(bf16[1,5,16,32,128]{4,3,2,1,0:T(8,128)(2,1)} %get-tuple-element.168), channel_id=1, source_target_pairs={{0,5},{1,4},{2,7},{3,6},{4,1},{5,0},{6,3},{7,2},{8,13},{9,12},{10,... | collective-permute-start | bytes 1966088 | tf_op jit(solution)/shard_map/ppermute | solution.py:365
  254.0 66.5 %collective-permute-start.55 = (bf16[1,5,16,32,128]{4,3,2,1,0:T(8,128)(2,1)}, bf16[1,5,16,32,128]{4,3,2,1,0:T(8,128)(2,1)}, u32[]{:S(2)}, u32[]{:S(2)}) collective-permute-start(bf16[1,5,16,32,128]{4,3,2,1,0:T(8,128)(2,1)} %get-tuple-element.169), channel_id=1, source_target_pairs={{0,6},{1,7},{2,4},{3,5},{4,2},{5,3},{6,0},{7,1},{8,14},{9,15},{10,... | collective-permute-start | bytes 1966088 | tf_op jit(solution)/shard_map/ppermute | solution.py:365
  255.2 145.1 %collective-permute-start.15 = (bf16[32,1,128,128]{3,2,1,0:T(8,128)(2,1)S(1)}, bf16[32,1,128,128]{3,2,1,0:T(8,128)(2,1)S(1)}, u32[]{:S(2)}, u32[]{:S(2)}) collective-permute-start(bf16[32,1,128,128]{3,2,1,0:T(8,128)(2,1)S(1)} %get-tuple-element.220), channel_id=1, source_target_pairs={{0,8},{8,16},{16,24},{24,0},{1,9},{9,17},{17,25},{25,1},{2,10},{10... | collective-permute-start | bytes 3145736 | tf_op jit(solution)/shard_map/ppermute | solution.py:414
  291.0 44.3 %collective-permute-start.56 = (bf16[1,5,16,32,128]{4,3,2,1,0:T(8,128)(2,1)}, bf16[1,5,16,32,128]{4,3,2,1,0:T(8,128)(2,1)}, u32[]{:S(2)}, u32[]{:S(2)}) collective-permute-start(bf16[1,5,16,32,128]{4,3,2,1,0:T(8,128)(2,1)} %get-tuple-element.170), channel_id=1, source_target_pairs={{0,7},{1,6},{2,5},{3,4},{4,3},{5,2},{6,1},{7,0},{8,15},{9,14},{10,... | collective-permute-start | bytes 1966088 | tf_op jit(solution)/shard_map/ppermute | solution.py:365
  320.5 30.1 %collective-permute-start.76 = (bf16[3,1,256,128]{3,2,1,0:T(8,128)(2,1)}, bf16[3,1,256,128]{3,2,1,0:T(8,128)(2,1)}, u32[]{:S(2)}, u32[]{:S(2)}) collective-permute-start(bf16[3,1,256,128]{3,2,1,0:T(8,128)(2,1)} %get-tuple-element.193), channel_id=1, source_target_pairs={{0,7},{1,0},{2,1},{3,2},{4,3},{5,4},{6,5},{7,6},{8,15},{9,8},{10,9... | collective-permute-start | bytes 589832 | tf_op jit(solution)/shard_map/ppermute | solution.py:461
  335.3 47.2 %collective-permute-start.57 = (bf16[5,1,256,128]{3,2,1,0:T(8,128)(2,1)}, bf16[5,1,256,128]{3,2,1,0:T(8,128)(2,1)}, u32[]{:S(2)}, u32[]{:S(2)}) collective-permute-start(bf16[5,1,256,128]{3,2,1,0:T(8,128)(2,1)} %get-tuple-element.172), channel_id=1, source_target_pairs={{0,1},{1,2},{2,3},{3,4},{4,5},{5,6},{6,7},{7,0},{8,9},{9,10},{10,1... | collective-permute-start | bytes 983048 | tf_op jit(solution)/shard_map/ppermute | solution.py:460
  345.9 39.5 %collective-permute-start.58 = (bf16[5,1,256,128]{3,2,1,0:T(8,128)(2,1)}, bf16[5,1,256,128]{3,2,1,0:T(8,128)(2,1)}, u32[]{:S(2)}, u32[]{:S(2)}) collective-permute-start(bf16[5,1,256,128]{3,2,1,0:T(8,128)(2,1)} %get-tuple-element.173), channel_id=1, source_target_pairs={{0,7},{1,0},{2,1},{3,2},{4,3},{5,4},{6,5},{7,6},{8,15},{9,8},{10,9... | collective-permute-start | bytes 983048 | tf_op jit(solution)/shard_map/ppermute | solution.py:461
  350.7 46.4 %collective-permute-start.66 = (bf16[5,1,256,128]{3,2,1,0:T(8,128)(2,1)}, bf16[5,1,256,128]{3,2,1,0:T(8,128)(2,1)}, u32[]{:S(2)}, u32[]{:S(2)}) collective-permute-start(bf16[5,1,256,128]{3,2,1,0:T(8,128)(2,1)} %get-tuple-element.182), channel_id=1, source_target_pairs={{0,1},{1,2},{2,3},{3,4},{4,5},{5,6},{6,7},{7,0},{8,9},{9,10},{10,1... | collective-permute-start | bytes 983048 | tf_op jit(solution)/shard_map/ppermute | solution.py:460
  375.0 37.6 %collective-permute-start.67 = (bf16[5,1,256,128]{3,2,1,0:T(8,128)(2,1)}, bf16[5,1,256,128]{3,2,1,0:T(8,128)(2,1)}, u32[]{:S(2)}, u32[]{:S(2)}) collective-permute-start(bf16[5,1,256,128]{3,2,1,0:T(8,128)(2,1)} %get-tuple-element.183), channel_id=1, source_target_pairs={{0,7},{1,0},{2,1},{3,2},{4,3},{5,4},{6,5},{7,6},{8,15},{9,8},{10,9... | collective-permute-start | bytes 983048 | tf_op jit(solution)/shard_map/ppermute | solution.py:461
  382.5 30.8 %collective-permute-start.1 = (bf16[1,1,16,32,128]{4,3,2,1,0:T(8,128)(2,1)}, bf16[1,1,16,32,128]{4,3,2,1,0:T(8,128)(2,1)S(1)}, u32[]{:S(2)}, u32[]{:S(2)}) collective-permute-start(bf16[1,1,16,32,128]{4,3,2,1,0:T(8,128)(2,1)} %get-tuple-element.108), channel_id=1, source_target_pairs={{0,1},{1,0},{2,3},{3,2},{4,5},{5,4},{6,7},{7,6},{8,9},{9,8},{10,11... | collective-permute-start | bytes 393224 | tf_op jit(solution)/shard_map/ppermute | solution.py:365
  385.5 31.6 %collective-permute-start.2 = (bf16[1,1,16,32,128]{4,3,2,1,0:T(8,128)(2,1)}, bf16[1,1,16,32,128]{4,3,2,1,0:T(8,128)(2,1)S(1)}, u32[]{:S(2)}, u32[]{:S(2)}) collective-permute-start(bf16[1,1,16,32,128]{4,3,2,1,0:T(8,128)(2,1)} %get-tuple-element.109), channel_id=1, source_target_pairs={{0,2},{1,3},{2,0},{3,1},{4,6},{5,7},{6,4},{7,5},{8,10},{9,11},{10,... | collective-permute-start | bytes 393224 | tf_op jit(solution)/shard_map/ppermute | solution.py:365
  412.6 39.2 %collective-permute-start.16 = (bf16[1,2,16,32,128]{4,3,2,1,0:T(8,128)(2,1)}, bf16[1,2,16,32,128]{4,3,2,1,0:T(8,128)(2,1)S(1)}, u32[]{:S(2)}, u32[]{:S(2)}) collective-permute-start(bf16[1,2,16,32,128]{4,3,2,1,0:T(8,128)(2,1)} %get-tuple-element.126), channel_id=1, source_target_pairs={{0,1},{1,0},{2,3},{3,2},{4,5},{5,4},{6,7},{7,6},{8,9},{9,8},{10,11... | collective-permute-start | bytes 786440 | tf_op jit(solution)/shard_map/ppermute | solution.py:365
  413.4 34.2 %collective-permute-start.5 = (bf16[1,1,16,32,128]{4,3,2,1,0:T(8,128)(2,1)S(1)}, bf16[1,1,16,32,128]{4,3,2,1,0:T(8,128)(2,1)S(1)}, u32[]{:S(2)}, u32[]{:S(2)}) collective-permute-start(bf16[1,1,16,32,128]{4,3,2,1,0:T(8,128)(2,1)S(1)} %copy-done.80), channel_id=1, source_target_pairs={{0,5},{1,4},{2,7},{3,6},{4,1},{5,0},{6,3},{7,2},{8,13},{9,12},{10,... | collective-permute-start | bytes 393224 | tf_op jit(solution)/shard_map/ppermute | solution.py:365
  417.1 34.7 %collective-permute-start.17 = (bf16[1,2,16,32,128]{4,3,2,1,0:T(8,128)(2,1)}, bf16[1,2,16,32,128]{4,3,2,1,0:T(8,128)(2,1)S(1)}, u32[]{:S(2)}, u32[]{:S(2)}) collective-permute-start(bf16[1,2,16,32,128]{4,3,2,1,0:T(8,128)(2,1)} %get-tuple-element.127), channel_id=1, source_target_pairs={{0,2},{1,3},{2,0},{3,1},{4,6},{5,7},{6,4},{7,5},{8,10},{9,11},{10,... | collective-permute-start | bytes 786440 | tf_op jit(solution)/shard_map/ppermute | solution.py:365
  418.1 31.5 %collective-permute-start.6 = (bf16[1,1,16,32,128]{4,3,2,1,0:T(8,128)(2,1)S(1)}, bf16[1,1,16,32,128]{4,3,2,1,0:T(8,128)(2,1)S(1)}, u32[]{:S(2)}, u32[]{:S(2)}) collective-permute-start(bf16[1,1,16,32,128]{4,3,2,1,0:T(8,128)(2,1)S(1)} %copy-done.79), channel_id=1, source_target_pairs={{0,6},{1,7},{2,4},{3,5},{4,2},{5,3},{6,0},{7,1},{8,14},{9,15},{10,... | collective-permute-start | bytes 393224 | tf_op jit(solution)/shard_map/ppermute | solution.py:365
  419.7 30.0 %collective-permute-start.7 = (bf16[1,1,16,32,128]{4,3,2,1,0:T(8,128)(2,1)S(1)}, bf16[1,1,16,32,128]{4,3,2,1,0:T(8,128)(2,1)S(1)}, u32[]{:S(2)}, u32[]{:S(2)}) collective-permute-start(bf16[1,1,16,32,128]{4,3,2,1,0:T(8,128)(2,1)S(1)} %copy-done.78), channel_id=1, source_target_pairs={{0,7},{1,6},{2,5},{3,4},{4,3},{5,2},{6,1},{7,0},{8,15},{9,14},{10,... | collective-permute-start | bytes 393224 | tf_op jit(solution)/shard_map/ppermute | solution.py:365
  447.5 53.8 %collective-permute-start.68 = (bf16[1,5,16,32,128]{4,3,2,1,0:T(8,128)(2,1)}, bf16[1,5,16,32,128]{4,3,2,1,0:T(8,128)(2,1)}, u32[]{:S(2)}, u32[]{:S(2)}) collective-permute-start(bf16[1,5,16,32,128]{4,3,2,1,0:T(8,128)(2,1)} %get-tuple-element.185), channel_id=1, source_target_pairs={{0,1},{1,0},{2,3},{3,2},{4,5},{5,4},{6,7},{7,6},{8,9},{9,8},{10,11... | collective-permute-start | bytes 1966088 | tf_op jit(solution)/shard_map/ppermute | solution.py:365
  451.8 51.4 %collective-permute-start.69 = (bf16[1,5,16,32,128]{4,3,2,1,0:T(8,128)(2,1)}, bf16[1,5,16,32,128]{4,3,2,1,0:T(8,128)(2,1)}, u32[]{:S(2)}, u32[]{:S(2)}) collective-permute-start(bf16[1,5,16,32,128]{4,3,2,1,0:T(8,128)(2,1)} %get-tuple-element.186), channel_id=1, source_target_pairs={{0,2},{1,3},{2,0},{3,1},{4,6},{5,7},{6,4},{7,5},{8,10},{9,11},{10,... | collective-permute-start | bytes 1966088 | tf_op jit(solution)/shard_map/ppermute | solution.py:365
  451.9 29.8 %collective-permute-start.20 = (bf16[1,2,16,32,128]{4,3,2,1,0:T(8,128)(2,1)S(1)}, bf16[1,2,16,32,128]{4,3,2,1,0:T(8,128)(2,1)S(1)}, u32[]{:S(2)}, u32[]{:S(2)}) collective-permute-start(bf16[1,2,16,32,128]{4,3,2,1,0:T(8,128)(2,1)S(1)} %copy-done.72), channel_id=1, source_target_pairs={{0,5},{1,4},{2,7},{3,6},{4,1},{5,0},{6,3},{7,2},{8,13},{9,12},{10,... | collective-permute-start | bytes 786440 | tf_op jit(solution)/shard_map/ppermute | solution.py:365
  481.7 45.8 %collective-permute-start.70 = (bf16[1,5,16,32,128]{4,3,2,1,0:T(8,128)(2,1)}, bf16[1,5,16,32,128]{4,3,2,1,0:T(8,128)(2,1)S(1)}, u32[]{:S(2)}, u32[]{:S(2)}) collective-permute-start(bf16[1,5,16,32,128]{4,3,2,1,0:T(8,128)(2,1)} %get-tuple-element.187), channel_id=1, source_target_pairs={{0,3},{1,2},{2,1},{3,0},{4,7},{5,6},{6,5},{7,4},{8,11},{9,10},{10,... | collective-permute-start | bytes 1966088 | tf_op jit(solution)/shard_map/ppermute | solution.py:365
  489.4 79.3 %collective-permute-start.71 = (bf16[1,5,16,32,128]{4,3,2,1,0:T(8,128)(2,1)}, bf16[1,5,16,32,128]{4,3,2,1,0:T(8,128)(2,1)S(1)}, u32[]{:S(2)}, u32[]{:S(2)}) collective-permute-start(bf16[1,5,16,32,128]{4,3,2,1,0:T(8,128)(2,1)} %get-tuple-element.188), channel_id=1, source_target_pairs={{0,4},{1,5},{2,6},{3,7},{4,0},{5,1},{6,2},{7,3},{8,12},{9,13},{10,... | collective-permute-start | bytes 1966088 | tf_op jit(solution)/shard_map/ppermute | solution.py:365
  496.0 86.9 %collective-permute-start.72 = (bf16[1,5,16,32,128]{4,3,2,1,0:T(8,128)(2,1)}, bf16[1,5,16,32,128]{4,3,2,1,0:T(8,128)(2,1)S(1)}, u32[]{:S(2)}, u32[]{:S(2)}) collective-permute-start(bf16[1,5,16,32,128]{4,3,2,1,0:T(8,128)(2,1)} %get-tuple-element.189), channel_id=1, source_target_pairs={{0,5},{1,4},{2,7},{3,6},{4,1},{5,0},{6,3},{7,2},{8,13},{9,12},{10,... | collective-permute-start | bytes 1966088 | tf_op jit(solution)/shard_map/ppermute | solution.py:365
  501.3 81.6 %collective-permute-start.73 = (bf16[1,5,16,32,128]{4,3,2,1,0:T(8,128)(2,1)}, bf16[1,5,16,32,128]{4,3,2,1,0:T(8,128)(2,1)S(1)}, u32[]{:S(2)}, u32[]{:S(2)}) collective-permute-start(bf16[1,5,16,32,128]{4,3,2,1,0:T(8,128)(2,1)} %get-tuple-element.190), channel_id=1, source_target_pairs={{0,6},{1,7},{2,4},{3,5},{4,2},{5,3},{6,0},{7,1},{8,14},{9,15},{10,... | collective-permute-start | bytes 1966088 | tf_op jit(solution)/shard_map/ppermute | solution.py:365
  503.3 98.9 %collective-permute-start.74 = (bf16[1,5,16,32,128]{4,3,2,1,0:T(8,128)(2,1)}, bf16[1,5,16,32,128]{4,3,2,1,0:T(8,128)(2,1)S(1)}, u32[]{:S(2)}, u32[]{:S(2)}) collective-permute-start(bf16[1,5,16,32,128]{4,3,2,1,0:T(8,128)(2,1)} %get-tuple-element.191), channel_id=1, source_target_pairs={{0,7},{1,6},{2,5},{3,4},{4,3},{5,2},{6,1},{7,0},{8,15},{9,14},{10,... | collective-permute-start | bytes 1966088 | tf_op jit(solution)/shard_map/ppermute | solution.py:365
  527.5 102.2 %collective-permute-start.77 = (bf16[1,3,16,32,128]{4,3,2,1,0:T(8,128)(2,1)}, bf16[1,3,16,32,128]{4,3,2,1,0:T(8,128)(2,1)}, u32[]{:S(2)}, u32[]{:S(2)}) collective-permute-start(bf16[1,3,16,32,128]{4,3,2,1,0:T(8,128)(2,1)} %get-tuple-element.195), channel_id=1, source_target_pairs={{0,1},{1,0},{2,3},{3,2},{4,5},{5,4},{6,7},{7,6},{8,9},{9,8},{10,11... | collective-permute-start | bytes 1179656 | tf_op jit(solution)/shard_map/ppermute | solution.py:365
  568.8 89.7 %collective-permute-start.78 = (bf16[1,3,16,32,128]{4,3,2,1,0:T(8,128)(2,1)}, bf16[1,3,16,32,128]{4,3,2,1,0:T(8,128)(2,1)}, u32[]{:S(2)}, u32[]{:S(2)}) collective-permute-start(bf16[1,3,16,32,128]{4,3,2,1,0:T(8,128)(2,1)} %get-tuple-element.196), channel_id=1, source_target_pairs={{0,2},{1,3},{2,0},{3,1},{4,6},{5,7},{6,4},{7,5},{8,10},{9,11},{10,... | collective-permute-start | bytes 1179656 | tf_op jit(solution)/shard_map/ppermute | solution.py:365
  582.9 76.6 %collective-permute-start.79 = (bf16[1,3,16,32,128]{4,3,2,1,0:T(8,128)(2,1)}, bf16[1,3,16,32,128]{4,3,2,1,0:T(8,128)(2,1)}, u32[]{:S(2)}, u32[]{:S(2)}) collective-permute-start(bf16[1,3,16,32,128]{4,3,2,1,0:T(8,128)(2,1)} %get-tuple-element.197), channel_id=1, source_target_pairs={{0,3},{1,2},{2,1},{3,0},{4,7},{5,6},{6,5},{7,4},{8,11},{9,10},{10,... | collective-permute-start | bytes 1179656 | tf_op jit(solution)/shard_map/ppermute | solution.py:365
  583.0 76.8 %collective-permute-start.80 = (bf16[1,3,16,32,128]{4,3,2,1,0:T(8,128)(2,1)}, bf16[1,3,16,32,128]{4,3,2,1,0:T(8,128)(2,1)}, u32[]{:S(2)}, u32[]{:S(2)}) collective-permute-start(bf16[1,3,16,32,128]{4,3,2,1,0:T(8,128)(2,1)} %get-tuple-element.198), channel_id=1, source_target_pairs={{0,4},{1,5},{2,6},{3,7},{4,0},{5,1},{6,2},{7,3},{8,12},{9,13},{10,... | collective-permute-start | bytes 1179656 | tf_op jit(solution)/shard_map/ppermute | solution.py:365
  602.1 59.9 %collective-permute-start.81 = (bf16[1,3,16,32,128]{4,3,2,1,0:T(8,128)(2,1)}, bf16[1,3,16,32,128]{4,3,2,1,0:T(8,128)(2,1)}, u32[]{:S(2)}, u32[]{:S(2)}) collective-permute-start(bf16[1,3,16,32,128]{4,3,2,1,0:T(8,128)(2,1)} %get-tuple-element.199), channel_id=1, source_target_pairs={{0,5},{1,4},{2,7},{3,6},{4,1},{5,0},{6,3},{7,2},{8,13},{9,12},{10,... | collective-permute-start | bytes 1179656 | tf_op jit(solution)/shard_map/ppermute | solution.py:365
  629.7 34.8 %collective-permute-start.82 = (bf16[1,3,16,32,128]{4,3,2,1,0:T(8,128)(2,1)}, bf16[1,3,16,32,128]{4,3,2,1,0:T(8,128)(2,1)}, u32[]{:S(2)}, u32[]{:S(2)}) collective-permute-start(bf16[1,3,16,32,128]{4,3,2,1,0:T(8,128)(2,1)} %get-tuple-element.200), channel_id=1, source_target_pairs={{0,6},{1,7},{2,4},{3,5},{4,2},{5,3},{6,0},{7,1},{8,14},{9,15},{10,... | collective-permute-start | bytes 1179656 | tf_op jit(solution)/shard_map/ppermute | solution.py:365
  658.5 71.8 %collective-permute-start.59 = (bf16[1,5,16,32,128]{4,3,2,1,0:T(8,128)(2,1)}, bf16[1,5,16,32,128]{4,3,2,1,0:T(8,128)(2,1)S(1)}, u32[]{:S(2)}, u32[]{:S(2)}) collective-permute-start(bf16[1,5,16,32,128]{4,3,2,1,0:T(8,128)(2,1)} %get-tuple-element.175), channel_id=1, source_target_pairs={{0,1},{1,0},{2,3},{3,2},{4,5},{5,4},{6,7},{7,6},{8,9},{9,8},{10,11... | collective-permute-start | bytes 1966088 | tf_op jit(solution)/shard_map/ppermute | solution.py:365
  659.5 72.2 %collective-permute-start.60 = (bf16[1,5,16,32,128]{4,3,2,1,0:T(8,128)(2,1)}, bf16[1,5,16,32,128]{4,3,2,1,0:T(8,128)(2,1)S(1)}, u32[]{:S(2)}, u32[]{:S(2)}) collective-permute-start(bf16[1,5,16,32,128]{4,3,2,1,0:T(8,128)(2,1)} %get-tuple-element.176), channel_id=1, source_target_pairs={{0,2},{1,3},{2,0},{3,1},{4,6},{5,7},{6,4},{7,5},{8,10},{9,11},{10,... | collective-permute-start | bytes 1966088 | tf_op jit(solution)/shard_map/ppermute | solution.py:365
  659.8 74.7 %collective-permute-start.61 = (bf16[1,5,16,32,128]{4,3,2,1,0:T(8,128)(2,1)}, bf16[1,5,16,32,128]{4,3,2,1,0:T(8,128)(2,1)S(1)}, u32[]{:S(2)}, u32[]{:S(2)}) collective-permute-start(bf16[1,5,16,32,128]{4,3,2,1,0:T(8,128)(2,1)} %get-tuple-element.177), channel_id=1, source_target_pairs={{0,3},{1,2},{2,1},{3,0},{4,7},{5,6},{6,5},{7,4},{8,11},{9,10},{10,... | collective-permute-start | bytes 1966088 | tf_op jit(solution)/shard_map/ppermute | solution.py:365
  662.1 74.6 %collective-permute-start.62 = (bf16[1,5,16,32,128]{4,3,2,1,0:T(8,128)(2,1)}, bf16[1,5,16,32,128]{4,3,2,1,0:T(8,128)(2,1)}, u32[]{:S(2)}, u32[]{:S(2)}) collective-permute-start(bf16[1,5,16,32,128]{4,3,2,1,0:T(8,128)(2,1)} %get-tuple-element.178), channel_id=1, source_target_pairs={{0,4},{1,5},{2,6},{3,7},{4,0},{5,1},{6,2},{7,3},{8,12},{9,13},{10,... | collective-permute-start | bytes 1966088 | tf_op jit(solution)/shard_map/ppermute | solution.py:365
  664.5 46.8 %collective-permute-start.83 = (bf16[1,3,16,32,128]{4,3,2,1,0:T(8,128)(2,1)}, bf16[1,3,16,32,128]{4,3,2,1,0:T(8,128)(2,1)S(1)}, u32[]{:S(2)}, u32[]{:S(2)}) collective-permute-start(bf16[1,3,16,32,128]{4,3,2,1,0:T(8,128)(2,1)} %get-tuple-element.201), channel_id=1, source_target_pairs={{0,7},{1,6},{2,5},{3,4},{4,3},{5,2},{6,1},{7,0},{8,15},{9,14},{10,... | collective-permute-start | bytes 1179656 | tf_op jit(solution)/shard_map/ppermute | solution.py:365
  711.3 57.4 %collective-permute-start.63 = (bf16[1,5,16,32,128]{4,3,2,1,0:T(8,128)(2,1)}, bf16[1,5,16,32,128]{4,3,2,1,0:T(8,128)(2,1)}, u32[]{:S(2)}, u32[]{:S(2)}) collective-permute-start(bf16[1,5,16,32,128]{4,3,2,1,0:T(8,128)(2,1)} %get-tuple-element.179), channel_id=1, source_target_pairs={{0,5},{1,4},{2,7},{3,6},{4,1},{5,0},{6,3},{7,2},{8,13},{9,12},{10,... | collective-permute-start | bytes 1966088 | tf_op jit(solution)/shard_map/ppermute | solution.py:365
  730.3 38.4 %collective-permute-start.64 = (bf16[1,5,16,32,128]{4,3,2,1,0:T(8,128)(2,1)}, bf16[1,5,16,32,128]{4,3,2,1,0:T(8,128)(2,1)}, u32[]{:S(2)}, u32[]{:S(2)}) collective-permute-start(bf16[1,5,16,32,128]{4,3,2,1,0:T(8,128)(2,1)} %get-tuple-element.180), channel_id=1, source_target_pairs={{0,6},{1,7},{2,4},{3,5},{4,2},{5,3},{6,0},{7,1},{8,14},{9,15},{10,... | collective-permute-start | bytes 1966088 | tf_op jit(solution)/shard_map/ppermute | solution.py:365
  731.8 37.0 %collective-permute-start.65 = (bf16[1,5,16,32,128]{4,3,2,1,0:T(8,128)(2,1)}, bf16[1,5,16,32,128]{4,3,2,1,0:T(8,128)(2,1)}, u32[]{:S(2)}, u32[]{:S(2)}) collective-permute-start(bf16[1,5,16,32,128]{4,3,2,1,0:T(8,128)(2,1)} %get-tuple-element.181), channel_id=1, source_target_pairs={{0,7},{1,6},{2,5},{3,4},{4,3},{5,2},{6,1},{7,0},{8,15},{9,14},{10,... | collective-permute-start | bytes 1966088 | tf_op jit(solution)/shard_map/ppermute | solution.py:365
  735.4 76.1 %collective-permute-start.33 = (bf16[1,16,256,128]{3,2,1,0:T(8,128)(2,1)S(1)}, bf16[1,16,256,128]{3,2,1,0:T(8,128)(2,1)}, u32[]{:S(2)}, u32[]{:S(2)}) collective-permute-start(bf16[1,16,256,128]{3,2,1,0:T(8,128)(2,1)S(1)} %copy-done.3), channel_id=1, source_target_pairs={{0,8},{8,16},{16,24},{24,0},{1,9},{9,17},{17,25},{25,1},{2,10},{10... | collective-permute-start | bytes 3145736 | tf_op jit(solution)/shard_map/ppermute | solution.py:462
  736.6 101.7 %collective-permute-start.23 = (bf16[1,16,256,128]{3,2,1,0:T(8,128)(2,1)}, bf16[1,16,256,128]{3,2,1,0:T(8,128)(2,1)S(1)}, u32[]{:S(2)}, u32[]{:S(2)}) collective-permute-start(bf16[1,16,256,128]{3,2,1,0:T(8,128)(2,1)} %slice.106), channel_id=1, source_target_pairs={{0,24},{8,0},{16,8},{24,16},{1,25},{9,1},{17,9},{25,17},{2,26},{10... | collective-permute-start | bytes 3145736 | tf_op jit(solution)/shard_map/ppermute | solution.py:463
  768.7 66.6 %collective-permute-start.84 = (f32[4,6,3,16,128]{4,3,2,1,0:T(8,128)}, f32[4,6,3,16,128]{4,3,2,1,0:T(8,128)}, u32[]{:S(2)}, u32[]{:S(2)}) collective-permute-start(f32[4,6,3,16,128]{4,3,2,1,0:T(8,128)} %slice_bitcast_fusion.2), channel_id=1, source_target_pairs={{0,1},{1,0},{2,3},{3,2},{4,5},{5,4},{6,7},{7,6},{8,9},{9,8},{10,11... | collective-permute-start | bytes 1769480 | tf_op jit(solution)/shard_map/ppermute | solution.py:365
  783.6 53.2 %collective-permute-start.90 = (bf16[4,6,5,16,128]{4,3,2,1,0:T(8,128)(2,1)}, bf16[4,6,5,16,128]{4,3,2,1,0:T(8,128)(2,1)}, u32[]{:S(2)}, u32[]{:S(2)}) collective-permute-start(bf16[4,6,5,16,128]{4,3,2,1,0:T(8,128)(2,1)} %fusion.13), channel_id=1, source_target_pairs={{0,1},{1,0},{2,3},{3,2},{4,5},{5,4},{6,7},{7,6},{8,9},{9,8},{10,11... | collective-permute-start | bytes 1474568 | tf_op jit(solution)/shard_map/ppermute | solution.py:365
  838.3 30.3 %collective-permute-start.47 = (bf16[1,2,16,32,128]{4,3,2,1,0:T(8,128)(2,1)}, bf16[1,2,16,32,128]{4,3,2,1,0:T(8,128)(2,1)}, u32[]{:S(2)}, u32[]{:S(2)}) collective-permute-start(bf16[1,2,16,32,128]{4,3,2,1,0:T(8,128)(2,1)} %get-tuple-element.160), channel_id=1, source_target_pairs={{0,5},{1,4},{2,7},{3,6},{4,1},{5,0},{6,3},{7,2},{8,13},{9,12},{10,... | collective-permute-start | bytes 786440 | tf_op jit(solution)/shard_map/ppermute | solution.py:365
  840.5 29.1 %collective-permute-start.48 = (bf16[1,2,16,32,128]{4,3,2,1,0:T(8,128)(2,1)}, bf16[1,2,16,32,128]{4,3,2,1,0:T(8,128)(2,1)}, u32[]{:S(2)}, u32[]{:S(2)}) collective-permute-start(bf16[1,2,16,32,128]{4,3,2,1,0:T(8,128)(2,1)} %get-tuple-element.161), channel_id=1, source_target_pairs={{0,6},{1,7},{2,4},{3,5},{4,2},{5,3},{6,0},{7,1},{8,14},{9,15},{10,... | collective-permute-start | bytes 786440 | tf_op jit(solution)/shard_map/ppermute | solution.py:365
  878.1 41.4 %collective-permute-start.87 = (f32[4,6,5,16,128]{4,3,2,1,0:T(8,128)}, f32[4,6,5,16,128]{4,3,2,1,0:T(8,128)}, u32[]{:S(2)}, u32[]{:S(2)}) collective-permute-start(f32[4,6,5,16,128]{4,3,2,1,0:T(8,128)} %slice_bitcast_fusion), channel_id=1, source_target_pairs={{0,1},{1,0},{2,3},{3,2},{4,5},{5,4},{6,7},{7,6},{8,9},{9,8},{10,11... | collective-permute-start | bytes 2949128 | tf_op jit(solution)/shard_map/ppermute | solution.py:365
  907.8 37.6 %collective-permute-start.92 = (bf16[1,6,5,16,128]{4,1,3,2,0:T(8,128)(2,1)}, bf16[1,6,5,16,128]{4,1,3,2,0:T(8,128)(2,1)}, u32[]{:S(2)}, u32[]{:S(2)}) collective-permute-start(bf16[1,6,5,16,128]{4,1,3,2,0:T(8,128)(2,1)} %fusion.26), channel_id=1, source_target_pairs={{0,4},{1,5},{2,6},{3,7},{4,0},{5,1},{6,2},{7,3},{8,12},{9,13},{10,... | collective-permute-start | bytes 368648 | tf_op jit(solution)/shard_map/ppermute | solution.py:365
  (113 other events, 3817.0 us)

commit v4 on v3

--- a/solution.py
+++ b/solution.py
@@ -304,19 +304,20 @@
     state, partial = refs[-2:]
     group, rows, count = (blocks[0].shape[i] for i in (0, 2, 3))
     base = place[0] if pieces > 1 else None
+    kinds = coef.shape[0]
     for index in range(pieces * group):
         part = owner_rows(base, index, rows)
         slot = jnp.bitwise_xor(base, index) if by_owner and pieces > 1 else index
         block = blocks[index // group]
         mine = jnp.swapaxes(block[index % group, 0].astype(F32), 0, 1)
         state[:, 0, part, :] = mine.astype(BF16)
-        sums = [None] * 6
+        sums = [None] * kinds
         for o in range(count):
             product = mine[o] * partner[o, 0, part, :].astype(F32)
-            for c in range(6):
+            for c in range(kinds):
                 term = coef[c, o] * product
                 sums[c] = term if sums[c] is None else sums[c] + term
-        for c in range(6):
+        for c in range(kinds):
             partial[slot, c, 0] = sums[c].astype(partial.dtype)
 
 
@@ -324,6 +325,7 @@
     pieces = len(blocks)
     group, depth, rows, count, lanes = blocks[0].shape
     owners = pieces * group
+    kinds = coef.shape[0]
     width = partner.shape[2]
     cells = owners * depth * rows * count * lanes
     slab = pl.BlockSpec((count, 1, width, lanes), lambda z: (0, start + z, 0, 0))
@@ -344,12 +346,12 @@
         in_specs=in_specs,
         out_specs=[
             slab,
-            pl.BlockSpec((owners, 6, 1, rows, lanes), lambda z: (0, 0, z, 0, 0)),
+            pl.BlockSpec((owners, kinds, 1, rows, lanes), lambda z: (0, 0, z, 0, 0)),
         ],
         out_shape=[
             jax.ShapeDtypeStruct(partner.shape, BF16),
             jax.ShapeDtypeStruct(
-                (owners, 6, depth, rows, lanes), BF16 if closing else F32
+                (owners, kinds, depth, rows, lanes), BF16 if closing else F32
             ),
         ],
         input_output_aliases=aliases,
@@ -417,8 +419,9 @@
     field_terms, tensor_terms = angle_tables(orientations)
     weights = stencil_weights(orientations)
     exponent_terms = -step_length * field_terms
+    free_terms = jnp.concatenate([tensor_terms[:2], tensor_terms[3:]])
     local_tensor = lax.dynamic_slice_in_dim(
-        tensor_terms * orient_weight[None, :], me * count, count, 1
+        free_terms * orient_weight[None, :], me * count, count, 1
     )
     wide_weights = jnp.broadcast_to(weights[:, :, None], weights.shape + (lanes,))
     top = lax.reduce_precision(exponent_terms, 8, 7)
@@ -487,7 +490,8 @@
             sums[c] = jnp.sum(exchange(partial).astype(F32), axis=0)
         else:
             sums[c] = halve(partial, c == RETURNING[2])
-    tensor = jnp.concatenate([sums[c] for c in range(chunks)], axis=1)
+    free = jnp.concatenate([sums[c] for c in range(chunks)], axis=1)
+    tensor = jnp.concatenate([free[:2], -(free[:1] + free[1:2]), free[2:]])
     new_field = (1.0 - relax_rate) * own_field.astype(F32) + relax_rate * coupling * tensor
     return (state, new_field)
 

time: 949 us -> 945 us (level)
  starting transfers between devices: 338 us -> 295 us
  waiting for transfers between devices: 325 us -> 366 us
    ppermute x79, waiting for transfers between devices: 307 us -> 350 us  [swapped(): lax.ppermute(block, 'orient', [(i, i ^ distance) for i in range(owners)])]
    ppermute x79, starting transfers between devices: 273 us -> 243 us  [swapped(): lax.ppermute(block, 'orient', [(i, i ^ distance) for i in range(owners)])]
    ppermute x5, starting transfers between devices: 40.8 us -> 25 us  [staged_device(): souths[c] = lax.ppermute(top_rows, 'orient', ring(owners, 1))]
  transfers between devices with their start and end apart: 95 -> 95, of which waited for: 25 -> 28; matrix products, arithmetic and copies ran while one was open for 3% -> 3% of each run, Pallas kernels for 24% -> 24%
where the time goes in v4:
time: 945 us; the launch traced here: 944 us
  waiting for transfers between devices  366 us (39%)
  starting transfers between devices  295 us (31%)
  Pallas kernels  242 us (26%)
  local copies, waits for them, and re-layouts  21.4 us (2%)
  other arithmetic  15.3 us (2%)
    ppermute x79, waiting for transfers between devices, swapped(): lax.ppermute(block, 'orient', [(i, i ^ distance) for i in range(owners)])  350 us
    ppermute x79, starting transfers between devices, swapped(): lax.ppermute(block, 'orient', [(i, i ^ distance) for i in range(owners)])  243 us
    pallas_call x5, Pallas kernels, advect_turn(): pl.pallas_call(functools.partial(advect_turn_kernel, pieces), grid=(depth...  85.7 us
    pallas_call x5, Pallas kernels, advect(): pl.pallas_call(functools.partial(advect_kernel, low is not None, high is...  76.1 us
    pallas_call x5, Pallas kernels, gather(): pl.pallas_call(functools.partial(gather_kernel, pieces, closing), grid=(d...  42.4 us
    pallas_call x5, Pallas kernels, turn(): pl.pallas_call(functools.partial(turn_kernel, pieces), grid=(depth,), in_...  37.9 us
    ppermute x5, starting transfers between devices, staged_device(): souths[c] = lax.ppermute(top_rows, 'orient', ring(owners, 1))  25 us
  transfers between devices with their start and end apart: 95, of which 28 were waited for; matrix products, arithmetic and copies ran while one was open for 3% of the time, Pallas kernels for 24%

profile of v4, /device:TPU:0, one launch (start us, length us, event | category | flops | bytes accessed | tf_op | source)
XLA Modules:
  0.0 943.6 jit_solution(13356434832567575561)
XLA Ops:
  0.7 14.2 %advect_first.8 = (bf16[1,3,16,32,128]{4,3,2,1,0:T(8,128)(2,1)}, bf16[1,3,16,32,128]{4,3,2,1,0:T(8,128)(2,1)}, bf16[1,3,16,32,128]{4,3,2,1,0:T(8,128)(2,1)}, bf1...) custom-call(f32[3,256]{1,0:T(4,128)} %refs_0_.9, ...), custom_call_target="tpu_custom_call" | custom-call | flops 47185920 | bytes 12582912 | tf_op jit(solution)/shard_map/advect_first/pallas_call | solution.py:147
  19.5 22.0 %advect_first.6 = (bf16[1,5,16,32,128]{4,3,2,1,0:T(8,128)(2,1)}, bf16[1,5,16,32,128]{4,3,2,1,0:T(8,128)(2,1)}, bf16[1,5,16,32,128]{4,3,2,1,0:T(8,128)(2,1)}, bf1...) custom-call(f32[3,256]{1,0:T(4,128)} %refs_0_.9, ...), custom_call_target="tpu_custom_call" | custom-call | flops 78643200 | bytes 20971520 | tf_op jit(solution)/shard_map/advect_first/pallas_call | solution.py:147
  46.1 3.9 collective-permute-start.39
  51.1 38.0 %collective-permute-done.37.refs_4_ = bf16[1,3,16,32,128]{4,3,2,1,0:T(8,128)(2,1)S(1)} collective-permute-done((bf16[1,3,16,32,128]{4,3,2,1,0:T(8,128)(2,1)}, bf16[1,3,16,32,128]{4,3,2,1,0:T(8,128)(2,1)S(1)}, u32[]{:S(2)}, u32[]{:S(2)}) %collective-permute-start.37) | collective-permute-done | bytes 393248 | tf_op jit(solution)/shard_map/ppermute | solution.py:367
  89.2 8.3 collective-permute-done.38.refs_5_
  98.3 9.3 collective-permute-start.11
  107.6 17.3 %collective-permute-start.12 = (bf16[1,5,16,32,128]{4,3,2,1,0:T(8,128)(2,1)}, bf16[1,5,16,32,128]{4,3,2,1,0:T(8,128)(2,1)S(1)}, u32[]{:S(2)}, u32[]{:S(2)}) collective-permute-start(bf16[1,5,16,32,128]{4,3,2,1,0:T(8,128)(2,1)} %get-tuple-element.121), channel_id=1, source_target_pairs={{0,5},{1,4},{2,7},{3,6},{4,1},{5,0},{6,3},{7,2},{8,13},{9,12},{10,... | collective-permute-start | bytes 1966088 | tf_op jit(solution)/shard_map/ppermute | solution.py:367
  125.0 22.1 %advect_first.9 = (bf16[1,5,16,32,128]{4,3,2,1,0:T(8,128)(2,1)}, bf16[1,5,16,32,128]{4,3,2,1,0:T(8,128)(2,1)}, bf16[1,5,16,32,128]{4,3,2,1,0:T(8,128)(2,1)}, bf1...) custom-call(f32[3,256]{1,0:T(4,128)} %refs_0_.9, ...), custom_call_target="tpu_custom_call" | custom-call | flops 78643200 | bytes 20971520 | tf_op jit(solution)/shard_map/advect_first/pallas_call | solution.py:147
  147.2 3.7 collective-permute-start.14
  153.3 36.5 %collective-permute-done.11.refs_4_ = bf16[1,5,16,32,128]{4,3,2,1,0:T(8,128)(2,1)S(1)} collective-permute-done((bf16[1,5,16,32,128]{4,3,2,1,0:T(8,128)(2,1)}, bf16[1,5,16,32,128]{4,3,2,1,0:T(8,128)(2,1)S(1)}, u32[]{:S(2)}, u32[]{:S(2)}) %collective-permute-start.11) | collective-permute-done | bytes 655392 | tf_op jit(solution)/shard_map/ppermute | solution.py:367
  191.5 12.2 %collective-permute-done.12.refs_5_ = bf16[1,5,16,32,128]{4,3,2,1,0:T(8,128)(2,1)S(1)} collective-permute-done((bf16[1,5,16,32,128]{4,3,2,1,0:T(8,128)(2,1)}, bf16[1,5,16,32,128]{4,3,2,1,0:T(8,128)(2,1)S(1)}, u32[]{:S(2)}, u32[]{:S(2)}) %collective-permute-start.12) | collective-permute-done | bytes 655392 | tf_op jit(solution)/shard_map/ppermute | solution.py:367
  205.5 16.0 %collective-permute-start.53 = (bf16[1,5,16,32,128]{4,3,2,1,0:T(8,128)(2,1)}, bf16[1,5,16,32,128]{4,3,2,1,0:T(8,128)(2,1)}, u32[]{:S(2)}, u32[]{:S(2)}) collective-permute-start(bf16[1,5,16,32,128]{4,3,2,1,0:T(8,128)(2,1)} %get-tuple-element.167), channel_id=1, source_target_pairs={{0,4},{1,5},{2,6},{3,7},{4,0},{5,1},{6,2},{7,3},{8,12},{9,13},{10,... | collective-permute-start | bytes 1966088 | tf_op jit(solution)/shard_map/ppermute | solution.py:367
  227.8 26.8 %collective-permute-start.54 = (bf16[1,5,16,32,128]{4,3,2,1,0:T(8,128)(2,1)}, bf16[1,5,16,32,128]{4,3,2,1,0:T(8,128)(2,1)}, u32[]{:S(2)}, u32[]{:S(2)}) collective-permute-start(bf16[1,5,16,32,128]{4,3,2,1,0:T(8,128)(2,1)} %get-tuple-element.168), channel_id=1, source_target_pairs={{0,5},{1,4},{2,7},{3,6},{4,1},{5,0},{6,3},{7,2},{8,13},{9,12},{10,... | collective-permute-start | bytes 1966088 | tf_op jit(solution)/shard_map/ppermute | solution.py:367
  257.4 33.4 %collective-permute-done.53.refs_4_ = bf16[1,5,16,32,128]{4,3,2,1,0:T(8,128)(2,1)} collective-permute-done((bf16[1,5,16,32,128]{4,3,2,1,0:T(8,128)(2,1)}, bf16[1,5,16,32,128]{4,3,2,1,0:T(8,128)(2,1)}, u32[]{:S(2)}, u32[]{:S(2)}) %collective-permute-start.53) | collective-permute-done | bytes 655392 | tf_op jit(solution)/shard_map/ppermute | solution.py:367
  290.8 4.5 collective-permute-start.56
  297.5 7.3 turn_first.8
  304.9 14.9 %collective-permute-done.54.refs_5_ = bf16[1,5,16,32,128]{4,3,2,1,0:T(8,128)(2,1)} collective-permute-done((bf16[1,5,16,32,128]{4,3,2,1,0:T(8,128)(2,1)}, bf16[1,5,16,32,128]{4,3,2,1,0:T(8,128)(2,1)}, u32[]{:S(2)}, u32[]{:S(2)}) %collective-permute-start.54) | collective-permute-done | bytes 655392 | tf_op jit(solution)/shard_map/ppermute | solution.py:367
  320.3 4.1 collective-permute-start.76
  324.5 10.6 %turn_first.6 = (bf16[5,16,256,128]{3,2,1,0:T(8,128)(2,1)}, bf16[5,1,256,128]{3,2,1,0:T(8,128)(2,1)}, bf16[5,1,256,128]{3,2,1,0:T(8,128)(2,1)}) custom-call(bf16[256,256]{1,0:T(8,128)(2,1)} %fusion.5.rotation, bf16[1,5,16,32,128]{4,3,2,1,0:T(8,128)(2,1)} %get-tuple-element.116.refs_0_, bf16[1,5,16,32,128]{4,3,2,1,0:T(8,128)(2,1)} %copy-done.10, ...), custom_call_target="tpu_custom_call" | custom-call | flops 1342177280 | bytes 10485760 | tf_op jit(solution)/shard_map/turn_first/pallas_call | solution.py:193
  335.1 10.5 %turn_first.9 = (bf16[5,16,256,128]{3,2,1,0:T(8,128)(2,1)}, bf16[5,1,256,128]{3,2,1,0:T(8,128)(2,1)}, bf16[5,1,256,128]{3,2,1,0:T(8,128)(2,1)}) custom-call(bf16[256,256]{1,0:T(8,128)(2,1)} %fusion.5.rotation, bf16[1,5,16,32,128]{4,3,2,1,0:T(8,128)(2,1)} %get-tuple-element.163.refs_0_, bf16[1,5,16,32,128]{4,3,2,1,0:T(8,128)(2,1)} %copy-done.15, ...), custom_call_target="tpu_custom_call" | custom-call | flops 1342177280 | bytes 10485760 | tf_op jit(solution)/shard_map/turn_first/pallas_call | solution.py:193
  346.3 4.7 collective-permute-start.58
  351.7 24.3 %collective-permute-start.66 = (bf16[5,1,256,128]{3,2,1,0:T(8,128)(2,1)}, bf16[5,1,256,128]{3,2,1,0:T(8,128)(2,1)S(1)}, u32[]{:S(2)}, u32[]{:S(2)}) collective-permute-start(bf16[5,1,256,128]{3,2,1,0:T(8,128)(2,1)} %get-tuple-element.182), channel_id=1, source_target_pairs={{0,1},{1,2},{2,3},{3,4},{4,5},{5,6},{6,7},{7,0},{8,9},{9,10},{10,1... | collective-permute-start | bytes 983048 | tf_op jit(solution)/shard_map/ppermute | solution.py:463
  377.2 6.5 advect_first.5
  389.1 11.3 %advect_first.7 = (bf16[1,2,16,32,128]{4,3,2,1,0:T(8,128)(2,1)}, bf16[1,2,16,32,128]{4,3,2,1,0:T(8,128)(2,1)}, bf16[1,2,16,32,128]{4,3,2,1,0:T(8,128)(2,1)}, bf1...) custom-call(f32[3,256]{1,0:T(4,128)} %refs_0_.9, ...), custom_call_target="tpu_custom_call" | custom-call | flops 31457280 | bytes 8388608 | tf_op jit(solution)/shard_map/advect_first/pallas_call | solution.py:147
  412.8 6.7 collective-permute-done.4.refs_4_
  420.1 4.0 collective-permute-done.5.refs_5_
  429.7 24.7 %advect_turn.8 = (bf16[1,5,16,32,128]{4,3,2,1,0:T(8,128)(2,1)}, bf16[1,5,16,32,128]{4,3,2,1,0:T(8,128)(2,1)}, bf16[1,5,16,32,128]{4,3,2,1,0:T(8,128)(2,1)}, bf16...) custom-call(bf16[256,256]{1,0:T(8,128)(2,1)} %convolution_convert_fu, ...), custom_call_target="tpu_custom_call" | custom-call | flops 1342177280 | bytes 20971520 | tf_op jit(solution)/shard_map/advect_turn/pallas_call | solution.py:271
  462.8 14.0 %collective-permute-done.20.refs_5_ = bf16[1,2,16,32,128]{4,3,2,1,0:T(8,128)(2,1)S(1)} collective-permute-done((bf16[1,2,16,32,128]{4,3,2,1,0:T(8,128)(2,1)S(1)}, bf16[1,2,16,32,128]{4,3,2,1,0:T(8,128)(2,1)S(1)}, u32[]{:S(2)}, u32[]{:S(2)}) %collective-permute-start.20) | collective-permute-done | bytes 262176 | tf_op jit(solution)/shard_map/ppermute | solution.py:367
  476.8 3.6 collective-permute-start.70
  480.4 4.1 collective-permute-done.21.refs_6_
  485.2 4.9 collective-permute-done.22.refs_7_
  490.1 5.1 collective-permute-start.72
  501.1 5.7 turn_first.7
  506.8 16.4 %advect_turn.9 = (bf16[1,3,16,32,128]{4,3,2,1,0:T(8,128)(2,1)}, bf16[1,3,16,32,128]{4,3,2,1,0:T(8,128)(2,1)}, bf16[1,3,16,32,128]{4,3,2,1,0:T(8,128)(2,1)}, bf16...) custom-call(bf16[256,256]{1,0:T(8,128)(2,1)} %convolution_convert_fu, ...), custom_call_target="tpu_custom_call" | custom-call | flops 805306368 | bytes 12582912 | tf_op jit(solution)/shard_map/advect_turn/pallas_call | solution.py:271
  523.3 40.7 %collective-permute-done.71.refs_4_ = bf16[1,5,16,32,128]{4,3,2,1,0:T(8,128)(2,1)S(1)} collective-permute-done((bf16[1,5,16,32,128]{4,3,2,1,0:T(8,128)(2,1)}, bf16[1,5,16,32,128]{4,3,2,1,0:T(8,128)(2,1)S(1)}, u32[]{:S(2)}, u32[]{:S(2)}) %collective-permute-start.71) | collective-permute-done | bytes 655392 | tf_op jit(solution)/shard_map/ppermute | solution.py:367
  564.0 15.3 %collective-permute-done.72.refs_5_ = bf16[1,5,16,32,128]{4,3,2,1,0:T(8,128)(2,1)S(1)} collective-permute-done((bf16[1,5,16,32,128]{4,3,2,1,0:T(8,128)(2,1)}, bf16[1,5,16,32,128]{4,3,2,1,0:T(8,128)(2,1)S(1)}, u32[]{:S(2)}, u32[]{:S(2)}) %collective-permute-start.72) | collective-permute-done | bytes 655392 | tf_op jit(solution)/shard_map/ppermute | solution.py:367
  579.3 16.8 %collective-permute-start.80 = (bf16[1,3,16,32,128]{4,3,2,1,0:T(8,128)(2,1)}, bf16[1,3,16,32,128]{4,3,2,1,0:T(8,128)(2,1)}, u32[]{:S(2)}, u32[]{:S(2)}) collective-permute-start(bf16[1,3,16,32,128]{4,3,2,1,0:T(8,128)(2,1)} %get-tuple-element.198), channel_id=1, source_target_pairs={{0,4},{1,5},{2,6},{3,7},{4,0},{5,1},{6,2},{7,3},{8,12},{9,13},{10,... | collective-permute-start | bytes 1179656 | tf_op jit(solution)/shard_map/ppermute | solution.py:367
  596.1 23.5 %collective-permute-start.81 = (bf16[1,3,16,32,128]{4,3,2,1,0:T(8,128)(2,1)}, bf16[1,3,16,32,128]{4,3,2,1,0:T(8,128)(2,1)}, u32[]{:S(2)}, u32[]{:S(2)}) collective-permute-start(bf16[1,3,16,32,128]{4,3,2,1,0:T(8,128)(2,1)} %get-tuple-element.199), channel_id=1, source_target_pairs={{0,5},{1,4},{2,7},{3,6},{4,1},{5,0},{6,3},{7,2},{8,13},{9,12},{10,... | collective-permute-start | bytes 1179656 | tf_op jit(solution)/shard_map/ppermute | solution.py:367
  619.7 3.9 turn_first.5
  623.6 24.6 %advect_turn.7 = (bf16[1,5,16,32,128]{4,3,2,1,0:T(8,128)(2,1)}, bf16[1,5,16,32,128]{4,3,2,1,0:T(8,128)(2,1)}, bf16[1,5,16,32,128]{4,3,2,1,0:T(8,128)(2,1)}, bf16...) custom-call(bf16[256,256]{1,0:T(8,128)(2,1)} %convolution_convert_fu, ...), custom_call_target="tpu_custom_call" | custom-call | flops 1342177280 | bytes 20971520 | tf_op jit(solution)/shard_map/advect_turn/pallas_call | solution.py:271
  656.5 21.1 %collective-permute-done.82.refs_6_ = bf16[1,3,16,32,128]{4,3,2,1,0:T(8,128)(2,1)} collective-permute-done((bf16[1,3,16,32,128]{4,3,2,1,0:T(8,128)(2,1)}, bf16[1,3,16,32,128]{4,3,2,1,0:T(8,128)(2,1)}, u32[]{:S(2)}, u32[]{:S(2)}) %collective-permute-start.82) | collective-permute-done | bytes 393248 | tf_op jit(solution)/shard_map/ppermute | solution.py:367
  677.7 21.8 %collective-permute-done.83.refs_7_ = bf16[1,3,16,32,128]{4,3,2,1,0:T(8,128)(2,1)S(1)} collective-permute-done((bf16[1,3,16,32,128]{4,3,2,1,0:T(8,128)(2,1)}, bf16[1,3,16,32,128]{4,3,2,1,0:T(8,128)(2,1)S(1)}, u32[]{:S(2)}, u32[]{:S(2)}) %collective-permute-start.83) | collective-permute-done | bytes 393248 | tf_op jit(solution)/shard_map/ppermute | solution.py:367
  705.4 8.4 gather_last.5
  715.7 39.2 %collective-permute-done.62.refs_4_ = bf16[1,5,16,32,128]{4,3,2,1,0:T(8,128)(2,1)} collective-permute-done((bf16[1,5,16,32,128]{4,3,2,1,0:T(8,128)(2,1)}, bf16[1,5,16,32,128]{4,3,2,1,0:T(8,128)(2,1)}, u32[]{:S(2)}, u32[]{:S(2)}) %collective-permute-start.62) | collective-permute-done | bytes 655392 | tf_op jit(solution)/shard_map/ppermute | solution.py:367
  756.8 12.0 %gather_last.6 = (bf16[32,16,128,128]{3,2,1,0:T(8,128)(2,1)}, f32[8,5,5,16,128]{4,3,2,1,0:T(8,128)}) custom-call(f32[5,32]{1,0:T(8,128)} %dynamic-slice_multiply_fusion.coef, s32[1]{0:T(128)} %bitcast.refs_1_.place, bf16[1,5,16,32,128]{4,3,2,1,0:T(8,128)(2,1)} %get-tuple-element.184.refs_0_, ...), custom_call_target="tpu_custom_call", output_to_operand_aliasing={{0}: (11, {})} | custom-call | flops 36700160 | bytes 15728640 | tf_op jit(solution)/shard_map/gather_last/pallas_call | solution.py:343
  771.7 12.1 %gather_last.7 = (bf16[32,16,128,128]{3,2,1,0:T(8,128)(2,1)}, f32[8,5,5,16,128]{4,3,2,1,0:T(8,128)}) custom-call(f32[5,32]{1,0:T(8,128)} %dynamic-slice_multiply_fusion.coef, s32[1]{0:T(128)} %bitcast.refs_1_.place, bf16[1,5,16,32,128]{4,3,2,1,0:T(8,128)(2,1)} %get-tuple-element.174.refs_0_, ...), custom_call_target="tpu_custom_call", output_to_operand_aliasing={{0}: (11, {})} | custom-call | flops 36700160 | bytes 15728640 | tf_op jit(solution)/shard_map/gather_last/pallas_call | solution.py:343
  785.0 4.7 collective-permute-start.42
  792.6 9.5 %collective-permute-done.42.north = bf16[2,1,256,128]{3,2,1,0:T(8,128)(2,1)S(1)} collective-permute-done((bf16[2,1,256,128]{3,2,1,0:T(8,128)(2,1)S(1)}, bf16[2,1,256,128]{3,2,1,0:T(8,128)(2,1)S(1)}, u32[]{:S(2)}, u32[]{:S(2)}) %collective-permute-start.42) | collective-permute-done | bytes 131104 | tf_op jit(solution)/shard_map/ppermute | solution.py:464
  802.1 13.1 %collective-permute-start.90 = (bf16[4,5,5,16,128]{4,3,2,1,0:T(8,128)(2,1)S(1)}, bf16[4,5,5,16,128]{4,3,2,1,0:T(8,128)(2,1)S(1)}, u32[]{:S(2)}, u32[]{:S(2)}) collective-permute-start(bf16[4,5,5,16,128]{4,3,2,1,0:T(8,128)(2,1)S(1)} %fusion.14), channel_id=1, source_target_pairs={{0,1},{1,0},{2,3},{3,2},{4,5},{5,4},{6,7},{7,6},{8,9},{9,8},{10,11... | collective-permute-start | bytes 1228808 | tf_op jit(solution)/shard_map/ppermute | solution.py:367
  816.0 12.2 %advect_turn.6 = (bf16[1,2,16,32,128]{4,3,2,1,0:T(8,128)(2,1)}, bf16[1,2,16,32,128]{4,3,2,1,0:T(8,128)(2,1)}, bf16[1,2,16,32,128]{4,3,2,1,0:T(8,128)(2,1)}, bf16...) custom-call(bf16[256,256]{1,0:T(8,128)(2,1)} %convolution_convert_fu, ...), custom_call_target="tpu_custom_call" | custom-call | flops 536870912 | bytes 8388608 | tf_op jit(solution)/shard_map/advect_turn/pallas_call | solution.py:271
  834.8 3.5 collective-permute-done.43.refs_1_
  838.3 3.7 collective-permute-start.47
  852.3 7.8 advect_turn.5
  860.1 7.6 collective-permute-done.46.refs_4_
  867.7 5.1 collective-permute-done.47.refs_5_
  872.8 5.9 collective-permute-start.28
  883.9 4.1 collective-permute-start.31
  888.7 5.7 gather_last.8
  897.3 4.1 collective-permute-done.30.refs_5_
  902.1 4.1 gather_last.9
  906.3 7.5 all-to-all-start.1
  922.4 3.4 all-to-all-start
  926.5 5.2 collective-permute-done.88
  933.1 5.5 all-to-all-done
  (354 shorter events, 138.4 us)
Async XLA Ops:
  14.9 31.2 %collective-permute-start.34 = (bf16[1,3,16,32,128]{4,3,2,1,0:T(8,128)(2,1)}, bf16[1,3,16,32,128]{4,3,2,1,0:T(8,128)(2,1)S(1)}, u32[]{:S(2)}, u32[]{:S(2)}) collective-permute-start(bf16[1,3,16,32,128]{4,3,2,1,0:T(8,128)(2,1)} %get-tuple-element.145), channel_id=1, source_target_pairs={{0,1},{1,0},{2,3},{3,2},{4,5},{5,4},{6,7},{7,6},{8,9},{9,8},{10,11... | collective-permute-start | bytes 1179656 | tf_op jit(solution)/shard_map/ppermute | solution.py:367
  17.9 28.1 %collective-permute-start.35 = (bf16[1,3,16,32,128]{4,3,2,1,0:T(8,128)(2,1)}, bf16[1,3,16,32,128]{4,3,2,1,0:T(8,128)(2,1)S(1)}, u32[]{:S(2)}, u32[]{:S(2)}) collective-permute-start(bf16[1,3,16,32,128]{4,3,2,1,0:T(8,128)(2,1)} %get-tuple-element.146), channel_id=1, source_target_pairs={{0,2},{1,3},{2,0},{3,1},{4,6},{5,7},{6,4},{7,5},{8,10},{9,11},{10,... | collective-permute-start | bytes 1179656 | tf_op jit(solution)/shard_map/ppermute | solution.py:367
  19.5 30.4 %collective-permute-start.36 = (bf16[1,3,16,32,128]{4,3,2,1,0:T(8,128)(2,1)}, bf16[1,3,16,32,128]{4,3,2,1,0:T(8,128)(2,1)S(1)}, u32[]{:S(2)}, u32[]{:S(2)}) collective-permute-start(bf16[1,3,16,32,128]{4,3,2,1,0:T(8,128)(2,1)} %get-tuple-element.147), channel_id=1, source_target_pairs={{0,3},{1,2},{2,1},{3,0},{4,7},{5,6},{6,5},{7,4},{8,11},{9,10},{10,... | collective-permute-start | bytes 1179656 | tf_op jit(solution)/shard_map/ppermute | solution.py:367
  41.5 83.5 %collective-permute-start.8 = (bf16[1,5,16,32,128]{4,3,2,1,0:T(8,128)(2,1)}, bf16[1,5,16,32,128]{4,3,2,1,0:T(8,128)(2,1)S(1)}, u32[]{:S(2)}, u32[]{:S(2)}) collective-permute-start(bf16[1,5,16,32,128]{4,3,2,1,0:T(8,128)(2,1)} %get-tuple-element.117), channel_id=1, source_target_pairs={{0,1},{1,0},{2,3},{3,2},{4,5},{5,4},{6,7},{7,6},{8,9},{9,8},{10,11... | collective-permute-start | bytes 1966088 | tf_op jit(solution)/shard_map/ppermute | solution.py:367
  43.5 45.7 %collective-permute-start.37 = (bf16[1,3,16,32,128]{4,3,2,1,0:T(8,128)(2,1)}, bf16[1,3,16,32,128]{4,3,2,1,0:T(8,128)(2,1)S(1)}, u32[]{:S(2)}, u32[]{:S(2)}) collective-permute-start(bf16[1,3,16,32,128]{4,3,2,1,0:T(8,128)(2,1)} %get-tuple-element.148), channel_id=1, source_target_pairs={{0,4},{1,5},{2,6},{3,7},{4,0},{5,1},{6,2},{7,3},{8,12},{9,13},{10,... | collective-permute-start | bytes 1179656 | tf_op jit(solution)/shard_map/ppermute | solution.py:367
  46.1 51.5 %collective-permute-start.38 = (bf16[1,3,16,32,128]{4,3,2,1,0:T(8,128)(2,1)}, bf16[1,3,16,32,128]{4,3,2,1,0:T(8,128)(2,1)S(1)}, u32[]{:S(2)}, u32[]{:S(2)}) collective-permute-start(bf16[1,3,16,32,128]{4,3,2,1,0:T(8,128)(2,1)} %get-tuple-element.149), channel_id=1, source_target_pairs={{0,5},{1,4},{2,7},{3,6},{4,1},{5,0},{6,3},{7,2},{8,13},{9,12},{10,... | collective-permute-start | bytes 1179656 | tf_op jit(solution)/shard_map/ppermute | solution.py:367
  46.1 51.5 %collective-permute-start.39 = (bf16[1,3,16,32,128]{4,3,2,1,0:T(8,128)(2,1)}, bf16[1,3,16,32,128]{4,3,2,1,0:T(8,128)(2,1)S(1)}, u32[]{:S(2)}, u32[]{:S(2)}) collective-permute-start(bf16[1,3,16,32,128]{4,3,2,1,0:T(8,128)(2,1)} %get-tuple-element.150), channel_id=1, source_target_pairs={{0,6},{1,7},{2,4},{3,5},{4,2},{5,3},{6,0},{7,1},{8,14},{9,15},{10,... | collective-permute-start | bytes 1179656 | tf_op jit(solution)/shard_map/ppermute | solution.py:367
  49.9 57.6 %collective-permute-start.40 = (bf16[1,3,16,32,128]{4,3,2,1,0:T(8,128)(2,1)}, bf16[1,3,16,32,128]{4,3,2,1,0:T(8,128)(2,1)S(1)}, u32[]{:S(2)}, u32[]{:S(2)}) collective-permute-start(bf16[1,3,16,32,128]{4,3,2,1,0:T(8,128)(2,1)} %get-tuple-element.151), channel_id=1, source_target_pairs={{0,7},{1,6},{2,5},{3,4},{4,3},{5,2},{6,1},{7,0},{8,15},{9,14},{10,... | collective-permute-start | bytes 1179656 | tf_op jit(solution)/shard_map/ppermute | solution.py:367
  89.1 58.1 %collective-permute-start.9 = (bf16[1,5,16,32,128]{4,3,2,1,0:T(8,128)(2,1)}, bf16[1,5,16,32,128]{4,3,2,1,0:T(8,128)(2,1)S(1)}, u32[]{:S(2)}, u32[]{:S(2)}) collective-permute-start(bf16[1,5,16,32,128]{4,3,2,1,0:T(8,128)(2,1)} %get-tuple-element.118), channel_id=1, source_target_pairs={{0,2},{1,3},{2,0},{3,1},{4,6},{5,7},{6,4},{7,5},{8,10},{9,11},{10,... | collective-permute-start | bytes 1966088 | tf_op jit(solution)/shard_map/ppermute | solution.py:367
  97.5 54.2 %collective-permute-start.10 = (bf16[1,5,16,32,128]{4,3,2,1,0:T(8,128)(2,1)}, bf16[1,5,16,32,128]{4,3,2,1,0:T(8,128)(2,1)S(1)}, u32[]{:S(2)}, u32[]{:S(2)}) collective-permute-start(bf16[1,5,16,32,128]{4,3,2,1,0:T(8,128)(2,1)} %get-tuple-element.119), channel_id=1, source_target_pairs={{0,3},{1,2},{2,1},{3,0},{4,7},{5,6},{6,5},{7,4},{8,11},{9,10},{10,... | collective-permute-start | bytes 1966088 | tf_op jit(solution)/shard_map/ppermute | solution.py:367
  98.3 91.5 %collective-permute-start.11 = (bf16[1,5,16,32,128]{4,3,2,1,0:T(8,128)(2,1)}, bf16[1,5,16,32,128]{4,3,2,1,0:T(8,128)(2,1)S(1)}, u32[]{:S(2)}, u32[]{:S(2)}) collective-permute-start(bf16[1,5,16,32,128]{4,3,2,1,0:T(8,128)(2,1)} %get-tuple-element.120), channel_id=1, source_target_pairs={{0,4},{1,5},{2,6},{3,7},{4,0},{5,1},{6,2},{7,3},{8,12},{9,13},{10,... | collective-permute-start | bytes 1966088 | tf_op jit(solution)/shard_map/ppermute | solution.py:367
  107.6 96.1 %collective-permute-start.12 = (bf16[1,5,16,32,128]{4,3,2,1,0:T(8,128)(2,1)}, bf16[1,5,16,32,128]{4,3,2,1,0:T(8,128)(2,1)S(1)}, u32[]{:S(2)}, u32[]{:S(2)}) collective-permute-start(bf16[1,5,16,32,128]{4,3,2,1,0:T(8,128)(2,1)} %get-tuple-element.121), channel_id=1, source_target_pairs={{0,5},{1,4},{2,7},{3,6},{4,1},{5,0},{6,3},{7,2},{8,13},{9,12},{10,... | collective-permute-start | bytes 1966088 | tf_op jit(solution)/shard_map/ppermute | solution.py:367
  125.0 80.6 %collective-permute-start.13 = (bf16[1,5,16,32,128]{4,3,2,1,0:T(8,128)(2,1)}, bf16[1,5,16,32,128]{4,3,2,1,0:T(8,128)(2,1)}, u32[]{:S(2)}, u32[]{:S(2)}) collective-permute-start(bf16[1,5,16,32,128]{4,3,2,1,0:T(8,128)(2,1)} %get-tuple-element.122), channel_id=1, source_target_pairs={{0,6},{1,7},{2,4},{3,5},{4,2},{5,3},{6,0},{7,1},{8,14},{9,15},{10,... | collective-permute-start | bytes 1966088 | tf_op jit(solution)/shard_map/ppermute | solution.py:367
  147.2 78.3 %collective-permute-start.14 = (bf16[1,5,16,32,128]{4,3,2,1,0:T(8,128)(2,1)}, bf16[1,5,16,32,128]{4,3,2,1,0:T(8,128)(2,1)S(1)}, u32[]{:S(2)}, u32[]{:S(2)}) collective-permute-start(bf16[1,5,16,32,128]{4,3,2,1,0:T(8,128)(2,1)} %get-tuple-element.123), channel_id=1, source_target_pairs={{0,7},{1,6},{2,5},{3,4},{4,3},{5,2},{6,1},{7,0},{8,15},{9,14},{10,... | collective-permute-start | bytes 1966088 | tf_op jit(solution)/shard_map/ppermute | solution.py:367
  151.8 76.0 %collective-permute-start.50 = (bf16[1,5,16,32,128]{4,3,2,1,0:T(8,128)(2,1)}, bf16[1,5,16,32,128]{4,3,2,1,0:T(8,128)(2,1)S(1)}, u32[]{:S(2)}, u32[]{:S(2)}) collective-permute-start(bf16[1,5,16,32,128]{4,3,2,1,0:T(8,128)(2,1)} %get-tuple-element.164), channel_id=1, source_target_pairs={{0,1},{1,0},{2,3},{3,2},{4,5},{5,4},{6,7},{7,6},{8,9},{9,8},{10,11... | collective-permute-start | bytes 1966088 | tf_op jit(solution)/shard_map/ppermute | solution.py:367
  189.8 64.8 %collective-permute-start.51 = (bf16[1,5,16,32,128]{4,3,2,1,0:T(8,128)(2,1)}, bf16[1,5,16,32,128]{4,3,2,1,0:T(8,128)(2,1)}, u32[]{:S(2)}, u32[]{:S(2)}) collective-permute-start(bf16[1,5,16,32,128]{4,3,2,1,0:T(8,128)(2,1)} %get-tuple-element.165), channel_id=1, source_target_pairs={{0,2},{1,3},{2,0},{3,1},{4,6},{5,7},{6,4},{7,5},{8,10},{9,11},{10,... | collective-permute-start | bytes 1966088 | tf_op jit(solution)/shard_map/ppermute | solution.py:367
  203.7 53.6 %collective-permute-start.52 = (bf16[1,5,16,32,128]{4,3,2,1,0:T(8,128)(2,1)}, bf16[1,5,16,32,128]{4,3,2,1,0:T(8,128)(2,1)}, u32[]{:S(2)}, u32[]{:S(2)}) collective-permute-start(bf16[1,5,16,32,128]{4,3,2,1,0:T(8,128)(2,1)} %get-tuple-element.166), channel_id=1, source_target_pairs={{0,3},{1,2},{2,1},{3,0},{4,7},{5,6},{6,5},{7,4},{8,11},{9,10},{10,... | collective-permute-start | bytes 1966088 | tf_op jit(solution)/shard_map/ppermute | solution.py:367
  205.5 85.2 %collective-permute-start.53 = (bf16[1,5,16,32,128]{4,3,2,1,0:T(8,128)(2,1)}, bf16[1,5,16,32,128]{4,3,2,1,0:T(8,128)(2,1)}, u32[]{:S(2)}, u32[]{:S(2)}) collective-permute-start(bf16[1,5,16,32,128]{4,3,2,1,0:T(8,128)(2,1)} %get-tuple-element.167), channel_id=1, source_target_pairs={{0,4},{1,5},{2,6},{3,7},{4,0},{5,1},{6,2},{7,3},{8,12},{9,13},{10,... | collective-permute-start | bytes 1966088 | tf_op jit(solution)/shard_map/ppermute | solution.py:367
  226.4 149.6 %collective-permute-start = (bf16[32,1,128,128]{3,2,1,0:T(8,128)(2,1)}, bf16[32,1,128,128]{3,2,1,0:T(8,128)(2,1)S(1)}, u32[]{:S(2)}, u32[]{:S(2)}) collective-permute-start(bf16[32,1,128,128]{3,2,1,0:T(8,128)(2,1)} %get-tuple-element.221), channel_id=1, source_target_pairs={{0,24},{8,0},{16,8},{24,16},{1,25},{9,1},{17,9},{25,17},{2,26},{10... | collective-permute-start | bytes 3145736 | tf_op jit(solution)/shard_map/ppermute | solution.py:417
  227.8 91.9 %collective-permute-start.54 = (bf16[1,5,16,32,128]{4,3,2,1,0:T(8,128)(2,1)}, bf16[1,5,16,32,128]{4,3,2,1,0:T(8,128)(2,1)}, u32[]{:S(2)}, u32[]{:S(2)}) collective-permute-start(bf16[1,5,16,32,128]{4,3,2,1,0:T(8,128)(2,1)} %get-tuple-element.168), channel_id=1, source_target_pairs={{0,5},{1,4},{2,7},{3,6},{4,1},{5,0},{6,3},{7,2},{8,13},{9,12},{10,... | collective-permute-start | bytes 1966088 | tf_op jit(solution)/shard_map/ppermute | solution.py:367
  254.6 65.7 %collective-permute-start.55 = (bf16[1,5,16,32,128]{4,3,2,1,0:T(8,128)(2,1)}, bf16[1,5,16,32,128]{4,3,2,1,0:T(8,128)(2,1)}, u32[]{:S(2)}, u32[]{:S(2)}) collective-permute-start(bf16[1,5,16,32,128]{4,3,2,1,0:T(8,128)(2,1)} %get-tuple-element.169), channel_id=1, source_target_pairs={{0,6},{1,7},{2,4},{3,5},{4,2},{5,3},{6,0},{7,1},{8,14},{9,15},{10,... | collective-permute-start | bytes 1966088 | tf_op jit(solution)/shard_map/ppermute | solution.py:367
  257.3 129.4 %collective-permute-start.15 = (bf16[32,1,128,128]{3,2,1,0:T(8,128)(2,1)}, bf16[32,1,128,128]{3,2,1,0:T(8,128)(2,1)S(1)}, u32[]{:S(2)}, u32[]{:S(2)}) collective-permute-start(bf16[32,1,128,128]{3,2,1,0:T(8,128)(2,1)} %get-tuple-element.220), channel_id=1, source_target_pairs={{0,8},{8,16},{16,24},{24,0},{1,9},{9,17},{17,25},{25,1},{2,10},{10... | collective-permute-start | bytes 3145736 | tf_op jit(solution)/shard_map/ppermute | solution.py:416
  290.8 44.3 %collective-permute-start.56 = (bf16[1,5,16,32,128]{4,3,2,1,0:T(8,128)(2,1)}, bf16[1,5,16,32,128]{4,3,2,1,0:T(8,128)(2,1)}, u32[]{:S(2)}, u32[]{:S(2)}) collective-permute-start(bf16[1,5,16,32,128]{4,3,2,1,0:T(8,128)(2,1)} %get-tuple-element.170), channel_id=1, source_target_pairs={{0,7},{1,6},{2,5},{3,4},{4,3},{5,2},{6,1},{7,0},{8,15},{9,14},{10,... | collective-permute-start | bytes 1966088 | tf_op jit(solution)/shard_map/ppermute | solution.py:367
  320.3 30.7 %collective-permute-start.76 = (bf16[3,1,256,128]{3,2,1,0:T(8,128)(2,1)}, bf16[3,1,256,128]{3,2,1,0:T(8,128)(2,1)S(1)}, u32[]{:S(2)}, u32[]{:S(2)}) collective-permute-start(bf16[3,1,256,128]{3,2,1,0:T(8,128)(2,1)} %get-tuple-element.193), channel_id=1, source_target_pairs={{0,7},{1,0},{2,1},{3,2},{4,3},{5,4},{6,5},{7,6},{8,15},{9,8},{10,9... | collective-permute-start | bytes 589832 | tf_op jit(solution)/shard_map/ppermute | solution.py:464
  335.0 48.7 %collective-permute-start.57 = (bf16[5,1,256,128]{3,2,1,0:T(8,128)(2,1)}, bf16[5,1,256,128]{3,2,1,0:T(8,128)(2,1)S(1)}, u32[]{:S(2)}, u32[]{:S(2)}) collective-permute-start(bf16[5,1,256,128]{3,2,1,0:T(8,128)(2,1)} %get-tuple-element.172), channel_id=1, source_target_pairs={{0,1},{1,2},{2,3},{3,4},{4,5},{5,6},{6,7},{7,0},{8,9},{9,10},{10,1... | collective-permute-start | bytes 983048 | tf_op jit(solution)/shard_map/ppermute | solution.py:463
  346.3 54.0 %collective-permute-start.58 = (bf16[5,1,256,128]{3,2,1,0:T(8,128)(2,1)}, bf16[5,1,256,128]{3,2,1,0:T(8,128)(2,1)S(1)}, u32[]{:S(2)}, u32[]{:S(2)}) collective-permute-start(bf16[5,1,256,128]{3,2,1,0:T(8,128)(2,1)} %get-tuple-element.173), channel_id=1, source_target_pairs={{0,7},{1,0},{2,1},{3,2},{4,3},{5,4},{6,5},{7,6},{8,15},{9,8},{10,9... | collective-permute-start | bytes 983048 | tf_op jit(solution)/shard_map/ppermute | solution.py:464
  351.7 50.7 %collective-permute-start.66 = (bf16[5,1,256,128]{3,2,1,0:T(8,128)(2,1)}, bf16[5,1,256,128]{3,2,1,0:T(8,128)(2,1)S(1)}, u32[]{:S(2)}, u32[]{:S(2)}) collective-permute-start(bf16[5,1,256,128]{3,2,1,0:T(8,128)(2,1)} %get-tuple-element.182), channel_id=1, source_target_pairs={{0,1},{1,2},{2,3},{3,4},{4,5},{5,6},{6,7},{7,0},{8,9},{9,10},{10,1... | collective-permute-start | bytes 983048 | tf_op jit(solution)/shard_map/ppermute | solution.py:463
  400.4 55.4 %collective-permute-start.16 = (bf16[1,2,16,32,128]{4,3,2,1,0:T(8,128)(2,1)}, bf16[1,2,16,32,128]{4,3,2,1,0:T(8,128)(2,1)S(1)}, u32[]{:S(2)}, u32[]{:S(2)}) collective-permute-start(bf16[1,2,16,32,128]{4,3,2,1,0:T(8,128)(2,1)} %get-tuple-element.126), channel_id=1, source_target_pairs={{0,1},{1,0},{2,3},{3,2},{4,5},{5,4},{6,7},{7,6},{8,9},{9,8},{10,11... | collective-permute-start | bytes 786440 | tf_op jit(solution)/shard_map/ppermute | solution.py:367
  409.6 44.8 %collective-permute-start.7 = (bf16[1,1,16,32,128]{4,3,2,1,0:T(8,128)(2,1)}, bf16[1,1,16,32,128]{4,3,2,1,0:T(8,128)(2,1)S(1)}, u32[]{:S(2)}, u32[]{:S(2)}) collective-permute-start(bf16[1,1,16,32,128]{4,3,2,1,0:T(8,128)(2,1)} %get-tuple-element.114), channel_id=1, source_target_pairs={{0,7},{1,6},{2,5},{3,4},{4,3},{5,2},{6,1},{7,0},{8,15},{9,14},{10,... | collective-permute-start | bytes 393224 | tf_op jit(solution)/shard_map/ppermute | solution.py:367
  419.5 36.3 %collective-permute-start.17 = (bf16[1,2,16,32,128]{4,3,2,1,0:T(8,128)(2,1)}, bf16[1,2,16,32,128]{4,3,2,1,0:T(8,128)(2,1)S(1)}, u32[]{:S(2)}, u32[]{:S(2)}) collective-permute-start(bf16[1,2,16,32,128]{4,3,2,1,0:T(8,128)(2,1)} %get-tuple-element.127), channel_id=1, source_target_pairs={{0,2},{1,3},{2,0},{3,1},{4,6},{5,7},{6,4},{7,5},{8,10},{9,11},{10,... | collective-permute-start | bytes 786440 | tf_op jit(solution)/shard_map/ppermute | solution.py:367
  424.8 33.0 %collective-permute-start.18 = (bf16[1,2,16,32,128]{4,3,2,1,0:T(8,128)(2,1)}, bf16[1,2,16,32,128]{4,3,2,1,0:T(8,128)(2,1)S(1)}, u32[]{:S(2)}, u32[]{:S(2)}) collective-permute-start(bf16[1,2,16,32,128]{4,3,2,1,0:T(8,128)(2,1)} %get-tuple-element.128), channel_id=1, source_target_pairs={{0,3},{1,2},{2,1},{3,0},{4,7},{5,6},{6,5},{7,4},{8,11},{9,10},{10,... | collective-permute-start | bytes 786440 | tf_op jit(solution)/shard_map/ppermute | solution.py:367
  425.4 35.0 %collective-permute-start.19 = (bf16[1,2,16,32,128]{4,3,2,1,0:T(8,128)(2,1)}, bf16[1,2,16,32,128]{4,3,2,1,0:T(8,128)(2,1)S(1)}, u32[]{:S(2)}, u32[]{:S(2)}) collective-permute-start(bf16[1,2,16,32,128]{4,3,2,1,0:T(8,128)(2,1)} %get-tuple-element.129), channel_id=1, source_target_pairs={{0,4},{1,5},{2,6},{3,7},{4,0},{5,1},{6,2},{7,3},{8,12},{9,13},{10,... | collective-permute-start | bytes 786440 | tf_op jit(solution)/shard_map/ppermute | solution.py:367
  454.4 40.8 %collective-permute-start.68 = (bf16[1,5,16,32,128]{4,3,2,1,0:T(8,128)(2,1)}, bf16[1,5,16,32,128]{4,3,2,1,0:T(8,128)(2,1)}, u32[]{:S(2)}, u32[]{:S(2)}) collective-permute-start(bf16[1,5,16,32,128]{4,3,2,1,0:T(8,128)(2,1)} %get-tuple-element.185), channel_id=1, source_target_pairs={{0,1},{1,0},{2,3},{3,2},{4,5},{5,4},{6,7},{7,6},{8,9},{9,8},{10,11... | collective-permute-start | bytes 1966088 | tf_op jit(solution)/shard_map/ppermute | solution.py:367
  455.8 42.6 %collective-permute-start.69 = (bf16[1,5,16,32,128]{4,3,2,1,0:T(8,128)(2,1)}, bf16[1,5,16,32,128]{4,3,2,1,0:T(8,128)(2,1)}, u32[]{:S(2)}, u32[]{:S(2)}) collective-permute-start(bf16[1,5,16,32,128]{4,3,2,1,0:T(8,128)(2,1)} %get-tuple-element.186), channel_id=1, source_target_pairs={{0,2},{1,3},{2,0},{3,1},{4,6},{5,7},{6,4},{7,5},{8,10},{9,11},{10,... | collective-permute-start | bytes 1966088 | tf_op jit(solution)/shard_map/ppermute | solution.py:367
  460.5 29.7 %collective-permute-start.22 = (bf16[1,2,16,32,128]{4,3,2,1,0:T(8,128)(2,1)S(1)}, bf16[1,2,16,32,128]{4,3,2,1,0:T(8,128)(2,1)S(1)}, u32[]{:S(2)}, u32[]{:S(2)}) collective-permute-start(bf16[1,2,16,32,128]{4,3,2,1,0:T(8,128)(2,1)S(1)} %copy-done.71), channel_id=1, source_target_pairs={{0,7},{1,6},{2,5},{3,4},{4,3},{5,2},{6,1},{7,0},{8,15},{9,14},{10,... | collective-permute-start | bytes 786440 | tf_op jit(solution)/shard_map/ppermute | solution.py:367
  476.8 46.4 %collective-permute-start.70 = (bf16[1,5,16,32,128]{4,3,2,1,0:T(8,128)(2,1)}, bf16[1,5,16,32,128]{4,3,2,1,0:T(8,128)(2,1)S(1)}, u32[]{:S(2)}, u32[]{:S(2)}) collective-permute-start(bf16[1,5,16,32,128]{4,3,2,1,0:T(8,128)(2,1)} %get-tuple-element.187), channel_id=1, source_target_pairs={{0,3},{1,2},{2,1},{3,0},{4,7},{5,6},{6,5},{7,4},{8,11},{9,10},{10,... | collective-permute-start | bytes 1966088 | tf_op jit(solution)/shard_map/ppermute | solution.py:367
  484.5 79.5 %collective-permute-start.71 = (bf16[1,5,16,32,128]{4,3,2,1,0:T(8,128)(2,1)}, bf16[1,5,16,32,128]{4,3,2,1,0:T(8,128)(2,1)S(1)}, u32[]{:S(2)}, u32[]{:S(2)}) collective-permute-start(bf16[1,5,16,32,128]{4,3,2,1,0:T(8,128)(2,1)} %get-tuple-element.188), channel_id=1, source_target_pairs={{0,4},{1,5},{2,6},{3,7},{4,0},{5,1},{6,2},{7,3},{8,12},{9,13},{10,... | collective-permute-start | bytes 1966088 | tf_op jit(solution)/shard_map/ppermute | solution.py:367
  490.1 89.1 %collective-permute-start.72 = (bf16[1,5,16,32,128]{4,3,2,1,0:T(8,128)(2,1)}, bf16[1,5,16,32,128]{4,3,2,1,0:T(8,128)(2,1)S(1)}, u32[]{:S(2)}, u32[]{:S(2)}) collective-permute-start(bf16[1,5,16,32,128]{4,3,2,1,0:T(8,128)(2,1)} %get-tuple-element.189), channel_id=1, source_target_pairs={{0,5},{1,4},{2,7},{3,6},{4,1},{5,0},{6,3},{7,2},{8,13},{9,12},{10,... | collective-permute-start | bytes 1966088 | tf_op jit(solution)/shard_map/ppermute | solution.py:367
  495.2 84.1 %collective-permute-start.73 = (bf16[1,5,16,32,128]{4,3,2,1,0:T(8,128)(2,1)}, bf16[1,5,16,32,128]{4,3,2,1,0:T(8,128)(2,1)S(1)}, u32[]{:S(2)}, u32[]{:S(2)}) collective-permute-start(bf16[1,5,16,32,128]{4,3,2,1,0:T(8,128)(2,1)} %get-tuple-element.190), channel_id=1, source_target_pairs={{0,6},{1,7},{2,4},{3,5},{4,2},{5,3},{6,0},{7,1},{8,14},{9,15},{10,... | collective-permute-start | bytes 1966088 | tf_op jit(solution)/shard_map/ppermute | solution.py:367
  498.4 97.7 %collective-permute-start.74 = (bf16[1,5,16,32,128]{4,3,2,1,0:T(8,128)(2,1)}, bf16[1,5,16,32,128]{4,3,2,1,0:T(8,128)(2,1)S(1)}, u32[]{:S(2)}, u32[]{:S(2)}) collective-permute-start(bf16[1,5,16,32,128]{4,3,2,1,0:T(8,128)(2,1)} %get-tuple-element.191), channel_id=1, source_target_pairs={{0,7},{1,6},{2,5},{3,4},{4,3},{5,2},{6,1},{7,0},{8,15},{9,14},{10,... | collective-permute-start | bytes 1966088 | tf_op jit(solution)/shard_map/ppermute | solution.py:367
  523.2 125.1 %collective-permute-start.77 = (bf16[1,3,16,32,128]{4,3,2,1,0:T(8,128)(2,1)}, bf16[1,3,16,32,128]{4,3,2,1,0:T(8,128)(2,1)}, u32[]{:S(2)}, u32[]{:S(2)}) collective-permute-start(bf16[1,3,16,32,128]{4,3,2,1,0:T(8,128)(2,1)} %get-tuple-element.195), channel_id=1, source_target_pairs={{0,1},{1,0},{2,3},{3,2},{4,5},{5,4},{6,7},{7,6},{8,9},{9,8},{10,11... | collective-permute-start | bytes 1179656 | tf_op jit(solution)/shard_map/ppermute | solution.py:367
  564.0 86.6 %collective-permute-start.78 = (bf16[1,3,16,32,128]{4,3,2,1,0:T(8,128)(2,1)}, bf16[1,3,16,32,128]{4,3,2,1,0:T(8,128)(2,1)}, u32[]{:S(2)}, u32[]{:S(2)}) collective-permute-start(bf16[1,3,16,32,128]{4,3,2,1,0:T(8,128)(2,1)} %get-tuple-element.196), channel_id=1, source_target_pairs={{0,2},{1,3},{2,0},{3,1},{4,6},{5,7},{6,4},{7,5},{8,10},{9,11},{10,... | collective-permute-start | bytes 1179656 | tf_op jit(solution)/shard_map/ppermute | solution.py:367
  579.3 71.3 %collective-permute-start.79 = (bf16[1,3,16,32,128]{4,3,2,1,0:T(8,128)(2,1)}, bf16[1,3,16,32,128]{4,3,2,1,0:T(8,128)(2,1)}, u32[]{:S(2)}, u32[]{:S(2)}) collective-permute-start(bf16[1,3,16,32,128]{4,3,2,1,0:T(8,128)(2,1)} %get-tuple-element.197), channel_id=1, source_target_pairs={{0,3},{1,2},{2,1},{3,0},{4,7},{5,6},{6,5},{7,4},{8,11},{9,10},{10,... | collective-permute-start | bytes 1179656 | tf_op jit(solution)/shard_map/ppermute | solution.py:367
  579.3 73.9 %collective-permute-start.80 = (bf16[1,3,16,32,128]{4,3,2,1,0:T(8,128)(2,1)}, bf16[1,3,16,32,128]{4,3,2,1,0:T(8,128)(2,1)}, u32[]{:S(2)}, u32[]{:S(2)}) collective-permute-start(bf16[1,3,16,32,128]{4,3,2,1,0:T(8,128)(2,1)} %get-tuple-element.198), channel_id=1, source_target_pairs={{0,4},{1,5},{2,6},{3,7},{4,0},{5,1},{6,2},{7,3},{8,12},{9,13},{10,... | collective-permute-start | bytes 1179656 | tf_op jit(solution)/shard_map/ppermute | solution.py:367
  596.1 57.8 %collective-permute-start.81 = (bf16[1,3,16,32,128]{4,3,2,1,0:T(8,128)(2,1)}, bf16[1,3,16,32,128]{4,3,2,1,0:T(8,128)(2,1)}, u32[]{:S(2)}, u32[]{:S(2)}) collective-permute-start(bf16[1,3,16,32,128]{4,3,2,1,0:T(8,128)(2,1)} %get-tuple-element.199), channel_id=1, source_target_pairs={{0,5},{1,4},{2,7},{3,6},{4,1},{5,0},{6,3},{7,2},{8,13},{9,12},{10,... | collective-permute-start | bytes 1179656 | tf_op jit(solution)/shard_map/ppermute | solution.py:367
  648.3 51.2 %collective-permute-start.59 = (bf16[1,5,16,32,128]{4,3,2,1,0:T(8,128)(2,1)}, bf16[1,5,16,32,128]{4,3,2,1,0:T(8,128)(2,1)S(1)}, u32[]{:S(2)}, u32[]{:S(2)}) collective-permute-start(bf16[1,5,16,32,128]{4,3,2,1,0:T(8,128)(2,1)} %get-tuple-element.175), channel_id=1, source_target_pairs={{0,1},{1,0},{2,3},{3,2},{4,5},{5,4},{6,7},{7,6},{8,9},{9,8},{10,11... | collective-permute-start | bytes 1966088 | tf_op jit(solution)/shard_map/ppermute | solution.py:367
  650.6 51.0 %collective-permute-start.60 = (bf16[1,5,16,32,128]{4,3,2,1,0:T(8,128)(2,1)}, bf16[1,5,16,32,128]{4,3,2,1,0:T(8,128)(2,1)S(1)}, u32[]{:S(2)}, u32[]{:S(2)}) collective-permute-start(bf16[1,5,16,32,128]{4,3,2,1,0:T(8,128)(2,1)} %get-tuple-element.176), channel_id=1, source_target_pairs={{0,2},{1,3},{2,0},{3,1},{4,6},{5,7},{6,4},{7,5},{8,10},{9,11},{10,... | collective-permute-start | bytes 1966088 | tf_op jit(solution)/shard_map/ppermute | solution.py:367
  653.2 60.6 %collective-permute-start.61 = (bf16[1,5,16,32,128]{4,3,2,1,0:T(8,128)(2,1)}, bf16[1,5,16,32,128]{4,3,2,1,0:T(8,128)(2,1)}, u32[]{:S(2)}, u32[]{:S(2)}) collective-permute-start(bf16[1,5,16,32,128]{4,3,2,1,0:T(8,128)(2,1)} %get-tuple-element.177), channel_id=1, source_target_pairs={{0,3},{1,2},{2,1},{3,0},{4,7},{5,6},{6,5},{7,4},{8,11},{9,10},{10,... | collective-permute-start | bytes 1966088 | tf_op jit(solution)/shard_map/ppermute | solution.py:367
  653.9 45.6 %collective-permute-start.83 = (bf16[1,3,16,32,128]{4,3,2,1,0:T(8,128)(2,1)}, bf16[1,3,16,32,128]{4,3,2,1,0:T(8,128)(2,1)S(1)}, u32[]{:S(2)}, u32[]{:S(2)}) collective-permute-start(bf16[1,3,16,32,128]{4,3,2,1,0:T(8,128)(2,1)} %get-tuple-element.201), channel_id=1, source_target_pairs={{0,7},{1,6},{2,5},{3,4},{4,3},{5,2},{6,1},{7,0},{8,15},{9,14},{10,... | collective-permute-start | bytes 1179656 | tf_op jit(solution)/shard_map/ppermute | solution.py:367
  677.6 77.3 %collective-permute-start.62 = (bf16[1,5,16,32,128]{4,3,2,1,0:T(8,128)(2,1)}, bf16[1,5,16,32,128]{4,3,2,1,0:T(8,128)(2,1)}, u32[]{:S(2)}, u32[]{:S(2)}) collective-permute-start(bf16[1,5,16,32,128]{4,3,2,1,0:T(8,128)(2,1)} %get-tuple-element.178), channel_id=1, source_target_pairs={{0,4},{1,5},{2,6},{3,7},{4,0},{5,1},{6,2},{7,3},{8,12},{9,13},{10,... | collective-permute-start | bytes 1966088 | tf_op jit(solution)/shard_map/ppermute | solution.py:367
  699.5 71.8 %collective-permute-start.63 = (bf16[1,5,16,32,128]{4,3,2,1,0:T(8,128)(2,1)}, bf16[1,5,16,32,128]{4,3,2,1,0:T(8,128)(2,1)}, u32[]{:S(2)}, u32[]{:S(2)}) collective-permute-start(bf16[1,5,16,32,128]{4,3,2,1,0:T(8,128)(2,1)} %get-tuple-element.179), channel_id=1, source_target_pairs={{0,5},{1,4},{2,7},{3,6},{4,1},{5,0},{6,3},{7,2},{8,13},{9,12},{10,... | collective-permute-start | bytes 1966088 | tf_op jit(solution)/shard_map/ppermute | solution.py:367
  699.5 71.8 %collective-permute-start.64 = (bf16[1,5,16,32,128]{4,3,2,1,0:T(8,128)(2,1)}, bf16[1,5,16,32,128]{4,3,2,1,0:T(8,128)(2,1)}, u32[]{:S(2)}, u32[]{:S(2)}) collective-permute-start(bf16[1,5,16,32,128]{4,3,2,1,0:T(8,128)(2,1)} %get-tuple-element.180), channel_id=1, source_target_pairs={{0,6},{1,7},{2,4},{3,5},{4,2},{5,3},{6,0},{7,1},{8,14},{9,15},{10,... | collective-permute-start | bytes 1966088 | tf_op jit(solution)/shard_map/ppermute | solution.py:367
  701.7 69.8 %collective-permute-start.65 = (bf16[1,5,16,32,128]{4,3,2,1,0:T(8,128)(2,1)}, bf16[1,5,16,32,128]{4,3,2,1,0:T(8,128)(2,1)}, u32[]{:S(2)}, u32[]{:S(2)}) collective-permute-start(bf16[1,5,16,32,128]{4,3,2,1,0:T(8,128)(2,1)} %get-tuple-element.181), channel_id=1, source_target_pairs={{0,7},{1,6},{2,5},{3,4},{4,3},{5,2},{6,1},{7,0},{8,15},{9,14},{10,... | collective-permute-start | bytes 1966088 | tf_op jit(solution)/shard_map/ppermute | solution.py:367
  713.8 101.5 %collective-permute-start.33 = (bf16[1,16,256,128]{3,2,1,0:T(8,128)(2,1)S(1)}, bf16[1,16,256,128]{3,2,1,0:T(8,128)(2,1)}, u32[]{:S(2)}, u32[]{:S(2)}) collective-permute-start(bf16[1,16,256,128]{3,2,1,0:T(8,128)(2,1)S(1)} %copy-done.3), channel_id=1, source_target_pairs={{0,8},{8,16},{16,24},{24,0},{1,9},{9,17},{17,25},{25,1},{2,10},{10... | collective-permute-start | bytes 3145736 | tf_op jit(solution)/shard_map/ppermute | solution.py:465
  754.9 30.1 %collective-permute-start.84 = (f32[4,5,3,16,128]{4,3,2,1,0:T(8,128)}, f32[4,5,3,16,128]{4,3,2,1,0:T(8,128)}, u32[]{:S(2)}, u32[]{:S(2)}) collective-permute-start(f32[4,5,3,16,128]{4,3,2,1,0:T(8,128)} %slice_bitcast_fusion.2), channel_id=1, source_target_pairs={{0,1},{1,0},{2,3},{3,2},{4,5},{5,4},{6,7},{7,6},{8,9},{9,8},{10,11... | collective-permute-start | bytes 1474568 | tf_op jit(solution)/shard_map/ppermute | solution.py:367
  771.3 56.8 %collective-permute-start.24 = (bf16[1,1,256,128]{3,2,1,0:T(8,128)(2,1)}, bf16[1,1,256,128]{3,2,1,0:T(8,128)(2,1)S(1)}, u32[]{:S(2)}, u32[]{:S(2)}) collective-permute-start(bf16[1,1,256,128]{3,2,1,0:T(8,128)(2,1)} %get-tuple-element.134), channel_id=1, source_target_pairs={{0,1},{1,2},{2,3},{3,4},{4,5},{5,6},{6,7},{7,0},{8,9},{9,10},{10,1... | collective-permute-start | bytes 196616 | tf_op jit(solution)/shard_map/ppermute | solution.py:463
  771.4 61.3 %collective-permute-start.23 = (bf16[1,16,256,128]{3,2,1,0:T(8,128)(2,1)}, bf16[1,16,256,128]{3,2,1,0:T(8,128)(2,1)}, u32[]{:S(2)}, u32[]{:S(2)}) collective-permute-start(bf16[1,16,256,128]{3,2,1,0:T(8,128)(2,1)} %slice.122), channel_id=1, source_target_pairs={{0,24},{8,0},{16,8},{24,16},{1,25},{9,1},{17,9},{25,17},{2,26},{10... | collective-permute-start | bytes 3145736 | tf_op jit(solution)/shard_map/ppermute | solution.py:466
  790.9 39.4 %collective-permute-start.25 = (bf16[1,1,256,128]{3,2,1,0:T(8,128)(2,1)}, bf16[1,1,256,128]{3,2,1,0:T(8,128)(2,1)}, u32[]{:S(2)}, u32[]{:S(2)}) collective-permute-start(bf16[1,1,256,128]{3,2,1,0:T(8,128)(2,1)} %get-tuple-element.135), channel_id=1, source_target_pairs={{0,7},{1,0},{2,1},{3,2},{4,3},{5,4},{6,5},{7,6},{8,15},{9,8},{10,9... | collective-permute-start | bytes 196616 | tf_op jit(solution)/shard_map/ppermute | solution.py:464
  802.1 29.3 %collective-permute-start.90 = (bf16[4,5,5,16,128]{4,3,2,1,0:T(8,128)(2,1)S(1)}, bf16[4,5,5,16,128]{4,3,2,1,0:T(8,128)(2,1)S(1)}, u32[]{:S(2)}, u32[]{:S(2)}) collective-permute-start(bf16[4,5,5,16,128]{4,3,2,1,0:T(8,128)(2,1)S(1)} %fusion.14), channel_id=1, source_target_pairs={{0,1},{1,0},{2,3},{3,2},{4,5},{5,4},{6,7},{7,6},{8,9},{9,8},{10,11... | collective-permute-start | bytes 1228808 | tf_op jit(solution)/shard_map/ppermute | solution.py:367
  831.4 82.3 %collective-permute-start.87 = (f32[4,5,5,16,128]{4,3,2,1,0:T(8,128)}, f32[4,5,5,16,128]{4,3,2,1,0:T(8,128)}, u32[]{:S(2)}, u32[]{:S(2)}) collective-permute-start(f32[4,5,5,16,128]{4,3,2,1,0:T(8,128)} %slice_bitcast_fusion), channel_id=1, source_target_pairs={{0,1},{1,0},{2,3},{3,2},{4,5},{5,4},{6,7},{7,6},{8,9},{9,8},{10,11... | collective-permute-start | bytes 2457608 | tf_op jit(solution)/shard_map/ppermute | solution.py:367
  834.8 32.9 %collective-permute-start.46 = (bf16[1,2,16,32,128]{4,3,2,1,0:T(8,128)(2,1)}, bf16[1,2,16,32,128]{4,3,2,1,0:T(8,128)(2,1)}, u32[]{:S(2)}, u32[]{:S(2)}) collective-permute-start(bf16[1,2,16,32,128]{4,3,2,1,0:T(8,128)(2,1)} %get-tuple-element.159), channel_id=1, source_target_pairs={{0,4},{1,5},{2,6},{3,7},{4,0},{5,1},{6,2},{7,3},{8,12},{9,13},{10,... | collective-permute-start | bytes 786440 | tf_op jit(solution)/shard_map/ppermute | solution.py:367
  838.3 34.5 %collective-permute-start.47 = (bf16[1,2,16,32,128]{4,3,2,1,0:T(8,128)(2,1)}, bf16[1,2,16,32,128]{4,3,2,1,0:T(8,128)(2,1)}, u32[]{:S(2)}, u32[]{:S(2)}) collective-permute-start(bf16[1,2,16,32,128]{4,3,2,1,0:T(8,128)(2,1)} %get-tuple-element.160), channel_id=1, source_target_pairs={{0,5},{1,4},{2,7},{3,6},{4,1},{5,0},{6,3},{7,2},{8,13},{9,12},{10,... | collective-permute-start | bytes 786440 | tf_op jit(solution)/shard_map/ppermute | solution.py:367
  850.2 29.7 %collective-permute-start.49 = (bf16[1,2,16,32,128]{4,3,2,1,0:T(8,128)(2,1)}, bf16[1,2,16,32,128]{4,3,2,1,0:T(8,128)(2,1)}, u32[]{:S(2)}, u32[]{:S(2)}) collective-permute-start(bf16[1,2,16,32,128]{4,3,2,1,0:T(8,128)(2,1)} %get-tuple-element.162), channel_id=1, source_target_pairs={{0,7},{1,6},{2,5},{3,4},{4,3},{5,2},{6,1},{7,0},{8,15},{9,14},{10,... | collective-permute-start | bytes 786440 | tf_op jit(solution)/shard_map/ppermute | solution.py:367
  901.4 37.3 %collective-permute-start.86 = (bf16[1,5,3,16,128]{4,1,3,2,0:T(8,128)(2,1)}, bf16[1,5,3,16,128]{4,1,3,2,0:T(8,128)(2,1)}, u32[]{:S(2)}, u32[]{:S(2)}) collective-permute-start(bf16[1,5,3,16,128]{4,1,3,2,0:T(8,128)(2,1)} %fusion.29), channel_id=1, source_target_pairs={{0,4},{1,5},{2,6},{3,7},{4,0},{5,1},{6,2},{7,3},{8,12},{9,13},{10,... | collective-permute-start | bytes 184328 | tf_op jit(solution)/shard_map/ppermute | solution.py:367
  (108 other events, 2776.0 us)
